TPU v7x, 32 devices: a whole 2x2x4 slice. The times are simulated.
32 devices in a mesh: dp: 2 (over x), ctx: 4 (over z), tp: 4 (over y, core).
Axes of the slice: x: 2, y: 2, z: 4, core: 2. Of those that a mesh axis runs over, the one named last changes fastest.
Arguments:
- block_input: bfloat16 [4, 4096, 768], P('dp', ('ctx', 'tp')), may hold values from -6 to 6
- lengths: int32 [4], P('dp'), may hold values from 1024 to 4096, as said below
- cotangent: bfloat16 [4, 4096, 768], P('dp', ('ctx', 'tp')), may hold values from -6 to 6
- query_weight: float32 [768, 768], P(('dp', 'ctx'), 'tp'), may hold values from -0.3125 to 0.3125
- query_bias: float32 [768], P('tp'), may hold values from -3 to 3
- key_weight: float32 [768, 768], P(('dp', 'ctx'), 'tp'), may hold values from -0.21875 to 0.21875
- value_weight: float32 [768, 768], P(('dp', 'ctx'), 'tp'), may hold values from -0.21875 to 0.21875
- value_bias: float32 [768], P('tp'), may hold values from -3 to 3
- output_weight: float32 [768, 768], P('tp', ('dp', 'ctx')), may hold values from -0.875 to 0.875
- output_bias: float32 [768], replicated, may hold values from -3 to 3
- first_gain: float32 [768], replicated, may hold values from 0.25 to 1.75
- first_shift: float32 [768], replicated, may hold values from -3 to 3
- inner_weight: float32 [768, 3072], P(('dp', 'ctx'), 'tp'), may hold values from -0.21875 to 0.21875
- inner_bias: float32 [3072], P('tp'), may hold values from -3 to 3
- outer_weight: float32 [3072, 768], P('tp', ('dp', 'ctx')), may hold values from -0.21875 to 0.21875
- closing_offset_vector: float32 [768], replicated, may hold values from -3 to 3
- second_gain: float32 [768], replicated, may hold values from 0.25 to 1.75
- second_shift: float32 [768], replicated, may hold values from -3 to 3
Outputs:
- output: float32 [4, 4096, 768], P('dp', ('ctx', 'tp'))
- input_grad: float32 [4, 4096, 768], P('dp', ('ctx', 'tp'))
- query_weight_grad: float32 [768, 768], P(('dp', 'ctx'), 'tp')
- query_bias_grad: float32 [768], P('tp')
- key_weight_grad: float32 [768, 768], P(('dp', 'ctx'), 'tp')
- value_weight_grad: float32 [768, 768], P(('dp', 'ctx'), 'tp')
- value_bias_grad: float32 [768], P('tp')
- output_weight_grad: float32 [768, 768], P('tp', ('dp', 'ctx'))
- output_bias_grad: float32 [768], replicated
- first_gain_grad: float32 [768], replicated
- first_shift_grad: float32 [768], replicated
- inner_weight_grad: float32 [768, 3072], P(('dp', 'ctx'), 'tp')
- inner_bias_grad: float32 [3072], P('tp')
- outer_weight_grad: float32 [3072, 768], P('tp', ('dp', 'ctx'))
- outer_bias_grad: float32 [768], replicated
- second_gain_grad: float32 [768], replicated
- second_shift_grad: float32 [768], replicated
Inputs may be any that keep to these rules, and one draw needn't show every extreme that they name: `lengths`: valid slots come first in each sequence; some sequence has exactly 4096 valid slots and another exactly 1024.
All inputs are finite; a program needn't handle non-finite values.
Results may differ from a plain program's by a relative error of at most 0.02.
The roundings to bfloat16 on the way count: a program that leaves them out, or rounds other values in their place, can miss the bound.
Values may be sent and summed in bfloat16 or wider, within the bound.
No kernel may reach another device: no remote copies, remote signals or barrier semaphores. Data moves between devices by JAX's collectives and lax.ppermute only.
A program may use at most 192 MiB of HBM per device.

v0:
```python
import functools
import math

import jax
import jax.numpy as jnp
from jax import lax
from jax.experimental import pallas as pl
from jax.experimental.pallas import tpu as pltpu
from jax.sharding import PartitionSpec as P

HD = 64
PAIR = 2 * HD
EPSILON = 1e-12
NEGATIVE = -1e30
LARGEST = 1e30
BF = jnp.bfloat16
F32 = jnp.float32
VMEM_LIMIT = 56 << 20
FEED_ROWS = 512

NN = (((1,), (0,)), ((), ()))
NT = (((1,), (1,)), ((), ()))
TN = (((0,), (0,)), ((), ()))


def dot(a, b, dims):
    return lax.dot_general(a, b, dims, preferred_element_type=F32)


def params():
    return pltpu.CompilerParams(vmem_limit_bytes=VMEM_LIMIT)


def cost(flops, moved, transcendentals=0):
    return pl.CostEstimate(flops=int(flops), bytes_accessed=int(moved), transcendentals=int(transcendentals))


def after(value, *others):
    if not others:
        return value
    return lax.optimization_barrier((value, *others))[0]


def swap(value, axis, bit, start=(), done=()):
    count = lax.axis_size(axis)
    return after(lax.ppermute(after(value, *start), axis, [(i, i ^ bit) for i in range(count)]), *done)


def bits_of(axis):
    count = lax.axis_size(axis)
    return [1 << k for k in range(count.bit_length() - 1)]


def halves(value, upper, dim):
    size = value.shape[dim] // 2
    at = upper.astype(jnp.int32) * size
    mine = lax.dynamic_slice_in_dim(value, at, size, dim)
    return mine, lax.dynamic_slice_in_dim(value, size - at, size, dim)


def ordered(mine, other, upper, dim):
    return jnp.concatenate([jnp.where(upper, other, mine), jnp.where(upper, mine, other)], axis=dim)


def call(kernel, name, outs, *arrays, prefetch=None, scratch=(), flops=0):
    spec = lambda shape: pl.BlockSpec(shape, lambda i, *c: (0,) * len(shape))
    arrays_moved = sum(a.size * a.dtype.itemsize for a in arrays) + sum(4 * math.prod(shape) for shape, _ in outs)
    return pl.pallas_call(
        kernel,
        grid_spec=pltpu.PrefetchScalarGridSpec(
            num_scalar_prefetch=0 if prefetch is None else 1,
            grid=(1,),
            in_specs=[spec(a.shape) for a in arrays],
            out_specs=[spec(shape) for shape, _ in outs],
            scratch_shapes=list(scratch),
        ),
        out_shape=[jax.ShapeDtypeStruct(shape, kind) for shape, kind in outs],
        compiler_params=params(),
        cost_estimate=cost(flops, arrays_moved),
        name=name,
    )(*(() if prefetch is None else (prefetch,)), *arrays)


def fits(rows):
    return rows % 16 == 0


def pack(pieces, turned):
    widths = [p.shape[0] if t else p.shape[1] for p, t in zip(pieces, turned)]
    rows = pieces[0].shape[1] if turned[0] else pieces[0].shape[0]
    if not fits(rows):
        return jnp.concatenate([p.T if t else p for p, t in zip(pieces, turned)], axis=1).astype(BF)

    spare = -sum(widths) % 128

    def kernel(*refs):
        whole = [r[...].T if t else r[...] for r, t in zip(refs, turned)]
        if spare:
            whole.append(jnp.zeros((rows, spare), F32))
        refs[-1][...] = jnp.concatenate(whole, axis=1).astype(BF)

    return call(kernel, "pack", [((rows, sum(widths) + spare), BF)], *pieces)[0]


def stack(parts):
    rows, width = parts[0].shape
    if not fits(rows):
        return jnp.concatenate(parts, axis=0)

    def kernel(*refs):
        for k, ref in enumerate(refs[:-1]):
            refs[-1][k * rows : k * rows + rows, :] = ref[...]

    return call(kernel, "stack", [((rows * len(parts), width), BF)], *parts)[0]


def over_dp(arrays, done=()):
    found = [arrays]
    for bit in bits_of("dp"):
        found = found + [[swap(a, "dp", bit, (), done) for a in one] for one in found]
    return found


def place(found, widths, joined):
    spots, spot = lax.axis_size("ctx"), lax.axis_index("ctx")
    line, side = lax.axis_index("dp"), lax.axis_index("tp") // 2
    lines = len(found)
    starts = [sum(widths[:k]) for k in range(len(widths))]
    block = found[0][0].shape[0]
    rows = block // spots
    cuts = list(zip(starts, widths))
    shapes = [(block * lines, 2 * sum(widths[m] for m in members)) for members in joined]
    if not fits(rows):
        order = ((jnp.arange(lines)[:, None] ^ line) * spots + (jnp.arange(spots)[None, :] ^ spot)).reshape(-1)
        own, oth = (
            jnp.stack([f[h] for f in found]).reshape(lines * spots, rows, -1)[order].reshape(lines * block, -1)
            for h in range(2)
        )
        low, high = jnp.where(side == 1, oth, own), jnp.where(side == 1, own, oth)
        full = [jnp.concatenate([low[:, t : t + w], high[:, t : t + w]], axis=1) for t, w in cuts]
        return [full[m[0]] if len(m) == 1 else interleaved(full[m[0]], full[m[1]]) for m in joined]

    def kernel(where, *refs):
        outs = refs[2 * lines :]
        upper = where[2] == 1
        for k in range(lines):
            own_ref, oth_ref = refs[2 * k], refs[2 * k + 1]
            for c in range(spots):
                came = pl.ds(pl.multiple_of((where[0] ^ c) * rows, rows), rows)
                to = pl.ds(pl.multiple_of(((where[1] ^ k) * spots + c) * rows, rows), rows)
                own, oth = own_ref[came, :], oth_ref[came, :]
                low, high = jnp.where(upper, oth, own), jnp.where(upper, own, oth)
                full = [jnp.concatenate([low[:, t : t + w], high[:, t : t + w]], axis=1) for t, w in cuts]
                for out, members in zip(outs, joined):
                    if len(members) == 1:
                        out[to, :] = full[members[0]]
                    else:
                        both = []
                        for p in range(0, full[members[0]].shape[1], PAIR):
                            both += [full[m][:, p : p + PAIR] for m in members]
                        out[to, :] = jnp.concatenate(both, axis=1)

    where = jnp.stack([spot, line, side]).astype(jnp.int32)
    flat = [a for one in found for a in one]
    return call(kernel, "place", [(shape, BF) for shape in shapes], *flat, prefetch=where)


def fold_sides(pairs, cuts):
    rows = pairs[0][0].shape[0]
    width = sum(w for low, _ in cuts for _, _, w in low)
    spare = -width % 128
    width += spare
    side = lax.axis_index("tp") // 2

    def both(totals):
        end = [jnp.zeros((totals[0].shape[0], spare), F32)] if spare else []
        low = jnp.concatenate([totals[p][:, t : t + w] for cut, _ in cuts for p, t, w in cut] + end, axis=1)
        high = jnp.concatenate([totals[p][:, t : t + w] for _, cut in cuts for p, t, w in cut] + end, axis=1)
        return low, high

    if not fits(rows):
        low, high = both([a.astype(F32) + b.astype(F32) for a, b in pairs])
        return jnp.where(side == 1, high, low), jnp.where(side == 1, low, high).astype(BF)

    block = rows // 4 if fits(rows // 4) else rows
    steps = rows // block

    def kernel(where, *refs):
        kept, sent = refs[2 * len(pairs) :]
        totals = [refs[2 * k][...].astype(F32) + refs[2 * k + 1][...].astype(F32) for k in range(len(pairs))]
        low, high = both(totals)
        upper = where[0] == 1
        kept[...] = jnp.where(upper, high, low)
        sent[...] = jnp.where(upper, low, high).astype(BF)

    spec = lambda w: pl.BlockSpec((block, w), lambda i, c: (i, 0))
    flat = [a for pair in pairs for a in pair]
    return pl.pallas_call(
        kernel,
        grid_spec=pltpu.PrefetchScalarGridSpec(
            num_scalar_prefetch=1,
            grid=(steps,),
            in_specs=[spec(a.shape[1]) for a in flat],
            out_specs=[spec(width), spec(width)],
        ),
        out_shape=[jax.ShapeDtypeStruct((rows, width), F32), jax.ShapeDtypeStruct((rows, width), BF)],
        compiler_params=params(),
        cost_estimate=cost(0, sum(a.size * a.dtype.itemsize for a in flat) + 6 * rows * width),
        name="fold_sides",
    )(side.astype(jnp.int32).reshape(1), *flat)


def fold_spots(kept, came):
    spots, spot = lax.axis_size("ctx"), lax.axis_index("ctx")
    rows, width = kept.shape[0] // spots, kept.shape[1]
    if not fits(rows):
        total = kept + came.astype(F32)
        cut = lambda k: lax.dynamic_slice_in_dim(total, (spot ^ k) * rows, rows, 0)
        return [cut(0)] + [cut(k).astype(BF) for k in range(1, spots)]

    def kernel(where, kept_ref, came_ref, *outs):
        for k, out in enumerate(outs):
            at = pl.ds(pl.multiple_of((where[0] ^ k) * rows, rows), rows)
            out[...] = (kept_ref[at, :] + came_ref[at, :].astype(F32)).astype(out.dtype)

    outs = [((rows, width), F32)] + [((rows, width), BF)] * (spots - 1)
    return call(kernel, "fold_spots", outs, kept, came, prefetch=spot.astype(jnp.int32).reshape(1))


def own_rows(where, value, rows):
    mine = pl.ds(pl.multiple_of(where * rows, rows), rows)
    other = pl.ds(pl.multiple_of((1 - where) * rows, rows), rows)
    return value[mine, :], value[other, :]


def assemble(upper, pieces, held):
    local = pieces[0].shape[0]
    for k in range(len(pieces) // 2):
        mine, came = pieces[2 * k][...], pieces[2 * k + 1][...]
        held[2 * k * local : (2 * k + 1) * local, :] = jnp.where(upper, came, mine)
        held[(2 * k + 1) * local : (2 * k + 2) * local, :] = jnp.where(upper, mine, came)


def project_kernel(slots, where, *refs):
    pieces = refs[: 2 * slots + 2]
    w_query, w_kv, b_query, b_kv, query_ref, kv_ref, held = refs[2 * slots + 2 :]
    local = pieces[0].shape[0]

    @pl.when(pl.program_id(0) == 0)
    def _():
        assemble(where[0] == 1, pieces, held)

    rows = 2 * slots * local
    kv_ref[...] = (dot(held[:rows, :], w_kv[...], NN) + b_kv[...]).astype(BF)
    scale = jnp.asarray(1.0 / math.sqrt(HD), BF)
    for start, to in ((0, 0), (rows, 2 * local)):
        query = (dot(held[start : start + 2 * local, :], w_query[...], NN) + b_query[...]).astype(BF)
        query_ref[to : to + 2 * local, :] = query * scale


def project(where, pieces, w_query, w_kv, b_query, b_kv):
    slots = len(pieces) - 1
    local, width = pieces[0][0].shape
    whole = lambda p, c: (0, 0)
    across = lambda p, c: (0, p)
    flat = [p for pair in pieces for p in pair]
    q_width, kv_width = w_query.shape[1], w_kv.shape[1]
    return pl.pallas_call(
        functools.partial(project_kernel, slots),
        grid_spec=pltpu.PrefetchScalarGridSpec(
            num_scalar_prefetch=1,
            grid=(q_width // PAIR,),
            in_specs=[pl.BlockSpec(a.shape, whole, pipeline_mode=pl.Buffered(1)) for a in flat]
            + [
                pl.BlockSpec((width, PAIR), across),
                pl.BlockSpec((width, 2 * PAIR), across),
                pl.BlockSpec((1, PAIR), across),
                pl.BlockSpec((1, 2 * PAIR), across),
            ],
            out_specs=[
                pl.BlockSpec((4 * local, PAIR), across),
                pl.BlockSpec((2 * slots * local, 2 * PAIR), across),
            ],
            scratch_shapes=[pltpu.VMEM(((2 * slots + 2) * local, width), BF)],
        ),
        out_shape=[
            jax.ShapeDtypeStruct((4 * local, q_width), BF),
            jax.ShapeDtypeStruct((2 * slots * local, kv_width), BF),
        ],
        compiler_params=params(),
        cost_estimate=cost(4 * slots * local * width * (kv_width + q_width // 2), 2 * len(flat) * local * width + 4 * slots * local * kv_width),
        name="project",
    )(where, *flat, w_query, w_kv, b_query, b_kv)


def kv_back_kernel(slots, steps, split, first, where, *refs):
    pieces = refs[: 2 * slots]
    at = 2 * slots
    dkv, w_kv = refs[at : at + 2]
    at += 2
    if not first:
        before, bias_before = refs[at : at + 2]
        at += 2
    mine_ref, other_ref, bias_ref = refs[at : at + 3]
    weight_refs = refs[at + 3 : -2]
    turned, part = refs[-2:]
    local = pieces[0].shape[0]
    step = pl.program_id(0)
    upper = where[0] == 1

    @pl.when(step == 0)
    def _():
        for k in range(slots):
            mine, came = pieces[2 * k][...], pieces[2 * k + 1][...]
            turned[:, 2 * k * local : (2 * k + 1) * local] = jnp.where(upper, came, mine).T
            turned[:, (2 * k + 1) * local : (2 * k + 2) * local] = jnp.where(upper, mine, came).T

    grads = dkv[...]
    total = dot(turned[...], grads, NN)
    bias = jnp.sum(grads.astype(F32), axis=0, keepdims=True)
    if not first:
        total, bias = total + before[...], bias + bias_before[...]
    bias_ref[...] = bias
    half = total.shape[0] // 2
    if split:
        lower_line = where[1] == 0
        weight_refs[0][...] = jnp.where(lower_line, total[:half], total[half:])
        weight_refs[1][...] = jnp.where(lower_line, total[half:], total[:half]).astype(BF)
    else:
        weight_refs[0][...] = total
    term = dot(grads, w_kv[...], NT)

    @pl.when(step == 0)
    def _():
        part[...] = term

    @pl.when(jnp.logical_and(step > 0, step < steps - 1))
    def _():
        part[...] += term

    @pl.when(step == steps - 1)
    def _():
        for k in range(slots):
            low = slice(2 * k * local, (2 * k + 1) * local)
            high = slice((2 * k + 1) * local, (2 * k + 2) * local)
            to = slice(k * local, k * local + local)
            low_part, high_part = part[low, :] + term[low], part[high, :] + term[high]
            mine_ref[to, :] = jnp.where(upper, high_part, low_part)
            other_ref[to, :] = jnp.where(upper, low_part, high_part).astype(BF)


def kv_back(where, pieces, dkv, w_kv, before, last):
    slots = len(pieces)
    local, width = pieces[0][0].shape
    kv_width = w_kv.shape[1]
    split = last and lax.axis_size("dp") == 2
    whole = lambda p, c: (0, 0)
    across = lambda p, c: (0, p)
    once = pl.Buffered(1)
    flat = [p for pair in pieces for p in pair]
    extra = () if before is None else before
    if split:
        weight_outs = [((width // 2, kv_width), F32), ((width // 2, kv_width), BF)]
    else:
        weight_outs = [((width, kv_width), F32)]
    steps = kv_width // (2 * PAIR)
    return pl.pallas_call(
        functools.partial(kv_back_kernel, slots, steps, split, before is None),
        grid_spec=pltpu.PrefetchScalarGridSpec(
            num_scalar_prefetch=1,
            grid=(steps,),
            in_specs=[pl.BlockSpec((local, width), whole, pipeline_mode=once) for _ in flat]
            + [pl.BlockSpec((a.shape[0], 2 * PAIR), across) for a in (dkv, w_kv, *extra)],
            out_specs=[
                pl.BlockSpec((slots * local, width), whole, pipeline_mode=once),
                pl.BlockSpec((slots * local, width), whole, pipeline_mode=once),
                pl.BlockSpec((1, 2 * PAIR), across),
            ]
            + [pl.BlockSpec((shape[0], 2 * PAIR), across) for shape, _ in weight_outs],
            scratch_shapes=[pltpu.VMEM((width, 2 * slots * local), BF), pltpu.VMEM((2 * slots * local, width), F32)],
        ),
        out_shape=[
            jax.ShapeDtypeStruct((slots * local, width), F32),
            jax.ShapeDtypeStruct((slots * local, width), BF),
            jax.ShapeDtypeStruct((1, kv_width), F32),
        ]
        + [jax.ShapeDtypeStruct(shape, kind) for shape, kind in weight_outs],
        compiler_params=params(),
        cost_estimate=cost(8 * slots * local * width * kv_width, 12 * slots * local * width + 4 * width * kv_width),
        name="kv_back",
    )(where, *flat, dkv, w_kv, *extra)


def query_back_kernel(seqs, lines, where, *refs):
    dq_own, dq_came, own, came = (refs[k * seqs : k * seqs + seqs] for k in range(4))
    weight, mine_ref, other_ref, bias_ref = refs[4 * seqs : 4 * seqs + 4]
    weight_refs, total = refs[4 * seqs + 4 : -1], refs[-1]
    upper = where[0] == 1
    half = own[0].shape[0]
    bias = None
    for s in range(seqs):
        low = (dq_own[s][...] + dq_came[s][...].astype(F32)).astype(BF)
        rows = jnp.concatenate(
            [jnp.where(upper, came[s][...], own[s][...]), jnp.where(upper, own[s][...], came[s][...])], axis=0
        )
        part = dot(low, weight[...], (((0,), (1,)), ((), ())))
        to = slice(s * half, s * half + half)
        mine_ref[to, :] = jnp.where(upper, part[half:], part[:half])
        other_ref[to, :] = jnp.where(upper, part[:half], part[half:]).astype(BF)
        grad = dot(rows, low, (((0,), (1,)), ((), ())))
        total[...] = grad if s == 0 else total[...] + grad
        sums = jnp.sum(low.astype(F32), axis=1, keepdims=True)
        bias = sums if bias is None else bias + sums
    bias_ref[...] = bias
    if lines == 2:
        kept, sent = own_rows(where[1], total, total.shape[0] // 2)
        weight_refs[0][...] = kept
        weight_refs[1][...] = sent.astype(BF)
    else:
        weight_refs[0][...] = total[...]


def query_back(where, dq_own, dq_came, own, came, weight):
    seqs, lines = len(dq_own), lax.axis_size("dp")
    local, width = own[0].shape
    own_width = weight.shape[1]
    outs = [((seqs * local, width), F32), ((seqs * local, width), BF), ((own_width, 1), F32)]
    if lines == 2:
        outs += [((width // 2, own_width), F32), ((width // 2, own_width), BF)]
    else:
        outs += [((width, own_width), F32)]
    return call(
        functools.partial(query_back_kernel, seqs, lines),
        "query_back",
        outs,
        *dq_own,
        *dq_came,
        *own,
        *came,
        weight,
        prefetch=where,
        scratch=[pltpu.VMEM((width, own_width), F32)],
        flops=8 * seqs * local * width * own_width,
    )


def half_lanes(value):
    lane = lax.broadcasted_iota(jnp.int32, value.shape, 1)
    zero = jnp.zeros_like(value)
    return [jnp.where(lane < HD, value, zero), jnp.where(lane >= HD, value, zero)]


def half_rows(value):
    row = lax.broadcasted_iota(jnp.int32, value.shape, 0)
    zero = jnp.zeros_like(value)
    return [jnp.where(row < HD, value, zero), jnp.where(row >= HD, value, zero)]


def top_bits(value):
    spread = value * 65537.0
    return spread - (spread - value)


def in_three(value):
    first = top_bits(value)
    rest = value - first
    second = top_bits(rest)
    return first.astype(BF), second.astype(BF), (rest - second).astype(BF)


def packed_rows(values):
    terms = jnp.concatenate(in_three(values), axis=0)
    return jnp.concatenate([terms, jnp.zeros((16 - terms.shape[0], terms.shape[1]), BF)], axis=0)


def unpacked_rows(packed, count):
    packed = packed.astype(F32)
    return packed[:count] + packed[count : 2 * count] + packed[2 * count : 3 * count]


def below(shape, count):
    return lax.broadcasted_iota(jnp.int32, shape, 0) < count


def attend_kernel(slots, probe, counts, queries, kv, *refs):
    o_own, packed, lse_ref, top, total, acc, heads = refs[-7:]
    rows = queries.shape[0] // 2
    keys = kv.shape[0] // slots
    for h, query in enumerate(half_lanes(queries[...])):
        heads[h] = query

    def block(k):
        at = pl.ds(pl.multiple_of(k * keys, keys), keys)
        return kv[at, :PAIR], kv[at, PAIR:]

    first = pl.ds(pl.multiple_of(counts[slots] * keys, keys), probe)
    for h in range(2):
        top[h] = jnp.max(dot(kv[first, :PAIR], heads[h], NT), axis=0, keepdims=True)
    total[...] = jnp.zeros_like(total)
    acc[...] = jnp.zeros_like(acc)

    def quick(k, h, valid):
        key, value = block(k)
        expo = jnp.exp(dot(key, heads[h], NT) - top[h])
        if valid is not None:
            expo = jnp.where(below(expo.shape, valid), expo, 0.0)
        total[h] += jnp.sum(expo, axis=0, keepdims=True)
        acc[h] += dot(value, expo.astype(BF), TN)

    @pl.loop(0, slots)
    def _(k):
        valid = counts[k]

        @pl.when(valid >= keys)
        def _():
            quick(k, 0, None)
            quick(k, 1, None)

        @pl.when(jnp.logical_and(valid > 0, valid < keys))
        def _():
            pl.loop(0, 2)(lambda h: quick(k, h, valid))

    @pl.when(jnp.logical_not(jnp.max(total[...]) < LARGEST))
    def _():
        total[...] = jnp.zeros_like(total)
        acc[...] = jnp.zeros_like(acc)

        def careful(k, h, valid):
            key, value = block(k)
            scores = dot(key, heads[h], NT)
            scores = jnp.where(below(scores.shape, valid), scores, NEGATIVE)
            old = top[h]
            new = jnp.maximum(old, jnp.max(scores, axis=0, keepdims=True))
            expo = jnp.where(below(scores.shape, valid), jnp.exp(scores - new), 0.0)
            scale = jnp.exp(old - new)
            total[h] = total[h] * scale + jnp.sum(expo, axis=0, keepdims=True)
            acc[h] = acc[h] * scale + dot(value, expo.astype(BF), TN)
            top[h] = new

        @pl.loop(0, slots)
        def _(k):
            valid = counts[k]

            @pl.when(valid > 0)
            def _():
                pl.loop(0, 2)(lambda h: careful(k, h, valid))

    lse = []
    for h in range(2):
        at = slice(h * HD, h * HD + HD)
        part = acc[h, at, :] / total[h]
        o_own[0, at, :] = part[:, :rows]
        packed[at, :] = part[:, rows:].astype(BF)
        lse.append(top[h] + jnp.log(total[h]))
        lse_ref[0, 0, h : h + 1, :] = lse[h][:, :rows]
    packed[PAIR:, :] = packed_rows(jnp.concatenate([l[:, rows:] for l in lse], axis=0))


def attend(counts, slots, seqs, s, queries, kv, before):
    rows, width = queries.shape[0] // 2, queries.shape[1]
    pairs = width // PAIR
    keys = kv.shape[0] // slots
    total = width * 2 * rows * kv.shape[0]
    anywhere = pl.BlockSpec(memory_space=pl.ANY)
    return pl.pallas_call(
        functools.partial(attend_kernel, slots, min(128, keys)),
        grid_spec=pltpu.PrefetchScalarGridSpec(
            num_scalar_prefetch=1,
            grid=(pairs,),
            in_specs=[
                pl.BlockSpec((2 * rows, PAIR), lambda p, c: (0, p)),
                pl.BlockSpec((kv.shape[0], 2 * PAIR), lambda p, c: (0, p)),
            ]
            + [anywhere] * len(before),
            out_specs=[
                pl.BlockSpec((1, PAIR, rows), lambda p, c: (s, p, 0)),
                pl.BlockSpec((PAIR + 16, rows), lambda p, c: (p, 0)),
                pl.BlockSpec((1, 1, 2, rows), lambda p, c: (s, p, 0, 0)),
            ],
            scratch_shapes=[
                pltpu.VMEM((2, 1, 2 * rows), F32),
                pltpu.VMEM((2, 1, 2 * rows), F32),
                pltpu.VMEM((2, PAIR, 2 * rows), F32),
                pltpu.VMEM((2, 2 * rows, PAIR), BF),
            ],
        ),
        out_shape=[
            jax.ShapeDtypeStruct((seqs, width, rows), F32),
            jax.ShapeDtypeStruct((pairs * (PAIR + 16), rows), BF),
            jax.ShapeDtypeStruct((seqs, pairs, 2, rows), F32),
        ],
        input_output_aliases={3: 0, 4: 2} if before else {},
        compiler_params=params(),
        cost_estimate=cost(16 * total, 8 * queries.size + 2 * kv.size, total // HD),
        name="attend",
    )(counts, queries, kv, *before)


def attend_back_kernel(slots, counts, both, g_own, g_oth, kv, dq_own, dq_oth, dkv, acc, queries, grads, summed, facts):
    rows = both.shape[0] // 2
    keys = kv.shape[0] // slots
    acc[...] = jnp.zeros_like(acc)
    for block, g_ref in enumerate((g_own, g_oth)):
        stats = unpacked_rows(g_ref[PAIR:, :], 4)
        for h, (query, grad) in enumerate(
            zip(half_lanes(both[block * rows : block * rows + rows, :]), half_rows(g_ref[:PAIR, :]))
        ):
            queries[2 * block + h] = query
            grads[2 * block + h] = grad
            facts[2 * block + h, 0:1, :] = stats[h : h + 1]
            facts[2 * block + h, 1:2, :] = stats[2 + h : 3 + h]

    @pl.loop(0, slots)
    def _(k):
        valid = counts[k]
        rows_at = pl.ds(pl.multiple_of(k * keys, keys), keys)

        def one(at, valid):
            key, value = kv[rows_at, :PAIR], kv[rows_at, PAIR:]
            query, grad = queries[at], grads[at]
            prob = jnp.exp(dot(key, query, NT) - facts[at, 0:1, :])
            if valid is not None:
                prob = jnp.where(below(prob.shape, valid), prob, 0.0)
            change = dot(value, grad, NN) - facts[at, 1:2, :]
            score = (prob * change).astype(BF)
            summed[:, PAIR:] += dot(prob.astype(BF), grad, NT)
            summed[:, :PAIR] += dot(score, query, NN)
            acc[at] += dot(key, score, TN)

        summed[...] = jnp.zeros_like(summed)

        @pl.when(valid >= keys)
        def _():
            for at in range(4):
                one(at, None)

        @pl.when(jnp.logical_and(valid > 0, valid < keys))
        def _():
            pl.loop(0, 4)(lambda at: one(at, valid))

        dkv[rows_at, :] = summed[...].astype(BF)

    scale = 1.0 / math.sqrt(HD)
    for h in range(2):
        at = slice(h * HD, h * HD + HD)
        dq_own[at, :] = acc[h, at, :] * scale
        dq_oth[at, :] = (acc[2 + h, at, :] * scale).astype(BF)


def attend_back(counts, slots, both, g_own, g_oth, kv):
    rows, width = both.shape[0] // 2, both.shape[1]
    pairs = width // PAIR
    keys = kv.shape[0] // slots
    q_spec = pl.BlockSpec((2 * rows, PAIR), lambda p, c: (0, p))
    t_spec = pl.BlockSpec((PAIR, rows), lambda p, c: (p, 0))
    g_spec = pl.BlockSpec((PAIR + 16, rows), lambda p, c: (p, 0))
    kv_spec = pl.BlockSpec((kv.shape[0], 2 * PAIR), lambda p, c: (0, p))
    total = width * 2 * rows * kv.shape[0]
    return pl.pallas_call(
        functools.partial(attend_back_kernel, slots),
        grid_spec=pltpu.PrefetchScalarGridSpec(
            num_scalar_prefetch=1,
            grid=(pairs,),
            in_specs=[q_spec, g_spec, g_spec, kv_spec],
            out_specs=[t_spec, t_spec, kv_spec],
            scratch_shapes=[
                pltpu.VMEM((4, PAIR, rows), F32),
                pltpu.VMEM((4, rows, PAIR), BF),
                pltpu.VMEM((4, PAIR, rows), BF),
                pltpu.VMEM((keys, 2 * PAIR), F32),
                pltpu.VMEM((4, 2, rows), F32),
            ],
        ),
        out_shape=[
            jax.ShapeDtypeStruct((width, rows), F32),
            jax.ShapeDtypeStruct((width, rows), BF),
            jax.ShapeDtypeStruct(kv.shape, BF),
        ],
        compiler_params=params(),
        cost_estimate=cost(40 * total, 8 * both.size + 4 * kv.size, total // HD),
        name="attend_back",
    )(counts, both, g_own, g_oth, kv)


def merge_kernel(pairs, seqs, where, o_own, lse_own, *refs):
    packs = refs[:seqs]
    weight, full_ref, low_ref, mine_ref, other_ref, lse_ref, low_s, packed = refs[seqs:]
    rows = o_own.shape[2]
    for s in range(seqs):

        @pl.when(pl.program_id(0) == s)
        def _(s=s):
            packed[...] = packs[s][...]

    for p in range(pairs):
        base = p * (PAIR + 16)
        own = lse_own[0, p]
        came = unpacked_rows(packed[base + PAIR : base + PAIR + 16, :], 2)
        highest = jnp.maximum(own, came)
        share_own, share_came = jnp.exp(own - highest), jnp.exp(came - highest)
        both = share_own + share_came
        lse_ref[0, p] = highest + jnp.log(both)
        share_own, share_came = share_own / both, share_came / both
        for h in range(2):
            at = slice(p * PAIR + h * HD, p * PAIR + h * HD + HD)
            term = packed[base + h * HD : base + h * HD + HD, :].astype(F32)
            merged = o_own[0, at, :] * share_own[h : h + 1] + term * share_came[h : h + 1]
            full_ref[0, at, :] = merged
            low_s[at, :] = merged.astype(BF)
    low_ref[0] = low_s[...]
    half = rows // 2
    mine = pl.ds(pl.multiple_of(where[0] * half, half), half)
    other = pl.ds(pl.multiple_of((1 - where[0]) * half, half), half)
    dims = (((0,), (1,)), ((), ()))
    mine_ref[0] = dot(low_s[:, mine], weight[...], dims)
    other_ref[0] = dot(low_s[:, other], weight[...], dims).astype(BF)


def merge(where, o_own, lse_own, packs, weight):
    seqs, width, rows = o_own.shape
    pairs = width // PAIR
    model = weight.shape[0]
    one = lambda *shape: pl.BlockSpec((1, *shape), lambda s, w: (s,) + (0,) * len(shape))
    return pl.pallas_call(
        functools.partial(merge_kernel, pairs, seqs),
        grid_spec=pltpu.PrefetchScalarGridSpec(
            num_scalar_prefetch=1,
            grid=(seqs,),
            in_specs=[
                one(width, rows),
                one(pairs, 2, rows),
            ]
            + [pl.BlockSpec(p.shape, lambda s, w: (0, 0)) for p in packs]
            + [
                pl.BlockSpec(weight.shape, lambda s, w: (0, 0)),
            ],
            out_specs=[one(width, rows), one(width, rows), one(rows // 2, model), one(rows // 2, model), one(pairs, 2, rows)],
            scratch_shapes=[pltpu.VMEM((width, rows), BF), pltpu.VMEM(packs[0].shape, BF)],
        ),
        out_shape=[
            jax.ShapeDtypeStruct((seqs, width, rows), F32),
            jax.ShapeDtypeStruct((seqs, width, rows), BF),
            jax.ShapeDtypeStruct((seqs, rows // 2, model), F32),
            jax.ShapeDtypeStruct((seqs, rows // 2, model), BF),
            jax.ShapeDtypeStruct((seqs, pairs, 2, rows), F32),
        ],
        compiler_params=params(),
        cost_estimate=cost(2 * seqs * width * rows * model, 12 * o_own.size + 4 * seqs * rows * model),
        name="merge",
    )(where, o_own, lse_own, *packs, weight)


def turn_kernel(pairs, seqs, lines, where, own_ref, came_ref, weight, full_ref, low_ref, lse_ref, *refs):
    packs, weight_refs = refs[:seqs], refs[seqs:-2]
    d_weight, packed = refs[-2:]
    step = pl.program_id(0)
    upper = where[0] == 1
    own, came = own_ref[0], came_ref[0]
    rows = jnp.concatenate([jnp.where(upper, came, own), jnp.where(upper, own, came)], axis=0)
    grad = dot(weight[...], rows, (((0,), (1,)), ((), ()))).astype(BF)
    product = grad.astype(F32) * full_ref[0]
    for p in range(pairs):
        base = p * (PAIR + 16)
        packed[base : base + PAIR, :] = grad[p * PAIR : p * PAIR + PAIR]
        stats = [lse_ref[0, p]]
        for h in range(2):
            at = slice(p * PAIR + h * HD, p * PAIR + h * HD + HD)
            stats.append(jnp.sum(product[at], axis=0, keepdims=True))
        packed[base + PAIR : base + PAIR + 16, :] = packed_rows(jnp.concatenate(stats, axis=0))
    for s in range(seqs):

        @pl.when(step == s)
        def _(s=s):
            packs[s][...] = packed[...]

    @pl.when(step == 0)
    def _():
        d_weight[...] = jnp.zeros_like(d_weight)

    d_weight[...] += dot(rows, low_ref[0], (((0,), (1,)), ((), ())))

    @pl.when(step == seqs - 1)
    def _():
        if lines == 2:
            kept, sent = own_rows(where[1], d_weight, d_weight.shape[0] // 2)
            weight_refs[0][...] = kept
            weight_refs[1][...] = sent.astype(BF)
        else:
            weight_refs[0][...] = d_weight[...]


def turn(where, own, came, weight, full, low, lse):
    seqs, width, rows = full.shape
    pairs = width // PAIR
    one = lambda *shape: pl.BlockSpec((1, *shape), lambda s, w: (s,) + (0,) * len(shape))
    whole = lambda *shape: pl.BlockSpec(shape, lambda s, w: (0, 0))
    lines = lax.axis_size("dp")
    pack_shape = (pairs * (PAIR + 16), rows)
    half = (weight.shape[0] // 2, weight.shape[1])
    weight_outs = [(half, F32), (half, BF)] if lines == 2 else [(weight.shape, F32)]
    return pl.pallas_call(
        functools.partial(turn_kernel, pairs, seqs, lines),
        grid_spec=pltpu.PrefetchScalarGridSpec(
            num_scalar_prefetch=1,
            grid=(seqs,),
            in_specs=[
                one(*own.shape[1:]),
                one(*own.shape[1:]),
                whole(*weight.shape),
                one(width, rows),
                one(width, rows),
                one(pairs, 2, rows),
            ],
            out_specs=[whole(*pack_shape)] * seqs + [whole(*shape) for shape, _ in weight_outs],
            scratch_shapes=[pltpu.VMEM(weight.shape, F32), pltpu.VMEM(pack_shape, BF)],
        ),
        out_shape=[jax.ShapeDtypeStruct(pack_shape, BF)] * seqs
        + [jax.ShapeDtypeStruct(shape, kind) for shape, kind in weight_outs],
        compiler_params=params(),
        cost_estimate=cost(4 * seqs * rows * weight.size, 8 * full.size + 4 * own.size),
        name="turn",
    )(where, own, came, weight, full, low, lse)


def gelu_parts(u):
    density = jnp.exp(-0.5 * u * u)
    t = 1.0 / (1.0 + (0.3275911 / math.sqrt(2.0)) * jnp.abs(u))
    series = t * (
        0.254829592
        + t * (-0.284496736 + t * (1.421413741 + t * (-1.453152027 + t * 1.061405429)))
    )
    tail = 0.5 * series * density
    share = jnp.where(u < 0.0, tail, 1.0 - tail)
    return u * share, share + u * (density * (1.0 / math.sqrt(2.0 * math.pi)))


def feed_kernel(chunk, half, own_ref, came_ref, w_in, bias, w_out, active_ref, slope_ref, mine_ref, other_ref):
    step = pl.program_id(0)
    rows = jnp.where(step < half, own_ref[...], came_ref[...])
    part = None
    for start in range(0, w_in.shape[1], chunk):
        at = slice(start, start + chunk)
        inner = dot(rows, w_in[:, at], NN) + bias[:, at]
        active, slope = gelu_parts(inner)
        active = active.astype(BF)
        active_ref[:, at] = active
        slope_ref[:, at] = slope.astype(BF)
        term = dot(active, w_out[:, at], NT)
        part = term if part is None else part + term

    @pl.when(step < half)
    def _():
        mine_ref[...] = part

    @pl.when(step >= half)
    def _():
        other_ref[...] = part.astype(BF)


def row_specs(block, half, width):
    own = pl.BlockSpec((block, width), lambda i, *c: (jnp.minimum(i, half - 1), 0))
    came = pl.BlockSpec((block, width), lambda i, *c: (jnp.maximum(i - half, 0), 0))
    return own, came


def feed(own, came, w_in, bias, w_out):
    count, width = own.shape
    units = w_in.shape[1]
    block = min(FEED_ROWS, count)
    half = count // block
    whole = lambda i: (0, 0)
    by_row = lambda i: (i, 0)
    own_spec, came_spec = row_specs(block, half, width)
    return pl.pallas_call(
        functools.partial(feed_kernel, units // 3 if units % 384 == 0 else units, half),
        grid=(2 * half,),
        in_specs=[
            own_spec,
            came_spec,
            pl.BlockSpec((width, units), whole, pipeline_mode=pl.Buffered(1)),
            pl.BlockSpec((1, units), whole),
            pl.BlockSpec((width, units), whole, pipeline_mode=pl.Buffered(1)),
        ],
        out_specs=[pl.BlockSpec((block, units), by_row), pl.BlockSpec((block, units), by_row), own_spec, came_spec],
        out_shape=[
            jax.ShapeDtypeStruct((2 * count, units), BF),
            jax.ShapeDtypeStruct((2 * count, units), BF),
            jax.ShapeDtypeStruct((count, width), F32),
            jax.ShapeDtypeStruct((count, width), BF),
        ],
        compiler_params=params(),
        cost_estimate=cost(8 * count * width * units, 4 * width * units + 8 * count * units + 12 * count * width, 2 * count * units),
        name="feed",
    )(own, came, w_in, bias, w_out)


def feed_back_kernel(half, lines, where, low_own, low_came, own_ref, came_ref, active_ref, slope_ref, w_in, w_out, *refs):
    mine_ref, other_ref, d_bias_ref = refs[:3]
    weight_refs, (d_in, d_out) = refs[3:-2], refs[-2:]
    step = pl.program_id(0)
    units = w_in.shape[1]

    @pl.when(step == 0)
    def _():
        d_in[...] = jnp.zeros_like(d_in)
        d_out[...] = jnp.zeros_like(d_out)
        d_bias_ref[...] = jnp.zeros_like(d_bias_ref)

    low = jnp.where(step < half, low_own[...], low_came[...])
    rows = jnp.where(step < half, own_ref[...], came_ref[...])
    inner = (dot(low, w_out[...], NN) * slope_ref[...].astype(F32)).astype(BF)
    part = dot(inner, w_in[...], NT)
    d_out[...] += dot(low, active_ref[...], TN)
    d_in[...] += dot(rows, inner, TN)
    d_bias_ref[...] += jnp.sum(inner.astype(F32), axis=0, keepdims=True)

    @pl.when(step < half)
    def _():
        mine_ref[...] = part

    @pl.when(step >= half)
    def _():
        other_ref[...] = part.astype(BF)

    @pl.when(step == 2 * half - 1)
    def _():
        for total, cut in ((d_in, slice(0, units)), (d_out, slice(units, 2 * units))):
            if lines == 2:
                kept, sent = own_rows(where[1], total, total.shape[0] // 2)
                weight_refs[0][:, cut] = kept.astype(BF)
                weight_refs[1][:, cut] = sent.astype(BF)
            else:
                weight_refs[0][:, cut] = total[...].astype(BF)


def feed_back(where, low_own, low_came, own, came, active, slope, w_in, w_out):
    count, width = own.shape
    units = w_in.shape[1]
    block = min(FEED_ROWS, count)
    half = count // block
    whole = lambda i, *c: (0, 0)
    by_row = lambda i, *c: (i, 0)
    once = pl.Buffered(1)
    lines = lax.axis_size("dp")
    own_spec, came_spec = row_specs(block, half, width)
    d_shape = (width // 2 if lines == 2 else width, 2 * units)
    d_count = 2 if lines == 2 else 1
    return pl.pallas_call(
        functools.partial(feed_back_kernel, half, lines),
        grid_spec=pltpu.PrefetchScalarGridSpec(
            num_scalar_prefetch=1,
            grid=(2 * half,),
            in_specs=[
                own_spec,
                came_spec,
                own_spec,
                came_spec,
                pl.BlockSpec((block, units), by_row),
                pl.BlockSpec((block, units), by_row),
                pl.BlockSpec((width, units), whole, pipeline_mode=once),
                pl.BlockSpec((width, units), whole, pipeline_mode=once),
            ],
            out_specs=[own_spec, came_spec, pl.BlockSpec((1, units), whole)]
            + [pl.BlockSpec(d_shape, whole, pipeline_mode=once)] * d_count,
            scratch_shapes=[pltpu.VMEM((width, units), F32), pltpu.VMEM((width, units), F32)],
        ),
        out_shape=[
            jax.ShapeDtypeStruct((count, width), F32),
            jax.ShapeDtypeStruct((count, width), BF),
            jax.ShapeDtypeStruct((1, units), F32),
        ]
        + [jax.ShapeDtypeStruct(d_shape, BF)] * d_count,
        compiler_params=params(),
        cost_estimate=cost(16 * count * width * units, 8 * width * units + 8 * count * units + 16 * count * width),
        name="feed_back",
    )(where, low_own, low_came, own, came, active, slope, w_in, w_out)


def centre(values):
    middle = values - jnp.mean(values, axis=-1, keepdims=True)
    scale = lax.rsqrt(jnp.mean(middle * middle, axis=-1, keepdims=True) + EPSILON)
    return middle * scale, scale


def back_through(weighted, normal, scale):
    first = jnp.mean(weighted, axis=-1, keepdims=True)
    second = jnp.mean(weighted * normal, axis=-1, keepdims=True)
    return (weighted - first - normal * second) * scale


def first_kernel(x_ref, mine_ref, came_ref, vec_ref, normal_ref, scale_ref, low_ref):
    sums = x_ref[...].astype(F32) + (mine_ref[...] + came_ref[...].astype(F32)) + vec_ref[0:1, :]
    normal, scale = centre(sums)
    normal_ref[...] = normal
    scale_ref[...] = scale
    low_ref[...] = (normal * vec_ref[1:2, :] + vec_ref[2:3, :]).astype(BF)


def second_kernel(per_seq, counts, normal_ref, mine_ref, came_ref, cot_ref, vec_ref, out_ref, grad_ref, low_ref, sums_ref):
    step = pl.program_id(0)
    block = normal_ref.shape[0]
    valid = counts[step // per_seq] - (step % per_seq) * block
    keep = lax.broadcasted_iota(jnp.int32, normal_ref.shape, 0) < valid

    @pl.when(step == 0)
    def _():
        sums_ref[...] = jnp.zeros_like(sums_ref)

    first = normal_ref[...] * vec_ref[1:2, :] + vec_ref[2:3, :]
    sums = first + (mine_ref[...] + came_ref[...].astype(F32)) + vec_ref[3:4, :]
    normal, scale = centre(sums)
    out_ref[...] = jnp.where(keep, normal * vec_ref[4:5, :] + vec_ref[5:6, :], 0.0)
    out_grad = jnp.where(keep, cot_ref[...].astype(F32), 0.0)
    grad = back_through(out_grad * vec_ref[4:5, :], normal, scale)
    grad_ref[...] = grad
    low_ref[...] = grad.astype(BF)
    sums_ref[0:1, :] += jnp.sum(out_grad * normal, axis=0, keepdims=True)
    sums_ref[1:2, :] += jnp.sum(out_grad, axis=0, keepdims=True)
    sums_ref[2:3, :] += jnp.sum(grad, axis=0, keepdims=True)


def first_back_kernel(grad_ref, mine_ref, came_ref, normal_ref, scale_ref, vec_ref, out_ref, low_ref, sums_ref):
    @pl.when(pl.program_id(0) == 0)
    def _():
        sums_ref[...] = jnp.zeros_like(sums_ref)

    given = grad_ref[...] + (mine_ref[...] + came_ref[...].astype(F32))
    normal = normal_ref[...]
    grad = back_through(given * vec_ref[1:2, :], normal, scale_ref[...])
    out_ref[...] = grad
    low_ref[...] = grad.astype(BF)
    sums_ref[0:1, :] += jnp.sum(given * normal, axis=0, keepdims=True)
    sums_ref[1:2, :] += jnp.sum(given, axis=0, keepdims=True)
    sums_ref[2:3, :] += jnp.sum(grad, axis=0, keepdims=True)


def row_call(kernel, name, block, count, width, inputs, whole_inputs, outs, sums, counts=None):
    by_row = lambda i, *c: (i, 0)
    whole = lambda i, *c: (0, 0)
    in_specs = [pl.BlockSpec((block, a.shape[1]), by_row) for a in inputs]
    in_specs += [pl.BlockSpec(a.shape, whole) for a in whole_inputs]
    out_specs = [pl.BlockSpec((block, w), by_row) for w, _ in outs]
    out_shape = [jax.ShapeDtypeStruct((count, w), t) for w, t in outs]
    if sums:
        out_specs.append(pl.BlockSpec((8, width), whole))
        out_shape.append(jax.ShapeDtypeStruct((8, width), F32))
    prefetch = 0 if counts is None else 1
    moved = sum(a.size * a.dtype.itemsize for a in inputs) + sum(count * w * 4 for w, _ in outs)
    return pl.pallas_call(
        kernel,
        grid_spec=pltpu.PrefetchScalarGridSpec(
            num_scalar_prefetch=prefetch, grid=(count // block,), in_specs=in_specs, out_specs=out_specs
        ),
        out_shape=out_shape,
        compiler_params=params(),
        cost_estimate=cost(20 * count * width, moved),
        name=name,
    )(*(() if counts is None else (counts,)), *inputs, *whole_inputs)


def interleaved(key, value):
    width = key.shape[1]
    pieces = []
    for start in range(0, width, PAIR):
        pieces += [key[:, start : start + PAIR], value[:, start : start + PAIR]]
    return jnp.concatenate(pieces, axis=1)


def apart(both):
    keys, values = [], []
    for start in range(0, both.shape[1], 2 * PAIR):
        keys.append(both[:, start : start + PAIR])
        values.append(both[:, start + PAIR : start + 2 * PAIR])
    return jnp.concatenate(keys, axis=1), jnp.concatenate(values, axis=1)


def on_device(
    block_input,
    lengths,
    cotangent,
    query_weight,
    query_bias,
    key_weight,
    value_weight,
    value_bias,
    output_weight,
    output_bias,
    first_gain,
    first_shift,
    inner_weight,
    inner_bias,
    outer_weight,
    closing_offset_vector,
    second_gain,
    second_shift,
):
    seqs, local, width = block_input.shape
    chip = 2 * local
    spots = lax.axis_size("ctx")
    spot = lax.axis_index("ctx")
    part = lax.axis_index("tp")
    core, side = part % 2, part // 2
    is_upper_core, is_upper_side = core == 1, side == 1
    span = local * lax.axis_size("tp")
    heads_width = query_weight.shape[1]
    unit_width = inner_weight.shape[1]
    count = seqs * local

    def other_core(value, **ties):
        return swap(value, "tp", 1, **ties)

    def other_side(value, **ties):
        return swap(value, "tp", 2, **ties)

    def flat(value):
        return value.reshape(-1, value.shape[-1])

    starts = jnp.stack([(spot ^ k) * span + side * chip for k in range(spots)])
    key_counts = jnp.clip(lengths[:, None] - starts[None, :], 0, chip)
    counts = jnp.concatenate([key_counts, jnp.full((seqs, 1), spot, jnp.int32)], axis=1).astype(jnp.int32)
    row_counts = jnp.clip(lengths - (spot * span + part * local), 0, local).astype(jnp.int32)
    where = jnp.stack([core, lax.axis_index("dp")]).astype(jnp.int32)

    def together(*values):
        return lax.optimization_barrier(values)

    def over_spots(value, done=()):
        return [swap(value, "ctx", k, (), done) for k in range(1, spots)]

    lines = lax.axis_size("dp")
    own_width = 2 * heads_width
    attention_shard = pack([query_weight, key_weight, value_weight], [False] * 3)
    feed_shard = pack([output_weight, inner_weight, outer_weight], [True, False, True])
    biases = jnp.concatenate([query_bias, value_bias, inner_bias])[None, :]
    x_rows = [block_input[s] for s in range(seqs)]

    came, biases_came, *near = together(other_core(block_input), other_side(biases), *over_spots(attention_shard))
    attention_near = stack([attention_shard] + near)

    def send_near(own):
        return [swap(own, "ctx", 2), swap(own, "ctx", 1)] if spots == 4 else over_spots(own)

    def send_last(own, far):
        return [
            lax.ppermute(own, "ctx", [(1, 2), (2, 1)]),
            lax.ppermute(far, "ctx", [(2, 3), (1, 0)]),
        ]

    def finish(nears, lasts):
        if spots != 4:
            return nears
        in_middle = jnp.logical_or(spot == 1, spot == 2)
        return [nears[1], nears[0], jnp.where(in_middle, lasts[0], lasts[1])]

    begin = together(attention_near, *x_rows)
    attention_near, first_rows_out = begin[0], begin[1]
    attention_other, attention_line, across_0, *nears = together(
        other_side(attention_near),
        swap(attention_near, "dp", 1),
        other_side(first_rows_out),
        *send_near(first_rows_out),
    )
    other_line = swap(attention_other, "dp", 1)
    across = [across_0, other_side(after(x_rows[1], attention_other))]
    cores = [other_core(n) for n in nears]
    lasts = send_last(after(x_rows[0], *nears), nears[0]) if spots == 4 else []
    other_line, across[1], *rest = together(other_line, across[1], *lasts, *cores)
    lasts, cores = rest[: len(lasts)], rest[len(lasts) :]
    arrived = [finish(nears, lasts)]
    if spots == 4:
        cores = [cores[1], cores[0], other_core(arrived[0][2])]
    if lines == 2:
        attention_all = [[attention_near, attention_other], [attention_line, other_line]]
    else:
        attention_all = over_dp([attention_near, attention_other])
    query_full, kv_full = place(attention_all, [heads_width] * 3, [(0,), (1, 2)])

    query_b = ordered(biases[:, :heads_width], biases_came[:, :heads_width], is_upper_side, 1)
    cut = slice(heads_width, own_width)
    value_b = ordered(biases[:, cut], biases_came[:, cut], is_upper_side, 1)
    cut = slice(own_width, None)
    inner_b = ordered(biases[:, cut], biases_came[:, cut], is_upper_side, 1)
    kv_bias = interleaved(jnp.zeros_like(value_b), value_b)

    pieces = [[(x_rows[0], came[0])] + list(zip(arrived[0], cores))]
    across_core = other_core(across[0])
    feed_shard = after(feed_shard, arrived[0][-1])
    feed_near = over_spots(feed_shard)
    second_nears = send_near(after(x_rows[1], arrived[0][-1]))
    q, made = project(where, pieces[0] + [(across[0], across_core)], query_full, kv_full, query_b, kv_bias)
    queries, kv = [q], [made]
    own, packed, lse = attend(counts[0], spots, seqs, 0, q, made, ())
    packs = [packed]

    own, *rest = together(own, *feed_near, *second_nears)
    feed_near, nears = rest[: len(feed_near)], rest[len(feed_near) :]
    across_core = other_core(across[1])
    feed_near = stack([feed_shard] + feed_near)
    second = after(x_rows[1], own)
    cores = [other_core(n) for n in nears]
    lasts = send_last(after(second, *nears), nears[0]) if spots == 4 else []
    feed_other, near_line, *rest = together(other_side(feed_near), swap(feed_near, "dp", 1), *lasts, *cores)
    lasts, cores = rest[: len(lasts)], rest[len(lasts) :]
    arrived.append(finish(nears, lasts))
    if spots == 4:
        cores = [cores[1], cores[0], other_core(arrived[1][2])]
    pieces.append([(x_rows[1], came[1])] + list(zip(arrived[1], cores)))
    packs[0] = other_side(after(packs[0], feed_other))
    q, made = project(where, pieces[1] + [(across[1], across_core)], query_full, kv_full, query_b, kv_bias)
    queries.append(q)
    kv.append(made)
    own, packed, lse = attend(counts[1], spots, seqs, 1, q, made, (own, lse))
    packs.append(other_side(packed))
    buffers = (own, lse)
    if lines == 2:
        feed_all = [[feed_near, feed_other], [near_line, swap(feed_other, "dp", 1, (), (own,))]]
    else:
        feed_all = over_dp([feed_near, feed_other])
    output_full, inner_full, outer_full = place(feed_all, [heads_width, unit_width, unit_width], [(0,), (1,), (2,)])

    vectors = jnp.stack([output_bias, first_gain, first_shift, closing_offset_vector, second_gain, second_shift])
    vectors = jnp.concatenate([vectors, jnp.zeros((2, width), F32)])
    block = local // 2

    attended, attended_low, mine, other, lse_all = merge(where, *buffers, packs, output_full)
    normal, spread, first_low = row_call(
        first_kernel,
        "first_norm",
        block,
        count,
        width,
        [flat(block_input), flat(mine), flat(other_core(other))],
        [vectors],
        [(width, F32), (1, F32), (width, BF)],
        False,
    )
    first_came = other_core(first_low)
    active, slope, mine, other = feed(first_low, first_came, inner_full, inner_b, outer_full)
    output, second_grad, outer_low, second_sums = row_call(
        functools.partial(second_kernel, local // block),
        "second_norm",
        block,
        count,
        width,
        [normal, mine, other_core(other), flat(cotangent)],
        [vectors],
        [(width, F32), (width, F32), (width, BF)],
        True,
        row_counts,
    )
    mine, other, d_inner_bias, *d_feed = feed_back(
        where, outer_low, other_core(outer_low), first_low, first_came, active, slope, inner_full, outer_full
    )
    first_grad, attn_low, first_sums = row_call(
        first_back_kernel,
        "first_norm_back",
        block,
        count,
        width,
        [second_grad, mine, other_core(other), normal, spread],
        [vectors],
        [(width, F32), (width, BF)],
        True,
    )
    attn_low = attn_low.reshape(seqs, local, width)
    turned = turn(
        where, attn_low, other_core(attn_low), output_full, attended, attended_low, lse_all
    )
    g_own, d_output = turned[:seqs], turned[seqs:]
    g_oth = [other_side(g) for g in g_own]

    lines = lax.axis_size("dp")

    def over_lines(made, done=()):
        if lines == 2:
            return made[0], swap(made[1], "dp", 1, (), done)
        value, place_at = made[0].astype(F32), lax.axis_index("dp")
        for bit in reversed(bits_of("dp")):
            mine, sent = halves(value, (place_at & bit) != 0, 0)
            term = swap(sent.astype(BF), "dp", bit, (), done)
            value = mine + term.astype(F32)
        return mine, term

    def sides_of(pair, width_of_side):
        return [(pair, 0, width_of_side)], [(pair, width_of_side, width_of_side)]

    def kv_step(s, dkv, before):
        mine, other, bias, *grads = kv_back(where, pieces[s], dkv, kv_full, before, s == seqs - 1)
        total = (mine + other_core(other).astype(F32)).reshape(spots, local, width)
        return total[0], [total[k].astype(BF) for k in range(1, spots)], bias, grads

    own, oth, dkv = attend_back(counts[0], spots, queries[0], g_own[0], g_oth[0], kv[0])
    dq_own, dq_came = [own], [other_side(oth)]
    feed_pairs = [over_lines(d_feed, (dkv,))]
    output_pair = over_lines(d_output, (dkv,))
    kept_0, sent_0, kv_bias_sum, kv_grads = kv_step(0, dkv, None)
    feed_kept, feed_sent = fold_sides(
        feed_pairs,
        [
            sides_of(0, unit_width),
            ([(0, 2 * unit_width, unit_width)], [(0, 3 * unit_width, unit_width)]),
        ],
    )
    feed_term = other_side(feed_sent)
    came_0 = [swap(t, "ctx", k + 1) for k, t in enumerate(sent_0)]
    g_in = after(g_oth[1], feed_sent, *sent_0)
    own, oth, dkv = attend_back(counts[1], spots, queries[1], g_own[1], g_in, kv[1])
    dq_own.append(own)
    dq_came.append(other_side(oth))

    dkv, feed_term, *came_0 = together(dkv, feed_term, *came_0)
    feed_rows = fold_spots(feed_kept, feed_term)
    feed_terms = [swap(t, "ctx", k + 1) for k, t in enumerate(feed_rows[1:])]
    dkv = after(dkv, *feed_rows)
    kept_1, sent_1, kv_bias_sum, kv_grads = kv_step(1, dkv, (kv_grads[0], kv_bias_sum))
    kv_pair = over_lines(kv_grads)
    mine, other, query_bias_sum, *query_grads = query_back(
        where, dq_own, [dq_came[0], after(dq_came[1], *kv_grads)], x_rows, [came[s] for s in range(seqs)], query_full
    )
    query_term = (mine + other_core(other).astype(F32)).reshape(seqs, local, width)
    query_pair = over_lines(query_grads)
    value_bias_sum = apart(kv_bias_sum)[1]
    shared = jnp.concatenate([second_sums[:3], first_sums[:3]])
    shared = shared + other_core(shared)
    vector = jnp.concatenate(
        [shared.reshape(1, -1), d_inner_bias, query_bias_sum.reshape(1, -1), value_bias_sum], axis=1
    )
    for bit in bits_of("dp"):
        vector = vector + swap(vector, "dp", bit)
    if lines == 2:
        query_last, kv_last, vector, *feed_terms = together(query_pair[1], kv_pair[1], vector, *feed_terms)
        query_pair, kv_pair = (query_pair[0], query_last), (kv_pair[0], kv_last)
    came_1 = [swap(after(t, vector), "ctx", k + 1) for k, t in enumerate(sent_1)]

    def side_cuts(pair, offset):
        cuts = []
        for start in (0, heads_width):
            pieces_of, at = [], start
            while at < start + heads_width:
                w = min(PAIR - at % PAIR, start + heads_width - at)
                pieces_of.append((pair, 2 * (at - at % PAIR) + offset + at % PAIR, w))
                at += w
            cuts.append(pieces_of)
        return tuple(cuts)

    kept, sent = fold_sides(
        [query_pair, kv_pair, output_pair],
        [sides_of(0, heads_width), side_cuts(1, 0), side_cuts(1, PAIR), sides_of(2, heads_width)],
    )
    term, *came_1 = together(other_side(sent), *came_1)
    rows = fold_spots(kept, term)
    vector = vector + sum(swap(vector, "ctx", k) for k in range(1, spots))
    terms = [swap(t, "ctx", k + 1) for k, t in enumerate(rows[1:])]
    vector = (vector + other_side(vector))[0]
    feed_owned = feed_rows[0] + sum(t.astype(F32) for t in feed_terms)
    owned = rows[0] + sum(t.astype(F32) for t in terms)
    first_grad = first_grad.reshape(seqs, local, width)
    input_grad = jnp.stack(
        [
            first_grad[s] + query_term[s] + kept + sum(t.astype(F32) for t in came)
            for s, (kept, came) in enumerate(((kept_0, came_0), (kept_1, came_1)))
        ]
    )

    shared = vector[: 6 * width].reshape(6, width)

    def own_side(start, size):
        return jnp.where(is_upper_side, vector[start + size : start + 2 * size], vector[start : start + size])

    base = 6 * width
    after_inner = base + 2 * unit_width
    return (
        output.reshape(seqs, local, width),
        input_grad,
        owned[:, :heads_width],
        own_side(after_inner, heads_width),
        owned[:, heads_width:own_width],
        owned[:, own_width : own_width + heads_width],
        own_side(after_inner + own_width, heads_width),
        owned[:, 3 * heads_width : 4 * heads_width].T,
        shared[5],
        shared[3],
        shared[4],
        feed_owned[:, :unit_width],
        own_side(base, unit_width),
        feed_owned[:, unit_width : 2 * unit_width].T,
        shared[2],
        shared[0],
        shared[1],
    )


def solution(mesh):
    rows = P("dp", ("ctx", "tp"), None)
    into = P(("dp", "ctx"), "tp")
    out_of = P("tp", ("dp", "ctx"))
    split, whole = P("tp"), P()
    return jax.shard_map(
        on_device,
        mesh=mesh,
        in_specs=(
            rows, P("dp"), rows, into, split, into, into, split, out_of, whole, whole, whole,
            into, split, out_of, whole, whole, whole,
        ),
        out_specs=(
            rows, rows, into, split, into, into, split, out_of, whole, whole, whole,
            into, split, out_of, whole, whole, whole,
        ),
        check_vma=False,
    )
```

profile of v0, /device:TPU:0, one launch (start us, length us, event | category | flops | bytes accessed | tf_op | source)
XLA Modules:
  0.0 516.5 jit_solution(13779542263595893797)
XLA Ops:
  2.9 4.6 collective-permute-start.4
  12.5 6.3 %collective-permute-done.3.refs_2_ = bf16[96,640]{1,0:T(8,128)(2,1)S(1)} collective-permute-done((bf16[96,640]{1,0:T(8,128)(2,1)}, bf16[96,640]{1,0:T(8,128)(2,1)S(1)}, u32[]{:S(2)}, u32[]{:S(2)}) %collective-permute-start.3) | collective-permute-done | bytes 122912 | tf_op jit(solution)/shard_map/ppermute | solution.py:46
  19.4 1.9 stack.87.refs_0_
  25.3 2.1 pack.3.refs_0_
  27.4 3.0 collective-permute-start.8
  31.7 14.1 %collective-permute-done.9.refs_2_ = bf16[256,768]{1,0:T(8,128)(2,1)S(1)} collective-permute-done((bf16[256,768]{1,0:T(8,128)(2,1)S(1)}, bf16[256,768]{1,0:T(8,128)(2,1)S(1)}, u32[]{:S(2)}, u32[]{:S(2)}) %collective-permute-start.9) | collective-permute-done | bytes 393248 | tf_op jit(solution)/shard_map/ppermute | solution.py:46
  52.0 10.3 %collective-permute-done.11.refs_8_ = bf16[256,768]{1,0:T(8,128)(2,1)} collective-permute-done((bf16[256,768]{1,0:T(8,128)(2,1)S(1)}, bf16[256,768]{1,0:T(8,128)(2,1)}, u32[]{:S(2)}, u32[]{:S(2)}) %collective-permute-start.11) | collective-permute-done | bytes 393248 | tf_op jit(solution)/shard_map/ppermute | solution.py:46
  65.8 2.4 collective-permute-start.20
  68.2 3.1 collective-permute-start.19
  71.3 3.8 place.2
  75.1 2.1 collective-permute-start.22
  78.0 8.9 %project.2 = (bf16[1024,384]{1,0:T(8,128)(2,1)}, bf16[2048,768]{1,0:T(8,128)(2,1)}) custom-call(s32[2]{0:T(128)} %pad_add_fusion.where, bf16[256,768]{1,0:T(8,128)(2,1)} %copy-done.2, bf16[256,768]{1,0:T(8,128)(2,1)} %get-tuple-element.342.refs_1_.refs_6_, bf16[256,768]{1,0:T(8,128)(2,1)} %copy-done.50, bf16[256,768]{1,0:T(8,128)(2,1)} %copy-done.54, ...), custom_call_target="tpu_custom_call" | custom-call | flops 3019898880 | bytes 7077888 | tf_op jit(solution)/shard_map/project/pallas_call | solution.py:268
  86.8 8.5 %attend.2 = (f32[2,384,512]{2,1,0:T(8,128)}, bf16[432,512]{1,0:T(8,128)(2,1)}, f32[2,3,2,512]{3,2,1,0:T(2,128)}) custom-call(s32[5]{0:T(128)} %get-tuple-element.360.counts, bf16[1024,384]{1,0:T(8,128)(2,1)} %get-tuple-element.174.queries.both, bf16[2048,768]{1,0:T(8,128)(2,1)} %get-tuple-element.175.kv), custom_call_target="tpu_custom_call" | custom-call | flops 12884901888 | bytes 6291456 | tf_op jit(solution)/shard_map/attend/pallas_call | solution.py:565
  95.4 5.0 collective-permute-done.19.refs_2_
  100.4 2.2 collective-permute-done.22.refs_2_
  102.6 14.5 %collective-permute-done.21.refs_4_ = bf16[256,768]{1,0:T(8,128)(2,1)S(1)} collective-permute-done((bf16[256,768]{1,0:T(8,128)(2,1)S(1)}, bf16[256,768]{1,0:T(8,128)(2,1)S(1)}, u32[]{:S(2)}, u32[]{:S(2)}) %collective-permute-start.21) | collective-permute-done | bytes 393248 | tf_op jit(solution)/shard_map/ppermute | solution.py:46
  117.1 2.6 stack.88.refs_0_
  124.0 17.9 %collective-permute-done.26 = bf16[256,768]{1,0:T(8,128)(2,1)S(1)} collective-permute-done((bf16[256,768]{1,0:T(8,128)(2,1)S(1)}, bf16[256,768]{1,0:T(8,128)(2,1)S(1)}, u32[]{:S(2)}, u32[]{:S(2)}) %collective-permute-start.26) | collective-permute-done | bytes 393248 | tf_op jit(solution)/shard_map/ppermute | solution.py:1146
  141.8 10.3 %collective-permute-done.24.refs_2_ = bf16[384,1792]{1,0:T(8,128)(2,1)S(1)} collective-permute-done((bf16[384,1792]{1,0:T(8,128)(2,1)}, bf16[384,1792]{1,0:T(8,128)(2,1)S(1)}, u32[]{:S(2)}, u32[]{:S(2)}) %collective-permute-start.24) | collective-permute-done | bytes 1376288 | tf_op jit(solution)/shard_map/ppermute | solution.py:46
  156.1 8.9 %project.3 = (bf16[1024,384]{1,0:T(8,128)(2,1)}, bf16[2048,768]{1,0:T(8,128)(2,1)}) custom-call(s32[2]{0:T(128)} %pad_add_fusion.where, bf16[256,768]{1,0:T(8,128)(2,1)} %copy-done.3, bf16[256,768]{1,0:T(8,128)(2,1)} %get-tuple-element.343.refs_1_.refs_7_, bf16[256,768]{1,0:T(8,128)(2,1)} %copy-done.52, bf16[256,768]{1,0:T(8,128)(2,1)} %copy-done.56, ...), custom_call_target="tpu_custom_call" | custom-call | flops 3019898880 | bytes 7077888 | tf_op jit(solution)/shard_map/project/pallas_call | solution.py:268
  165.0 13.3 %attend.3 = (f32[2,384,512]{2,1,0:T(8,128)}, bf16[432,512]{1,0:T(8,128)(2,1)}, f32[2,3,2,512]{3,2,1,0:T(2,128)}) custom-call(s32[5]{0:T(128)} %get-tuple-element.361.counts, bf16[1024,384]{1,0:T(8,128)(2,1)} %get-tuple-element.192.queries.both, bf16[2048,768]{1,0:T(8,128)(2,1)} %get-tuple-element.193.kv, ...), custom_call_target="tpu_custom_call", output_to_operand_aliasing={{0}: (3, {}), {2}: (4, {})} | custom-call | flops 12884901888 | bytes 6291456 | tf_op jit(solution)/shard_map/attend/pallas_call | solution.py:565
  178.3 6.8 %collective-permute-done.33.refs_3_ = bf16[384,1792]{1,0:T(8,128)(2,1)S(1)} collective-permute-done((bf16[384,1792]{1,0:T(8,128)(2,1)S(1)}, bf16[384,1792]{1,0:T(8,128)(2,1)S(1)}, u32[]{:S(2)}, u32[]{:S(2)}) %collective-permute-start.33) | collective-permute-done | bytes 1376288 | tf_op jit(solution)/shard_map/ppermute | solution.py:46
  186.2 6.8 %place.3 = (bf16[768,384]{1,0:T(8,128)(2,1)}, bf16[768,1536]{1,0:T(8,128)(2,1)}, bf16[768,1536]{1,0:T(8,128)(2,1)}) custom-call(s32[3]{0:T(128)} %pad_add_fusion.2.where, bf16[384,1792]{1,0:T(8,128)(2,1)} %stack.88.refs_0_, bf16[384,1792]{1,0:T(8,128)(2,1)} %copy-done.6, bf16[384,1792]{1,0:T(8,128)(2,1)} %copy-done.5, bf16[384,1792]{1,0:T(8,128)(2,1)} %copy-done.7), custom_call_target="tpu_custom_call" | custom-call | bytes 16121856 | tf_op jit(solution)/shard_map/place/pallas_call | solution.py:68
  194.1 5.1 merge.1
  202.5 4.5 first_norm.1
  210.4 14.9 %feed.1 = (bf16[1024,1536]{1,0:T(8,128)(2,1)}, bf16[1024,1536]{1,0:T(8,128)(2,1)}, f32[512,768]{1,0:T(8,128)}, bf16[512,768]{1,0:T(8,128)(2,1)}) custom-call(bf16[512,768]{1,0:T(8,128)(2,1)} %get-tuple-element.207.own_ref, bf16[512,768]{1,0:T(8,128)(2,1)} %copy-done.46, bf16[768,1536]{1,0:T(8,128)(2,1)} %get-tuple-element.208.w_in, ...), custom_call_target="tpu_custom_call" | custom-call | flops 4831838208 | bytes 15728640 | tf_op jit(solution)/shard_map/feed/pallas_call | solution.py:874
  226.0 1.8 collective-permute-done.36.came_ref
  228.7 6.1 %second_norm.1 = (f32[512,768]{1,0:T(8,128)}, f32[512,768]{1,0:T(8,128)}, bf16[512,768]{1,0:T(8,128)(2,1)}, f32[8,768]{1,0:T(8,128)}) custom-call(s32[2]{0:T(128)} %subtract_clamp_fusion.1.counts, f32[512,768]{1,0:T(8,128)} %get-tuple-element.206.normal_ref, f32[512,768]{1,0:T(8,128)} %get-tuple-element.210.mine_ref, bf16[512,768]{1,0:T(8,128)(2,1)} %copy-done.10, ...), custom_call_target="tpu_custom_call" | custom-call | flops 7864320 | bytes 9437184 | tf_op jit(solution)/shard_map/second_norm/pallas_call | solution.py:1049
  235.0 2.4 collective-permute-done.37.low_came
  238.3 19.5 %feed_back.1 = (f32[512,768]{1,0:T(8,128)}, bf16[512,768]{1,0:T(8,128)(2,1)}, f32[1,1536]{1,0:T(1,128)}, bf16[384,3072]{1,0:T(8,128)(2,1)}, bf16[384,3072]{1,0:T(8,128)(2,1)}) custom-call(s32[2]{0:T(128)} %pad_add_fusion.where, bf16[512,768]{1,0:T(8,128)(2,1)} %get-tuple-element.214.low_own, bf16[512,768]{1,0:T(8,128)(2,1)} %copy-done.47, ...), custom_call_target="tpu_custom_call" | custom-call | flops 9663676416 | bytes 22020096 | tf_op jit(solution)/shard_map/feed_back/pallas_call | solution.py:948
  258.0 2.4 collective-permute-done.38.came_ref
  261.2 5.1 first_norm_back.1
  266.5 2.4 collective-permute-done.39.came_ref
  269.7 7.0 %turn.1 = (bf16[432,512]{1,0:T(8,128)(2,1)}, bf16[432,512]{1,0:T(8,128)(2,1)}, f32[384,384]{1,0:T(8,128)}, bf16[384,384]{1,0:T(8,128)(2,1)}) custom-call(s32[2]{0:T(128)} %pad_add_fusion.where, bf16[2,256,768]{2,1,0:T(8,128)(2,1)} %bitcast.44, bf16[2,256,768]{2,1,0:T(8,128)(2,1)} %copy-done.11, bf16[768,384]{1,0:T(8,128)(2,1)} %get-tuple-element.203.refs_2_.weight, ...), custom_call_target="tpu_custom_call" | custom-call | flops 1207959552 | bytes 4718592 | tf_op jit(solution)/shard_map/turn/pallas_call | solution.py:801
  278.7 10.4 %collective-permute-done.40.g_oth = bf16[432,512]{1,0:T(8,128)(2,1)S(1)} collective-permute-done((bf16[432,512]{1,0:T(8,128)(2,1)}, bf16[432,512]{1,0:T(8,128)(2,1)S(1)}, u32[]{:S(2)}, u32[]{:S(2)}) %collective-permute-start.40) | collective-permute-done | bytes 442400 | tf_op jit(solution)/shard_map/ppermute | solution.py:46
  289.9 12.9 %attend_back.2 = (f32[384,512]{1,0:T(8,128)}, bf16[384,512]{1,0:T(8,128)(2,1)}, bf16[2048,768]{1,0:T(8,128)(2,1)}) custom-call(s32[5]{0:T(128)} %get-tuple-element.360.counts, bf16[1024,384]{1,0:T(8,128)(2,1)} %get-tuple-element.174.queries.both, bf16[432,512]{1,0:T(8,128)(2,1)} %get-tuple-element.225.g_own, bf16[432,512]{1,0:T(8,128)(2,1)} %copy-done.49, ...), custom_call_target="tpu_custom_call" | custom-call | flops 32212254720 | bytes 9437184 | tf_op jit(solution)/shard_map/attend_back/pallas_call | solution.py:659
  302.8 14.1 %kv_back.2 = (f32[1024,768]{1,0:T(8,128)}, bf16[1024,768]{1,0:T(8,128)(2,1)}, f32[1,768]{1,0:T(1,128)}, f32[768,768]{1,0:T(8,128)}) custom-call(s32[2]{0:T(128)} %pad_add_fusion.where, bf16[256,768]{1,0:T(8,128)(2,1)} %copy-done.2, bf16[256,768]{1,0:T(8,128)(2,1)} %get-tuple-element.342.refs_1_.refs_6_, bf16[256,768]{1,0:T(8,128)(2,1)} %copy-done.50, ...), custom_call_target="tpu_custom_call" | custom-call | flops 4831838208 | bytes 11796480 | tf_op jit(solution)/shard_map/kv_back/pallas_call | solution.py:367
  317.5 2.5 collective-permute-done.54
  320.1 25.2 %collective-permute-start.59 = (bf16[384,384]{1,0:T(8,128)(2,1)}, bf16[384,384]{1,0:T(8,128)(2,1)}, u32[]{:S(2)}, u32[]{:S(2)}) collective-permute-start(bf16[384,384]{1,0:T(8,128)(2,1)} %get-tuple-element.270), channel_id=1, source_target_pairs={{0,16},{16,0},{1,17},{17,1},{2,18},{18,2},{3,19},{19,3},{4,20},{20... | collective-permute-start | bytes 884744 | tf_op jit(solution)/shard_map/ppermute | solution.py:46
  347.2 5.0 fold_sides.2
  355.6 2.4 collective-permute-start.49
  360.1 23.1 %attend_back.3 = (f32[384,512]{1,0:T(8,128)}, bf16[384,512]{1,0:T(8,128)(2,1)}, bf16[2048,768]{1,0:T(8,128)(2,1)}) custom-call(s32[5]{0:T(128)} %get-tuple-element.361.counts, bf16[1024,384]{1,0:T(8,128)(2,1)} %get-tuple-element.192.queries.both, bf16[432,512]{1,0:T(8,128)(2,1)} %get-tuple-element.227.g_own, bf16[432,512]{1,0:T(8,128)(2,1)} %collective-permute-done.41.g_oth, ...), custom_call_target="tpu_custom_call" | custom-call | flops 32212254720 | bytes 9437184 | tf_op jit(solution)/shard_map/attend_back/pallas_call | solution.py:659
  383.4 1.9 collective-permute-start.45
  385.3 5.2 %collective-permute-done.48 = bf16[256,768]{1,0:T(8,128)(2,1)S(1)} collective-permute-done((bf16[256,768]{1,0:T(8,128)(2,1)S(1)}, bf16[256,768]{1,0:T(8,128)(2,1)S(1)}, u32[]{:S(2)}, u32[]{:S(2)}) %collective-permute-start.48) | collective-permute-done | bytes 393248 | tf_op jit(solution)/shard_map/ppermute | solution.py:46
  390.5 3.6 fold_spots.2
  394.1 14.4 %kv_back.3 = (f32[1024,768]{1,0:T(8,128)}, bf16[1024,768]{1,0:T(8,128)(2,1)}, f32[1,768]{1,0:T(1,128)}, f32[384,768]{1,0:T(8,128)}, bf16[384,768]{1,0:T(8,128)(2,1)}) custom-call(s32[2]{0:T(128)} %pad_add_fusion.where, bf16[256,768]{1,0:T(8,128)(2,1)} %copy-done.3, bf16[256,768]{1,0:T(8,128)(2,1)} %get-tuple-element.343.refs_1_.refs_7_, ...), custom_call_target="tpu_custom_call" | custom-call | flops 4831838208 | bytes 11796480 | tf_op jit(solution)/shard_map/kv_back/pallas_call | solution.py:367
  408.5 2.8 collective-permute-start.53
  412.3 6.2 %query_back.1 = (f32[512,768]{1,0:T(8,128)}, bf16[512,768]{1,0:T(8,128)(2,1)}, f32[384,1]{1,0:T(8,128)}, f32[384,384]{1,0:T(8,128)}, bf16[384,384]{1,0:T(8,128)(2,1)}) custom-call(s32[2]{0:T(128)} %pad_add_fusion.where, f32[384,512]{1,0:T(8,128)} %get-tuple-element.226.refs_0_, f32[384,512]{1,0:T(8,128)} %get-tuple-element.236.refs_1_, ...), custom_call_target="tpu_custom_call" | custom-call | flops 1207959552 | bytes 8848896 | tf_op jit(solution)/shard_map/query_back/pallas_call | solution.py:68
  421.7 2.0 collective-permute-start.52
  424.3 2.3 collective-permute-start.57
  430.4 5.7 %collective-permute-done.56 = bf16[96,1536]{1,0:T(8,128)(2,1)S(1)} collective-permute-done((bf16[96,1536]{1,0:T(8,128)(2,1)}, bf16[96,1536]{1,0:T(8,128)(2,1)S(1)}, u32[]{:S(2)}, u32[]{:S(2)}) %collective-permute-start.56) | collective-permute-done | bytes 294944 | tf_op jit(solution)/shard_map/ppermute | solution.py:46
  436.1 11.6 %collective-permute-done.57 = bf16[96,1536]{1,0:T(8,128)(2,1)S(1)} collective-permute-done((bf16[96,1536]{1,0:T(8,128)(2,1)}, bf16[96,1536]{1,0:T(8,128)(2,1)S(1)}, u32[]{:S(2)}, u32[]{:S(2)}) %collective-permute-start.57) | collective-permute-done | bytes 294944 | tf_op jit(solution)/shard_map/ppermute | solution.py:46
  447.6 1.9 collective-permute-start.69
  449.6 3.5 collective-permute-start.68
  458.3 4.3 fold_sides.3
  465.0 2.7 fusion.7
  468.5 2.0 collective-permute-start.62
  474.3 6.7 %collective-permute-done.61 = bf16[256,768]{1,0:T(8,128)(2,1)} collective-permute-done((bf16[256,768]{1,0:T(8,128)(2,1)S(1)}, bf16[256,768]{1,0:T(8,128)(2,1)}, u32[]{:S(2)}, u32[]{:S(2)}) %collective-permute-start.61) | collective-permute-done | bytes 393248 | tf_op jit(solution)/shard_map/ppermute | solution.py:46
  480.9 15.9 %collective-permute-done.62 = bf16[256,768]{1,0:T(8,128)(2,1)} collective-permute-done((bf16[256,768]{1,0:T(8,128)(2,1)S(1)}, bf16[256,768]{1,0:T(8,128)(2,1)}, u32[]{:S(2)}, u32[]{:S(2)}) %collective-permute-start.62) | collective-permute-done | bytes 393248 | tf_op jit(solution)/shard_map/ppermute | solution.py:46
  496.8 2.4 fold_spots.3
  499.2 4.9 collective-permute-start.64
  504.6 1.9 collective-permute-start.66
  506.5 2.5 fusion.3
  510.3 4.5 collective-permute-done.65
  (296 shorter events, 79.8 us)
Async XLA Ops:
  0.7 18.1 %collective-permute-start = (bf16[2,256,768]{2,1,0:T(8,128)(2,1)}, bf16[2,256,768]{2,1,0:T(8,128)(2,1)S(1)}, u32[]{:S(2)}, u32[]{:S(2)}) collective-permute-start(bf16[2,256,768]{2,1,0:T(8,128)(2,1)} %param.18), channel_id=1, source_target_pairs={{0,1},{1,0},{2,3},{3,2},{4,5},{5,4},{6,7},{7,6},{8,9},{9,8},{10,11... | collective-permute-start | bytes 2359304 | tf_op jit(solution)/shard_map/ppermute | solution.py:46
  2.9 9.6 %collective-permute-start.4 = (bf16[96,640]{1,0:T(8,128)(2,1)}, bf16[96,640]{1,0:T(8,128)(2,1)S(1)}, u32[]{:S(2)}, u32[]{:S(2)}) collective-permute-start(bf16[96,640]{1,0:T(8,128)(2,1)} %pack.2.refs_0_), channel_id=1, source_target_pairs={{0,12},{4,8},{8,4},{12,0},{1,13},{5,9},{9,5},{13,1},{2,14},{6,10},... | collective-permute-start | bytes 368648 | tf_op jit(solution)/shard_map/ppermute | solution.py:46
  7.5 11.2 %collective-permute-start.3 = (bf16[96,640]{1,0:T(8,128)(2,1)}, bf16[96,640]{1,0:T(8,128)(2,1)S(1)}, u32[]{:S(2)}, u32[]{:S(2)}) collective-permute-start(bf16[96,640]{1,0:T(8,128)(2,1)} %pack.2.refs_0_), channel_id=1, source_target_pairs={{0,8},{4,12},{8,0},{12,4},{1,9},{5,13},{9,1},{13,5},{2,10},{6,14},... | collective-permute-start | bytes 368648 | tf_op jit(solution)/shard_map/ppermute | solution.py:46
  7.5 11.2 %collective-permute-start.2 = (bf16[96,640]{1,0:T(8,128)(2,1)}, bf16[96,640]{1,0:T(8,128)(2,1)S(1)}, u32[]{:S(2)}, u32[]{:S(2)}) collective-permute-start(bf16[96,640]{1,0:T(8,128)(2,1)} %pack.2.refs_0_), channel_id=1, source_target_pairs={{0,4},{4,0},{8,12},{12,8},{1,5},{5,1},{9,13},{13,9},{2,6},{6,2},{1... | collective-permute-start | bytes 368648 | tf_op jit(solution)/shard_map/ppermute | solution.py:46
  8.9 3.6 collective-permute-start.1
  21.3 25.7 %collective-permute-start.6 = (bf16[384,640]{1,0:T(8,128)(2,1)}, bf16[384,640]{1,0:T(8,128)(2,1)S(1)}, u32[]{:S(2)}, u32[]{:S(2)}) collective-permute-start(bf16[384,640]{1,0:T(8,128)(2,1)} %stack.87.refs_0_), channel_id=1, source_target_pairs={{0,16},{16,0},{1,17},{17,1},{2,18},{18,2},{3,19},{19,3},{4,20},{20... | collective-permute-start | bytes 1474568 | tf_op jit(solution)/shard_map/ppermute | solution.py:46
  22.8 24.2 %collective-permute-start.5 = (bf16[384,640]{1,0:T(8,128)(2,1)}, bf16[384,640]{1,0:T(8,128)(2,1)S(1)}, u32[]{:S(2)}, u32[]{:S(2)}) collective-permute-start(bf16[384,640]{1,0:T(8,128)(2,1)} %stack.87.refs_0_), channel_id=1, source_target_pairs={{0,2},{1,3},{2,0},{3,1},{4,6},{5,7},{6,4},{7,5},{8,10},{9,11},{10,... | collective-permute-start | bytes 1474568 | tf_op jit(solution)/shard_map/ppermute | solution.py:46
  27.4 18.4 %collective-permute-start.9 = (bf16[256,768]{1,0:T(8,128)(2,1)S(1)}, bf16[256,768]{1,0:T(8,128)(2,1)S(1)}, u32[]{:S(2)}, u32[]{:S(2)}) collective-permute-start(bf16[256,768]{1,0:T(8,128)(2,1)S(1)} %get-tuple-element.163.refs_0_.refs_4_), channel_id=1, source_target_pairs={{0,4},{4,0},{8,12},{12,8},{1,5},{5,1},{9,13},{13,9},{2,6},{6,2},{1... | collective-permute-start | bytes 1179656 | tf_op jit(solution)/shard_map/ppermute | solution.py:46
  27.4 19.7 %collective-permute-start.8 = (bf16[256,768]{1,0:T(8,128)(2,1)S(1)}, bf16[256,768]{1,0:T(8,128)(2,1)S(1)}, u32[]{:S(2)}, u32[]{:S(2)}) collective-permute-start(bf16[256,768]{1,0:T(8,128)(2,1)S(1)} %get-tuple-element.163.refs_0_.refs_4_), channel_id=1, source_target_pairs={{0,8},{4,12},{8,0},{12,4},{1,9},{5,13},{9,1},{13,5},{2,10},{6,14},... | collective-permute-start | bytes 1179656 | tf_op jit(solution)/shard_map/ppermute | solution.py:46
  30.4 16.6 %collective-permute-start.7 = (bf16[256,768]{1,0:T(8,128)(2,1)S(1)}, bf16[256,768]{1,0:T(8,128)(2,1)S(1)}, u32[]{:S(2)}, u32[]{:S(2)}) collective-permute-start(bf16[256,768]{1,0:T(8,128)(2,1)S(1)} %get-tuple-element.163.refs_0_.refs_4_), channel_id=1, source_target_pairs={{0,2},{1,3},{2,0},{3,1},{4,6},{5,7},{6,4},{7,5},{8,10},{9,11},{10,... | collective-permute-start | bytes 1179656 | tf_op jit(solution)/shard_map/ppermute | solution.py:46
  47.1 4.3 collective-permute-start.12
  49.0 13.3 %collective-permute-start.15 = (bf16[256,768]{1,0:T(8,128)(2,1)S(1)}, bf16[256,768]{1,0:T(8,128)(2,1)S(1)}, u32[]{:S(2)}, u32[]{:S(2)}) collective-permute-start(bf16[256,768]{1,0:T(8,128)(2,1)S(1)} %collective-permute-done.9.refs_2_), channel_id=1, source_target_pairs={{0,1},{1,0},{2,3},{3,2},{4,5},{5,4},{6,7},{7,6},{8,9},{9,8},{10,11... | collective-permute-start | bytes 1179656 | tf_op jit(solution)/shard_map/ppermute | solution.py:46
  49.0 13.3 %collective-permute-start.14 = (bf16[256,768]{1,0:T(8,128)(2,1)S(1)}, bf16[256,768]{1,0:T(8,128)(2,1)S(1)}, u32[]{:S(2)}, u32[]{:S(2)}) collective-permute-start(bf16[256,768]{1,0:T(8,128)(2,1)S(1)} %collective-permute-done.8.refs_4_), channel_id=1, source_target_pairs={{0,1},{1,0},{2,3},{3,2},{4,5},{5,4},{6,7},{7,6},{8,9},{9,8},{10,11... | collective-permute-start | bytes 1179656 | tf_op jit(solution)/shard_map/ppermute | solution.py:46
  49.5 13.0 %collective-permute-start.13 = (bf16[256,768]{1,0:T(8,128)(2,1)S(1)}, bf16[256,768]{1,0:T(8,128)(2,1)S(1)}, u32[]{:S(2)}, u32[]{:S(2)}) collective-permute-start(bf16[256,768]{1,0:T(8,128)(2,1)S(1)} %collective-permute-done.8.refs_4_), channel_id=1, source_target_pairs={{8,12},{4,0},{9,13},{5,1},{10,14},{6,2},{11,15},{7,3},{24,28},{20,... | collective-permute-start | bytes 1179656 | tf_op jit(solution)/shard_map/ppermute | solution.py:1146
  50.8 13.3 %collective-permute-start.10 = (bf16[384,640]{1,0:T(8,128)(2,1)S(1)}, bf16[384,640]{1,0:T(8,128)(2,1)S(1)}, u32[]{:S(2)}, u32[]{:S(2)}) collective-permute-start(bf16[384,640]{1,0:T(8,128)(2,1)S(1)} %collective-permute-done.5.refs_1_), channel_id=1, source_target_pairs={{0,16},{16,0},{1,17},{17,1},{2,18},{18,2},{3,19},{19,3},{4,20},{20... | collective-permute-start | bytes 1474568 | tf_op jit(solution)/shard_map/ppermute | solution.py:46
  51.4 10.9 %collective-permute-start.11 = (bf16[256,768]{1,0:T(8,128)(2,1)S(1)}, bf16[256,768]{1,0:T(8,128)(2,1)}, u32[]{:S(2)}, u32[]{:S(2)}) collective-permute-start(bf16[256,768]{1,0:T(8,128)(2,1)S(1)} %get-tuple-element.186.refs_0_.refs_5_), channel_id=1, source_target_pairs={{0,2},{1,3},{2,0},{3,1},{4,6},{5,7},{6,4},{7,5},{8,10},{9,11},{10,... | collective-permute-start | bytes 1179656 | tf_op jit(solution)/shard_map/ppermute | solution.py:46
  62.3 12.8 %collective-permute-start.17 = (bf16[256,768]{1,0:T(8,128)(2,1)S(1)}, bf16[256,768]{1,0:T(8,128)(2,1)S(1)}, u32[]{:S(2)}, u32[]{:S(2)}) collective-permute-start(bf16[256,768]{1,0:T(8,128)(2,1)S(1)} %collective-permute-done.7.refs_8_), channel_id=1, source_target_pairs={{0,1},{1,0},{2,3},{3,2},{4,5},{5,4},{6,7},{7,6},{8,9},{9,8},{10,11... | collective-permute-start | bytes 1179656 | tf_op jit(solution)/shard_map/ppermute | solution.py:46
  64.1 13.1 %collective-permute-start.16 = (bf16[256,768]{1,0:T(8,128)(2,1)S(1)}, bf16[256,768]{1,0:T(8,128)(2,1)S(1)}, u32[]{:S(2)}, u32[]{:S(2)}) collective-permute-start(bf16[256,768]{1,0:T(8,128)(2,1)S(1)} %broadcast_select_fusion.1.refs_6_), channel_id=1, source_target_pairs={{0,1},{1,0},{2,3},{3,2},{4,5},{5,4},{6,7},{7,6},{8,9},{9,8},{10,11... | collective-permute-start | bytes 1179656 | tf_op jit(solution)/shard_map/ppermute | solution.py:46
  65.8 29.5 %collective-permute-start.20 = (bf16[96,1792]{1,0:T(8,128)(2,1)S(1)}, bf16[96,1792]{1,0:T(8,128)(2,1)S(1)}, u32[]{:S(2)}, u32[]{:S(2)}) collective-permute-start(bf16[96,1792]{1,0:T(8,128)(2,1)S(1)} %copy-done.8), channel_id=1, source_target_pairs={{0,12},{4,8},{8,4},{12,0},{1,13},{5,9},{9,5},{13,1},{2,14},{6,10},... | collective-permute-start | bytes 1032200 | tf_op jit(solution)/shard_map/ppermute | solution.py:46
  68.2 32.2 %collective-permute-start.19 = (bf16[96,1792]{1,0:T(8,128)(2,1)S(1)}, bf16[96,1792]{1,0:T(8,128)(2,1)S(1)}, u32[]{:S(2)}, u32[]{:S(2)}) collective-permute-start(bf16[96,1792]{1,0:T(8,128)(2,1)S(1)} %copy-done.8), channel_id=1, source_target_pairs={{0,8},{4,12},{8,0},{12,4},{1,9},{5,13},{9,1},{13,5},{2,10},{6,14},... | collective-permute-start | bytes 1032200 | tf_op jit(solution)/shard_map/ppermute | solution.py:46
  71.3 29.1 %collective-permute-start.18 = (bf16[96,1792]{1,0:T(8,128)(2,1)S(1)}, bf16[96,1792]{1,0:T(8,128)(2,1)S(1)}, u32[]{:S(2)}, u32[]{:S(2)}) collective-permute-start(bf16[96,1792]{1,0:T(8,128)(2,1)S(1)} %copy-done.8), channel_id=1, source_target_pairs={{0,4},{4,0},{8,12},{12,8},{1,5},{5,1},{9,13},{13,9},{2,6},{6,2},{1... | collective-permute-start | bytes 1032200 | tf_op jit(solution)/shard_map/ppermute | solution.py:46
  75.1 27.4 %collective-permute-start.22 = (bf16[256,768]{1,0:T(8,128)(2,1)S(1)}, bf16[256,768]{1,0:T(8,128)(2,1)S(1)}, u32[]{:S(2)}, u32[]{:S(2)}) collective-permute-start(bf16[256,768]{1,0:T(8,128)(2,1)S(1)} %get-tuple-element.186.refs_0_.refs_5_), channel_id=1, source_target_pairs={{0,4},{4,0},{8,12},{12,8},{1,5},{5,1},{9,13},{13,9},{2,6},{6,2},{1... | collective-permute-start | bytes 1179656 | tf_op jit(solution)/shard_map/ppermute | solution.py:46
  77.2 39.9 %collective-permute-start.21 = (bf16[256,768]{1,0:T(8,128)(2,1)S(1)}, bf16[256,768]{1,0:T(8,128)(2,1)S(1)}, u32[]{:S(2)}, u32[]{:S(2)}) collective-permute-start(bf16[256,768]{1,0:T(8,128)(2,1)S(1)} %get-tuple-element.186.refs_0_.refs_5_), channel_id=1, source_target_pairs={{0,8},{4,12},{8,0},{12,4},{1,9},{5,13},{9,1},{13,5},{2,10},{6,14},... | collective-permute-start | bytes 1179656 | tf_op jit(solution)/shard_map/ppermute | solution.py:46
  119.8 32.3 %collective-permute-start.24 = (bf16[384,1792]{1,0:T(8,128)(2,1)}, bf16[384,1792]{1,0:T(8,128)(2,1)S(1)}, u32[]{:S(2)}, u32[]{:S(2)}) collective-permute-start(bf16[384,1792]{1,0:T(8,128)(2,1)} %stack.88.refs_0_), channel_id=1, source_target_pairs={{0,16},{16,0},{1,17},{17,1},{2,18},{18,2},{3,19},{19,3},{4,20},{20... | collective-permute-start | bytes 4128776 | tf_op jit(solution)/shard_map/ppermute | solution.py:46
  120.3 32.1 %collective-permute-start.23 = (bf16[384,1792]{1,0:T(8,128)(2,1)}, bf16[384,1792]{1,0:T(8,128)(2,1)S(1)}, u32[]{:S(2)}, u32[]{:S(2)}) collective-permute-start(bf16[384,1792]{1,0:T(8,128)(2,1)} %stack.88.refs_0_), channel_id=1, source_target_pairs={{0,2},{1,3},{2,0},{3,1},{4,6},{5,7},{6,4},{7,5},{8,10},{9,11},{10,... | collective-permute-start | bytes 4128776 | tf_op jit(solution)/shard_map/ppermute | solution.py:46
  122.1 19.8 %collective-permute-start.26 = (bf16[256,768]{1,0:T(8,128)(2,1)S(1)}, bf16[256,768]{1,0:T(8,128)(2,1)S(1)}, u32[]{:S(2)}, u32[]{:S(2)}) collective-permute-start(bf16[256,768]{1,0:T(8,128)(2,1)S(1)} %collective-permute-done.21.refs_4_), channel_id=1, source_target_pairs={{8,12},{4,0},{9,13},{5,1},{10,14},{6,2},{11,15},{7,3},{24,28},{20,... | collective-permute-start | bytes 1179656 | tf_op jit(solution)/shard_map/ppermute | solution.py:1146
  123.8 30.7 %collective-permute-start.30 = (bf16[256,768]{1,0:T(8,128)(2,1)}, bf16[256,768]{1,0:T(8,128)(2,1)S(1)}, u32[]{:S(2)}, u32[]{:S(2)}) collective-permute-start(bf16[256,768]{1,0:T(8,128)(2,1)} %collective-permute-done.11.refs_8_), channel_id=1, source_target_pairs={{0,1},{1,0},{2,3},{3,2},{4,5},{5,4},{6,7},{7,6},{8,9},{9,8},{10,11... | collective-permute-start | bytes 1179656 | tf_op jit(solution)/shard_map/ppermute | solution.py:46
  152.5 32.6 %collective-permute-start.33 = (bf16[384,1792]{1,0:T(8,128)(2,1)S(1)}, bf16[384,1792]{1,0:T(8,128)(2,1)S(1)}, u32[]{:S(2)}, u32[]{:S(2)}) collective-permute-start(bf16[384,1792]{1,0:T(8,128)(2,1)S(1)} %collective-permute-done.23.refs_1_), channel_id=1, source_target_pairs={{0,16},{16,0},{1,17},{17,1},{2,18},{18,2},{3,19},{19,3},{4,20},{20... | collective-permute-start | bytes 4128776 | tf_op jit(solution)/shard_map/ppermute | solution.py:46
  154.1 39.0 %collective-permute-start.31 = (bf16[432,512]{1,0:T(8,128)(2,1)S(1)}, bf16[432,512]{1,0:T(8,128)(2,1)S(1)}, u32[]{:S(2)}, u32[]{:S(2)}) collective-permute-start(bf16[432,512]{1,0:T(8,128)(2,1)S(1)} %copy-done.48), channel_id=1, source_target_pairs={{0,2},{1,3},{2,0},{3,1},{4,6},{5,7},{6,4},{7,5},{8,10},{9,11},{10,... | collective-permute-start | bytes 1327112 | tf_op jit(solution)/shard_map/ppermute | solution.py:46
  178.3 14.8 %collective-permute-start.32 = (bf16[432,512]{1,0:T(8,128)(2,1)}, bf16[432,512]{1,0:T(8,128)(2,1)S(1)}, u32[]{:S(2)}, u32[]{:S(2)}) collective-permute-start(bf16[432,512]{1,0:T(8,128)(2,1)} %get-tuple-element.200), channel_id=1, source_target_pairs={{0,2},{1,3},{2,0},{3,1},{4,6},{5,7},{6,4},{7,5},{8,10},{9,11},{10,... | collective-permute-start | bytes 1327112 | tf_op jit(solution)/shard_map/ppermute | solution.py:46
  234.8 2.5 collective-permute-start.37
  257.8 2.6 collective-permute-start.38
  266.3 2.5 collective-permute-start.39
  276.7 12.4 %collective-permute-start.40 = (bf16[432,512]{1,0:T(8,128)(2,1)}, bf16[432,512]{1,0:T(8,128)(2,1)S(1)}, u32[]{:S(2)}, u32[]{:S(2)}) collective-permute-start(bf16[432,512]{1,0:T(8,128)(2,1)} %get-tuple-element.225.g_own), channel_id=1, source_target_pairs={{0,2},{1,3},{2,0},{3,1},{4,6},{5,7},{6,4},{7,5},{8,10},{9,11},{10,... | collective-permute-start | bytes 1327112 | tf_op jit(solution)/shard_map/ppermute | solution.py:46
  277.3 68.5 %collective-permute-start.42 = (bf16[384,3072]{1,0:T(8,128)(2,1)S(1)}, bf16[384,3072]{1,0:T(8,128)(2,1)S(1)}, u32[]{:S(2)}, u32[]{:S(2)}) collective-permute-start(bf16[384,3072]{1,0:T(8,128)(2,1)S(1)} %copy-done.45), channel_id=1, source_target_pairs={{0,16},{16,0},{1,17},{17,1},{2,18},{18,2},{3,19},{19,3},{4,20},{20... | collective-permute-start | bytes 7077896 | tf_op jit(solution)/shard_map/ppermute | solution.py:46
  316.9 36.8 %collective-permute-start.43 = (bf16[1024,768]{1,0:T(8,128)(2,1)}, bf16[1024,768]{1,0:T(8,128)(2,1)}, u32[]{:S(2)}, u32[]{:S(2)}) collective-permute-start(bf16[1024,768]{1,0:T(8,128)(2,1)} %get-tuple-element.234), channel_id=1, source_target_pairs={{0,1},{1,0},{2,3},{3,2},{4,5},{5,4},{6,7},{7,6},{8,9},{9,8},{10,11... | collective-permute-start | bytes 4718600 | tf_op jit(solution)/shard_map/ppermute | solution.py:46
  317.0 3.0 collective-permute-start.54
  320.1 104.2 %collective-permute-start.59 = (bf16[384,384]{1,0:T(8,128)(2,1)}, bf16[384,384]{1,0:T(8,128)(2,1)}, u32[]{:S(2)}, u32[]{:S(2)}) collective-permute-start(bf16[384,384]{1,0:T(8,128)(2,1)} %get-tuple-element.270), channel_id=1, source_target_pairs={{0,16},{16,0},{1,17},{17,1},{2,18},{18,2},{3,19},{19,3},{4,20},{20... | collective-permute-start | bytes 884744 | tf_op jit(solution)/shard_map/ppermute | solution.py:46
  345.3 13.3 %collective-permute-start.41 = (bf16[432,512]{1,0:T(8,128)(2,1)}, bf16[432,512]{1,0:T(8,128)(2,1)}, u32[]{:S(2)}, u32[]{:S(2)}) collective-permute-start(bf16[432,512]{1,0:T(8,128)(2,1)} %get-tuple-element.227.g_own), channel_id=1, source_target_pairs={{0,2},{1,3},{2,0},{3,1},{4,6},{5,7},{6,4},{7,5},{8,10},{9,11},{10,... | collective-permute-start | bytes 1327112 | tf_op jit(solution)/shard_map/ppermute | solution.py:46
  352.2 31.0 %collective-permute-start.46 = (bf16[384,1536]{1,0:T(8,128)(2,1)}, bf16[384,1536]{1,0:T(8,128)(2,1)S(1)}, u32[]{:S(2)}, u32[]{:S(2)}) collective-permute-start(bf16[384,1536]{1,0:T(8,128)(2,1)} %get-tuple-element.232), channel_id=1, source_target_pairs={{0,2},{1,3},{2,0},{3,1},{4,6},{5,7},{6,4},{7,5},{8,10},{9,11},{10,... | collective-permute-start | bytes 3538952 | tf_op jit(solution)/shard_map/ppermute | solution.py:46
  355.6 27.8 %collective-permute-start.49 = (bf16[256,768]{1,0:T(8,128)(2,1)S(1)}, bf16[256,768]{1,0:T(8,128)(2,1)S(1)}, u32[]{:S(2)}, u32[]{:S(2)}) collective-permute-start(bf16[256,768]{1,0:T(8,128)(2,1)S(1)} %get-tuple-element.339), channel_id=1, source_target_pairs={{0,12},{4,8},{8,4},{12,0},{1,13},{5,9},{9,5},{13,1},{2,14},{6,10},... | collective-permute-start | bytes 1179656 | tf_op jit(solution)/shard_map/ppermute | solution.py:46
  358.0 32.5 %collective-permute-start.48 = (bf16[256,768]{1,0:T(8,128)(2,1)S(1)}, bf16[256,768]{1,0:T(8,128)(2,1)S(1)}, u32[]{:S(2)}, u32[]{:S(2)}) collective-permute-start(bf16[256,768]{1,0:T(8,128)(2,1)S(1)} %get-tuple-element.340), channel_id=1, source_target_pairs={{0,8},{4,12},{8,0},{12,4},{1,9},{5,13},{9,1},{13,5},{2,10},{6,14},... | collective-permute-start | bytes 1179656 | tf_op jit(solution)/shard_map/ppermute | solution.py:46
  358.6 31.9 %collective-permute-start.47 = (bf16[256,768]{1,0:T(8,128)(2,1)S(1)}, bf16[256,768]{1,0:T(8,128)(2,1)S(1)}, u32[]{:S(2)}, u32[]{:S(2)}) collective-permute-start(bf16[256,768]{1,0:T(8,128)(2,1)S(1)} %get-tuple-element.341), channel_id=1, source_target_pairs={{0,4},{4,0},{8,12},{12,8},{1,5},{5,1},{9,13},{13,9},{2,6},{6,2},{1... | collective-permute-start | bytes 1179656 | tf_op jit(solution)/shard_map/ppermute | solution.py:46
  383.2 28.2 %collective-permute-start.44 = (bf16[384,512]{1,0:T(8,128)(2,1)S(1)}, bf16[384,512]{1,0:T(8,128)(2,1)S(1)}, u32[]{:S(2)}, u32[]{:S(2)}) collective-permute-start(bf16[384,512]{1,0:T(8,128)(2,1)S(1)} %copy-done.60), channel_id=1, source_target_pairs={{0,2},{1,3},{2,0},{3,1},{4,6},{5,7},{6,4},{7,5},{8,10},{9,11},{10,... | collective-permute-start | bytes 1179656 | tf_op jit(solution)/shard_map/ppermute | solution.py:46
  383.4 28.0 %collective-permute-start.45 = (bf16[384,512]{1,0:T(8,128)(2,1)}, bf16[384,512]{1,0:T(8,128)(2,1)S(1)}, u32[]{:S(2)}, u32[]{:S(2)}) collective-permute-start(bf16[384,512]{1,0:T(8,128)(2,1)} %get-tuple-element.238), channel_id=1, source_target_pairs={{0,2},{1,3},{2,0},{3,1},{4,6},{5,7},{6,4},{7,5},{8,10},{9,11},{10,... | collective-permute-start | bytes 1179656 | tf_op jit(solution)/shard_map/ppermute | solution.py:46
  408.5 39.1 %collective-permute-start.53 = (bf16[384,768]{1,0:T(8,128)(2,1)}, bf16[384,768]{1,0:T(8,128)(2,1)}, u32[]{:S(2)}, u32[]{:S(2)}) collective-permute-start(bf16[384,768]{1,0:T(8,128)(2,1)} %get-tuple-element.251), channel_id=1, source_target_pairs={{0,16},{16,0},{1,17},{17,1},{2,18},{18,2},{3,19},{19,3},{4,20},{20... | collective-permute-start | bytes 1769480 | tf_op jit(solution)/shard_map/ppermute | solution.py:46
  421.7 5.0 collective-permute-start.55
  421.7 8.6 %collective-permute-start.52 = (bf16[384,384]{1,0:T(8,128)(2,1)}, bf16[384,384]{1,0:T(8,128)(2,1)S(1)}, u32[]{:S(2)}, u32[]{:S(2)}) collective-permute-start(bf16[384,384]{1,0:T(8,128)(2,1)} %get-tuple-element.261), channel_id=1, source_target_pairs={{0,16},{16,0},{1,17},{17,1},{2,18},{18,2},{3,19},{19,3},{4,20},{20... | collective-permute-start | bytes 884744 | tf_op jit(solution)/shard_map/ppermute | solution.py:46
  423.8 12.3 %collective-permute-start.56 = (bf16[96,1536]{1,0:T(8,128)(2,1)}, bf16[96,1536]{1,0:T(8,128)(2,1)S(1)}, u32[]{:S(2)}, u32[]{:S(2)}) collective-permute-start(bf16[96,1536]{1,0:T(8,128)(2,1)} %get-tuple-element.244), channel_id=1, source_target_pairs={{0,4},{4,0},{8,12},{12,8},{1,5},{5,1},{9,13},{13,9},{2,6},{6,2},{1... | collective-permute-start | bytes 884744 | tf_op jit(solution)/shard_map/ppermute | solution.py:46
  424.3 23.3 %collective-permute-start.57 = (bf16[96,1536]{1,0:T(8,128)(2,1)}, bf16[96,1536]{1,0:T(8,128)(2,1)S(1)}, u32[]{:S(2)}, u32[]{:S(2)}) collective-permute-start(bf16[96,1536]{1,0:T(8,128)(2,1)} %get-tuple-element.245), channel_id=1, source_target_pairs={{0,8},{4,12},{8,0},{12,4},{1,9},{5,13},{9,1},{13,5},{2,10},{6,14},... | collective-permute-start | bytes 884744 | tf_op jit(solution)/shard_map/ppermute | solution.py:46
  426.7 21.0 %collective-permute-start.58 = (bf16[96,1536]{1,0:T(8,128)(2,1)}, bf16[96,1536]{1,0:T(8,128)(2,1)S(1)}, u32[]{:S(2)}, u32[]{:S(2)}) collective-permute-start(bf16[96,1536]{1,0:T(8,128)(2,1)} %get-tuple-element.246), channel_id=1, source_target_pairs={{0,12},{4,8},{8,4},{12,0},{1,13},{5,9},{9,5},{13,1},{2,14},{6,10},... | collective-permute-start | bytes 884744 | tf_op jit(solution)/shard_map/ppermute | solution.py:46
  430.4 42.5 %collective-permute-start.50 = (bf16[512,768]{1,0:T(8,128)(2,1)}, bf16[512,768]{1,0:T(8,128)(2,1)}, u32[]{:S(2)}, u32[]{:S(2)}) collective-permute-start(bf16[512,768]{1,0:T(8,128)(2,1)} %get-tuple-element.254), channel_id=1, source_target_pairs={{0,1},{1,0},{2,3},{3,2},{4,5},{5,4},{6,7},{7,6},{8,9},{9,8},{10,11... | collective-permute-start | bytes 2359304 | tf_op jit(solution)/shard_map/ppermute | solution.py:46
  436.1 28.9 %collective-permute-start.51 = (bf16[1024,768]{1,0:T(8,128)(2,1)}, bf16[1024,768]{1,0:T(8,128)(2,1)}, u32[]{:S(2)}, u32[]{:S(2)}) collective-permute-start(bf16[1024,768]{1,0:T(8,128)(2,1)} %get-tuple-element.259), channel_id=1, source_target_pairs={{0,1},{1,0},{2,3},{3,2},{4,5},{5,4},{6,7},{7,6},{8,9},{9,8},{10,11... | collective-permute-start | bytes 4718600 | tf_op jit(solution)/shard_map/ppermute | solution.py:46
  447.6 6.6 %collective-permute-start.69 = (f32[1,6912]{1,0:T(1,128)S(1)}, f32[1,6912]{1,0:T(1,128)S(1)}, u32[]{:S(2)}, u32[]{:S(2)}) collective-permute-start(f32[1,6912]{1,0:T(1,128)S(1)} %add.114), channel_id=1, source_target_pairs={{0,12},{4,8},{8,4},{12,0},{1,13},{5,9},{9,5},{13,1},{2,14},{6,10},... | collective-permute-start | bytes 82952 | tf_op jit(solution)/shard_map/ppermute | solution.py:46
  449.6 5.7 %collective-permute-start.68 = (f32[1,6912]{1,0:T(1,128)S(1)}, f32[1,6912]{1,0:T(1,128)S(1)}, u32[]{:S(2)}, u32[]{:S(2)}) collective-permute-start(f32[1,6912]{1,0:T(1,128)S(1)} %add.114), channel_id=1, source_target_pairs={{0,8},{4,12},{8,0},{12,4},{1,9},{5,13},{9,1},{13,5},{2,10},{6,14},... | collective-permute-start | bytes 82952 | tf_op jit(solution)/shard_map/ppermute | solution.py:46
  453.1 3.9 collective-permute-start.67
  457.0 7.3 %collective-permute-start.70 = (f32[1,6912]{1,0:T(1,128)S(1)}, f32[1,6912]{1,0:T(1,128)S(1)}, u32[]{:S(2)}, u32[]{:S(2)}) collective-permute-start(f32[1,6912]{1,0:T(1,128)S(1)} %add_add_fusion.2), channel_id=1, source_target_pairs={{0,2},{1,3},{2,0},{3,1},{4,6},{5,7},{6,4},{7,5},{8,10},{9,11},{10,... | collective-permute-start | bytes 82952 | tf_op jit(solution)/shard_map/ppermute | solution.py:46
  462.7 11.6 %collective-permute-start.60 = (bf16[384,768]{1,0:T(8,128)(2,1)}, bf16[384,768]{1,0:T(8,128)(2,1)}, u32[]{:S(2)}, u32[]{:S(2)}) collective-permute-start(bf16[384,768]{1,0:T(8,128)(2,1)} %get-tuple-element.272), channel_id=1, source_target_pairs={{0,2},{1,3},{2,0},{3,1},{4,6},{5,7},{6,4},{7,5},{8,10},{9,11},{10,... | collective-permute-start | bytes 1769480 | tf_op jit(solution)/shard_map/ppermute | solution.py:46
  467.8 13.1 %collective-permute-start.61 = (bf16[256,768]{1,0:T(8,128)(2,1)S(1)}, bf16[256,768]{1,0:T(8,128)(2,1)}, u32[]{:S(2)}, u32[]{:S(2)}) collective-permute-start(bf16[256,768]{1,0:T(8,128)(2,1)S(1)} %get-tuple-element.274), channel_id=1, source_target_pairs={{0,4},{4,0},{8,12},{12,8},{1,5},{5,1},{9,13},{13,9},{2,6},{6,2},{1... | collective-permute-start | bytes 1179656 | tf_op jit(solution)/shard_map/ppermute | solution.py:46
  468.5 28.3 %collective-permute-start.62 = (bf16[256,768]{1,0:T(8,128)(2,1)S(1)}, bf16[256,768]{1,0:T(8,128)(2,1)}, u32[]{:S(2)}, u32[]{:S(2)}) collective-permute-start(bf16[256,768]{1,0:T(8,128)(2,1)S(1)} %get-tuple-element.275), channel_id=1, source_target_pairs={{0,8},{4,12},{8,0},{12,4},{1,9},{5,13},{9,1},{13,5},{2,10},{6,14},... | collective-permute-start | bytes 1179656 | tf_op jit(solution)/shard_map/ppermute | solution.py:46
  470.5 26.3 %collective-permute-start.63 = (bf16[256,768]{1,0:T(8,128)(2,1)S(1)}, bf16[256,768]{1,0:T(8,128)(2,1)}, u32[]{:S(2)}, u32[]{:S(2)}) collective-permute-start(bf16[256,768]{1,0:T(8,128)(2,1)S(1)} %get-tuple-element.276), channel_id=1, source_target_pairs={{0,12},{4,8},{8,4},{12,0},{1,13},{5,9},{9,5},{13,1},{2,14},{6,10},... | collective-permute-start | bytes 1179656 | tf_op jit(solution)/shard_map/ppermute | solution.py:46
  499.2 11.0 %collective-permute-start.64 = (bf16[96,768]{1,0:T(8,128)(2,1)}, bf16[96,768]{1,0:T(8,128)(2,1)S(1)}, u32[]{:S(2)}, u32[]{:S(2)}) collective-permute-start(bf16[96,768]{1,0:T(8,128)(2,1)} %get-tuple-element.283), channel_id=1, source_target_pairs={{0,4},{4,0},{8,12},{12,8},{1,5},{5,1},{9,13},{13,9},{2,6},{6,2},{1... | collective-permute-start | bytes 442376 | tf_op jit(solution)/shard_map/ppermute | solution.py:46
  504.1 10.6 %collective-permute-start.65 = (bf16[96,768]{1,0:T(8,128)(2,1)}, bf16[96,768]{1,0:T(8,128)(2,1)S(1)}, u32[]{:S(2)}, u32[]{:S(2)}) collective-permute-start(bf16[96,768]{1,0:T(8,128)(2,1)} %get-tuple-element.284), channel_id=1, source_target_pairs={{0,8},{4,12},{8,0},{12,4},{1,9},{5,13},{9,1},{13,5},{2,10},{6,14},... | collective-permute-start | bytes 442376 | tf_op jit(solution)/shard_map/ppermute | solution.py:46
  504.6 10.2 %collective-permute-start.66 = (bf16[96,768]{1,0:T(8,128)(2,1)}, bf16[96,768]{1,0:T(8,128)(2,1)S(1)}, u32[]{:S(2)}, u32[]{:S(2)}) collective-permute-start(bf16[96,768]{1,0:T(8,128)(2,1)} %get-tuple-element.285), channel_id=1, source_target_pairs={{0,12},{4,8},{8,4},{12,0},{1,13},{5,9},{9,5},{13,1},{2,14},{6,10},... | collective-permute-start | bytes 442376 | tf_op jit(solution)/shard_map/ppermute | solution.py:46
  (73 other events, 951.9 us)
where the time goes:
time: 524 us; the launch traced here: 516 us
  Pallas kernels  207 us (40%)
  waiting for transfers between devices  170 us (32%)
  starting transfers between devices  96.9 us (18%)
  local copies, waits for them, and re-layouts  23.3 us (4%)
  other arithmetic  17.4 us (3%)
    ppermute x67, waiting for transfers between devices, swap(): lax.ppermute(after(value, *start), axis, [(i, i ^ bit) for i in range(cou...  152 us
    ppermute x67, starting transfers between devices, swap(): lax.ppermute(after(value, *start), axis, [(i, i ^ bit) for i in range(cou...  92.5 us
    pallas_call x2, Pallas kernels, attend_back(): pl.pallas_call(functools.partial(attend_back_kernel, slots), grid_spec=pl...  36 us
    pallas_call x9, Pallas kernels, call(): pl.pallas_call(kernel, grid_spec=pltpu.PrefetchScalarGridSpec(num_scalar_...  31.2 us
    pallas_call x2, Pallas kernels, kv_back(): pl.pallas_call(functools.partial(kv_back_kernel, slots, steps, split, bef...  28.5 us
    pallas_call x2, Pallas kernels, attend(): pl.pallas_call(functools.partial(attend_kernel, slots, min(128, keys)), g...  21.8 us
    pallas_call x1, Pallas kernels, feed_back(): pl.pallas_call(functools.partial(feed_back_kernel, half, lines), grid_spe...  19.5 us
    ppermute x2, waiting for transfers between devices, send_last(): lax.ppermute(far, 'ctx', [(2, 3), (1, 0)])  18 us
  transfers between devices with their start and end apart: 71, of which 32 were waited for; matrix products, arithmetic and copies ran while one was open for 5% of the time, Pallas kernels for 27%

commit v1 on v0

--- a/solution.py
+++ b/solution.py
@@ -85,33 +85,43 @@
     return rows % 16 == 0
 
 
-def pack(pieces, turned):
-    widths = [p.shape[0] if t else p.shape[1] for p, t in zip(pieces, turned)]
-    rows = pieces[0].shape[1] if turned[0] else pieces[0].shape[0]
+def pack(groups):
+    flat = [piece for group in groups for piece in group]
+    widths = [sum(w.shape[0] if t else w.shape[1] for w, t in group) for group in groups]
+    first, turned = flat[0]
+    rows = first.shape[1] if turned else first.shape[0]
+
+    def joined(values):
+        values, out = list(values), []
+        for group, width in zip(groups, widths):
+            out += [values.pop(0) for _ in group]
+            if -width % 128:
+                out.append(jnp.zeros((rows, -width % 128), F32))
+        return jnp.concatenate(out, axis=1).astype(BF)
+
     if not fits(rows):
-        return jnp.concatenate([p.T if t else p for p, t in zip(pieces, turned)], axis=1).astype(BF)
-
-    spare = -sum(widths) % 128
+        return joined(w.T if t else w for w, t in flat)
 
     def kernel(*refs):
-        whole = [r[...].T if t else r[...] for r, t in zip(refs, turned)]
-        if spare:
-            whole.append(jnp.zeros((rows, spare), F32))
-        refs[-1][...] = jnp.concatenate(whole, axis=1).astype(BF)
-
-    return call(kernel, "pack", [((rows, sum(widths) + spare), BF)], *pieces)[0]
-
-
-def stack(parts):
+        refs[-1][...] = joined(r[...].T if t else r[...] for r, (_, t) in zip(refs, flat))
+
+    total = sum(w + -w % 128 for w in widths)
+    return call(kernel, "pack", [((rows, total), BF)], *[w for w, _ in flat])[0]
+
+
+def stack(parts, cuts=None):
     rows, width = parts[0].shape
+    ranges = [(0, width)] if cuts is None else [(0, cuts), (cuts, width)]
     if not fits(rows):
-        return jnp.concatenate(parts, axis=0)
+        whole = jnp.concatenate(parts, axis=0)
+        return [whole[:, start:stop] for start, stop in ranges]
 
     def kernel(*refs):
-        for k, ref in enumerate(refs[:-1]):
-            refs[-1][k * rows : k * rows + rows, :] = ref[...]
-
-    return call(kernel, "stack", [((rows * len(parts), width), BF)], *parts)[0]
+        for k, ref in enumerate(refs[: len(parts)]):
+            for out, (start, stop) in zip(refs[len(parts) :], ranges):
+                out[k * rows : k * rows + rows, :] = ref[:, start:stop]
+
+    return call(kernel, "stack", [((rows * len(parts), stop - start), BF) for start, stop in ranges], *parts)
 
 
 def over_dp(arrays, done=()):
@@ -227,6 +237,27 @@
     return call(kernel, "fold_spots", outs, kept, came, prefetch=spot.astype(jnp.int32).reshape(1))
 
 
+def add_low(kept, came):
+    if not fits(kept.shape[0] // 4):
+        return (kept + came.astype(F32)).astype(BF)
+
+    def kernel(kept_ref, came_ref, out):
+        out[...] = (kept_ref[...] + came_ref[...].astype(F32)).astype(BF)
+
+    rows, width = kept.shape
+    spec = pl.BlockSpec((rows // 4, width), lambda i: (i, 0))
+    return pl.pallas_call(
+        kernel,
+        grid=(4,),
+        in_specs=[spec, spec],
+        out_specs=spec,
+        out_shape=jax.ShapeDtypeStruct(kept.shape, BF),
+        compiler_params=params(),
+        cost_estimate=cost(kept.size, 8 * kept.size),
+        name="add_low",
+    )(kept, came)
+
+
 def own_rows(where, value, rows):
     mine = pl.ds(pl.multiple_of(where * rows, rows), rows)
     other = pl.ds(pl.multiple_of((1 - where) * rows, rows), rows)
@@ -239,156 +270,6 @@
         mine, came = pieces[2 * k][...], pieces[2 * k + 1][...]
         held[2 * k * local : (2 * k + 1) * local, :] = jnp.where(upper, came, mine)
         held[(2 * k + 1) * local : (2 * k + 2) * local, :] = jnp.where(upper, mine, came)
-
-
-def project_kernel(slots, where, *refs):
-    pieces = refs[: 2 * slots + 2]
-    w_query, w_kv, b_query, b_kv, query_ref, kv_ref, held = refs[2 * slots + 2 :]
-    local = pieces[0].shape[0]
-
-    @pl.when(pl.program_id(0) == 0)
-    def _():
-        assemble(where[0] == 1, pieces, held)
-
-    rows = 2 * slots * local
-    kv_ref[...] = (dot(held[:rows, :], w_kv[...], NN) + b_kv[...]).astype(BF)
-    scale = jnp.asarray(1.0 / math.sqrt(HD), BF)
-    for start, to in ((0, 0), (rows, 2 * local)):
-        query = (dot(held[start : start + 2 * local, :], w_query[...], NN) + b_query[...]).astype(BF)
-        query_ref[to : to + 2 * local, :] = query * scale
-
-
-def project(where, pieces, w_query, w_kv, b_query, b_kv):
-    slots = len(pieces) - 1
-    local, width = pieces[0][0].shape
-    whole = lambda p, c: (0, 0)
-    across = lambda p, c: (0, p)
-    flat = [p for pair in pieces for p in pair]
-    q_width, kv_width = w_query.shape[1], w_kv.shape[1]
-    return pl.pallas_call(
-        functools.partial(project_kernel, slots),
-        grid_spec=pltpu.PrefetchScalarGridSpec(
-            num_scalar_prefetch=1,
-            grid=(q_width // PAIR,),
-            in_specs=[pl.BlockSpec(a.shape, whole, pipeline_mode=pl.Buffered(1)) for a in flat]
-            + [
-                pl.BlockSpec((width, PAIR), across),
-                pl.BlockSpec((width, 2 * PAIR), across),
-                pl.BlockSpec((1, PAIR), across),
-                pl.BlockSpec((1, 2 * PAIR), across),
-            ],
-            out_specs=[
-                pl.BlockSpec((4 * local, PAIR), across),
-                pl.BlockSpec((2 * slots * local, 2 * PAIR), across),
-            ],
-            scratch_shapes=[pltpu.VMEM(((2 * slots + 2) * local, width), BF)],
-        ),
-        out_shape=[
-            jax.ShapeDtypeStruct((4 * local, q_width), BF),
-            jax.ShapeDtypeStruct((2 * slots * local, kv_width), BF),
-        ],
-        compiler_params=params(),
-        cost_estimate=cost(4 * slots * local * width * (kv_width + q_width // 2), 2 * len(flat) * local * width + 4 * slots * local * kv_width),
-        name="project",
-    )(where, *flat, w_query, w_kv, b_query, b_kv)
-
-
-def kv_back_kernel(slots, steps, split, first, where, *refs):
-    pieces = refs[: 2 * slots]
-    at = 2 * slots
-    dkv, w_kv = refs[at : at + 2]
-    at += 2
-    if not first:
-        before, bias_before = refs[at : at + 2]
-        at += 2
-    mine_ref, other_ref, bias_ref = refs[at : at + 3]
-    weight_refs = refs[at + 3 : -2]
-    turned, part = refs[-2:]
-    local = pieces[0].shape[0]
-    step = pl.program_id(0)
-    upper = where[0] == 1
-
-    @pl.when(step == 0)
-    def _():
-        for k in range(slots):
-            mine, came = pieces[2 * k][...], pieces[2 * k + 1][...]
-            turned[:, 2 * k * local : (2 * k + 1) * local] = jnp.where(upper, came, mine).T
-            turned[:, (2 * k + 1) * local : (2 * k + 2) * local] = jnp.where(upper, mine, came).T
-
-    grads = dkv[...]
-    total = dot(turned[...], grads, NN)
-    bias = jnp.sum(grads.astype(F32), axis=0, keepdims=True)
-    if not first:
-        total, bias = total + before[...], bias + bias_before[...]
-    bias_ref[...] = bias
-    half = total.shape[0] // 2
-    if split:
-        lower_line = where[1] == 0
-        weight_refs[0][...] = jnp.where(lower_line, total[:half], total[half:])
-        weight_refs[1][...] = jnp.where(lower_line, total[half:], total[:half]).astype(BF)
-    else:
-        weight_refs[0][...] = total
-    term = dot(grads, w_kv[...], NT)
-
-    @pl.when(step == 0)
-    def _():
-        part[...] = term
-
-    @pl.when(jnp.logical_and(step > 0, step < steps - 1))
-    def _():
-        part[...] += term
-
-    @pl.when(step == steps - 1)
-    def _():
-        for k in range(slots):
-            low = slice(2 * k * local, (2 * k + 1) * local)
-            high = slice((2 * k + 1) * local, (2 * k + 2) * local)
-            to = slice(k * local, k * local + local)
-            low_part, high_part = part[low, :] + term[low], part[high, :] + term[high]
-            mine_ref[to, :] = jnp.where(upper, high_part, low_part)
-            other_ref[to, :] = jnp.where(upper, low_part, high_part).astype(BF)
-
-
-def kv_back(where, pieces, dkv, w_kv, before, last):
-    slots = len(pieces)
-    local, width = pieces[0][0].shape
-    kv_width = w_kv.shape[1]
-    split = last and lax.axis_size("dp") == 2
-    whole = lambda p, c: (0, 0)
-    across = lambda p, c: (0, p)
-    once = pl.Buffered(1)
-    flat = [p for pair in pieces for p in pair]
-    extra = () if before is None else before
-    if split:
-        weight_outs = [((width // 2, kv_width), F32), ((width // 2, kv_width), BF)]
-    else:
-        weight_outs = [((width, kv_width), F32)]
-    steps = kv_width // (2 * PAIR)
-    return pl.pallas_call(
-        functools.partial(kv_back_kernel, slots, steps, split, before is None),
-        grid_spec=pltpu.PrefetchScalarGridSpec(
-            num_scalar_prefetch=1,
-            grid=(steps,),
-            in_specs=[pl.BlockSpec((local, width), whole, pipeline_mode=once) for _ in flat]
-            + [pl.BlockSpec((a.shape[0], 2 * PAIR), across) for a in (dkv, w_kv, *extra)],
-            out_specs=[
-                pl.BlockSpec((slots * local, width), whole, pipeline_mode=once),
-                pl.BlockSpec((slots * local, width), whole, pipeline_mode=once),
-                pl.BlockSpec((1, 2 * PAIR), across),
-            ]
-            + [pl.BlockSpec((shape[0], 2 * PAIR), across) for shape, _ in weight_outs],
-            scratch_shapes=[pltpu.VMEM((width, 2 * slots * local), BF), pltpu.VMEM((2 * slots * local, width), F32)],
-        ),
-        out_shape=[
-            jax.ShapeDtypeStruct((slots * local, width), F32),
-            jax.ShapeDtypeStruct((slots * local, width), BF),
-            jax.ShapeDtypeStruct((1, kv_width), F32),
-        ]
-        + [jax.ShapeDtypeStruct(shape, kind) for shape, kind in weight_outs],
-        compiler_params=params(),
-        cost_estimate=cost(8 * slots * local * width * kv_width, 12 * slots * local * width + 4 * width * kv_width),
-        name="kv_back",
-    )(where, *flat, dkv, w_kv, *extra)
 
 
 def query_back_kernel(seqs, lines, where, *refs):
@@ -482,12 +363,35 @@
     return lax.broadcasted_iota(jnp.int32, shape, 0) < count
 
 
-def attend_kernel(slots, probe, counts, queries, kv, *refs):
-    o_own, packed, lse_ref, top, total, acc, heads = refs[-7:]
-    rows = queries.shape[0] // 2
-    keys = kv.shape[0] // slots
+def attend_kernel(slots, probe, old, counts, *refs):
+    pieces = refs[: 2 * slots + 2]
+    w_query, w_kv, b_query, b_kv = refs[2 * slots + 2 : 2 * slots + 6]
+    queries, kv, o_own, packed, lse_ref, held, top, total, acc, heads = refs[2 * slots + 6 + old :]
+    local = pieces[0].shape[0]
+    rows = keys = 2 * local
+
+    @pl.when(pl.program_id(0) == 0)
+    def _():
+        assemble(counts[slots + 1] == 1, pieces, held)
+
+    scale = jnp.asarray(1.0 / math.sqrt(HD), BF)
+    for start, to in ((0, 0), (slots * keys, rows)):
+        query = (dot(held[start : start + rows, :], w_query[...], NN) + b_query[...]).astype(BF)
+        queries[to : to + rows, :] = query * scale
     for h, query in enumerate(half_lanes(queries[...])):
         heads[h] = query
+
+    @pl.loop(0, slots)
+    def _(k):
+        at = pl.ds(pl.multiple_of(k * keys, keys), keys)
+
+        @pl.when(counts[k] > 0)
+        def _():
+            kv[at, :] = (dot(held[at, :], w_kv[...], NN) + b_kv[...]).astype(BF)
+
+        @pl.when(counts[k] <= 0)
+        def _():
+            kv[at, :] = jnp.zeros((keys, 2 * PAIR), BF)
 
     def block(k):
         at = pl.ds(pl.multiple_of(k * keys, keys), keys)
@@ -529,12 +433,12 @@
             key, value = block(k)
             scores = dot(key, heads[h], NT)
             scores = jnp.where(below(scores.shape, valid), scores, NEGATIVE)
-            old = top[h]
-            new = jnp.maximum(old, jnp.max(scores, axis=0, keepdims=True))
+            before = top[h]
+            new = jnp.maximum(before, jnp.max(scores, axis=0, keepdims=True))
             expo = jnp.where(below(scores.shape, valid), jnp.exp(scores - new), 0.0)
-            scale = jnp.exp(old - new)
-            total[h] = total[h] * scale + jnp.sum(expo, axis=0, keepdims=True)
-            acc[h] = acc[h] * scale + dot(value, expo.astype(BF), TN)
+            ratio = jnp.exp(before - new)
+            total[h] = total[h] * ratio + jnp.sum(expo, axis=0, keepdims=True)
+            acc[h] = acc[h] * ratio + dot(value, expo.astype(BF), TN)
             top[h] = new
 
         @pl.loop(0, slots)
@@ -556,28 +460,40 @@
     packed[PAIR:, :] = packed_rows(jnp.concatenate([l[:, rows:] for l in lse], axis=0))
 
 
-def attend(counts, slots, seqs, s, queries, kv, before):
-    rows, width = queries.shape[0] // 2, queries.shape[1]
+def attend(counts, seqs, s, pieces, weights, before):
+    w_query, w_kv, b_query, b_kv = weights
+    slots = len(pieces) - 1
+    local, model = pieces[0][0].shape
+    rows, width = 2 * local, w_query.shape[1]
     pairs = width // PAIR
-    keys = kv.shape[0] // slots
-    total = width * 2 * rows * kv.shape[0]
+    keys = 2 * local
+    total = width * 2 * rows * slots * keys
     anywhere = pl.BlockSpec(memory_space=pl.ANY)
+    across = lambda p, c: (0, p)
+    flat = [p for pair in pieces for p in pair]
+    held = ((slots + 1) * keys, model)
     return pl.pallas_call(
-        functools.partial(attend_kernel, slots, min(128, keys)),
+        functools.partial(attend_kernel, slots, min(128, keys), len(before)),
         grid_spec=pltpu.PrefetchScalarGridSpec(
             num_scalar_prefetch=1,
             grid=(pairs,),
-            in_specs=[
-                pl.BlockSpec((2 * rows, PAIR), lambda p, c: (0, p)),
-                pl.BlockSpec((kv.shape[0], 2 * PAIR), lambda p, c: (0, p)),
+            in_specs=[pl.BlockSpec((local, model), lambda p, c: (0, 0), pipeline_mode=pl.Buffered(1)) for _ in flat]
+            + [
+                pl.BlockSpec((model, PAIR), across),
+                pl.BlockSpec((model, 2 * PAIR), across),
+                pl.BlockSpec((1, PAIR), across),
+                pl.BlockSpec((1, 2 * PAIR), across),
             ]
             + [anywhere] * len(before),
             out_specs=[
+                pl.BlockSpec((2 * rows, PAIR), across),
+                pl.BlockSpec((slots * keys, 2 * PAIR), across),
                 pl.BlockSpec((1, PAIR, rows), lambda p, c: (s, p, 0)),
                 pl.BlockSpec((PAIR + 16, rows), lambda p, c: (p, 0)),
                 pl.BlockSpec((1, 1, 2, rows), lambda p, c: (s, p, 0, 0)),
             ],
             scratch_shapes=[
+                pltpu.VMEM(held, BF),
                 pltpu.VMEM((2, 1, 2 * rows), F32),
                 pltpu.VMEM((2, 1, 2 * rows), F32),
                 pltpu.VMEM((2, PAIR, 2 * rows), F32),
@@ -585,21 +501,45 @@
             ],
         ),
         out_shape=[
+            jax.ShapeDtypeStruct((2 * rows, width), BF),
+            jax.ShapeDtypeStruct((slots * keys, 2 * width), BF),
             jax.ShapeDtypeStruct((seqs, width, rows), F32),
             jax.ShapeDtypeStruct((pairs * (PAIR + 16), rows), BF),
             jax.ShapeDtypeStruct((seqs, pairs, 2, rows), F32),
         ],
-        input_output_aliases={3: 0, 4: 2} if before else {},
+        input_output_aliases={2 * slots + 7: 2, 2 * slots + 8: 4} if before else {},
         compiler_params=params(),
-        cost_estimate=cost(16 * total, 8 * queries.size + 2 * kv.size, total // HD),
+        cost_estimate=cost(16 * total, 2 * len(flat) * local * model + 8 * slots * keys * width, total // HD),
         name="attend",
-    )(counts, queries, kv, *before)
-
-
-def attend_back_kernel(slots, counts, both, g_own, g_oth, kv, dq_own, dq_oth, dkv, acc, queries, grads, summed, facts):
+    )(counts, *flat, *weights, *before)
+
+
+def attend_back_kernel(slots, steps, split, first, counts, both, g_own, g_oth, kv, w_kv, *refs):
+    pieces = refs[: 2 * slots]
+    refs = refs[2 * slots :]
+    if not first:
+        before, bias_before = refs[:2]
+        refs = refs[2:]
+    dq_own, dq_oth, mine_ref, other_ref, bias_ref = refs[:5]
+    weight_refs = refs[5:-8]
+    acc, queries, grads, summed, facts, turned, part, d_weight = refs[-8:]
     rows = both.shape[0] // 2
-    keys = kv.shape[0] // slots
+    local = pieces[0].shape[0]
+    keys = 2 * local
+    step = pl.program_id(0)
+    upper = counts[slots + 1] == 1
+
+    @pl.when(step == 0)
+    def _():
+        part[...] = jnp.zeros_like(part)
+        for k in range(slots):
+            mine, came = pieces[2 * k][...], pieces[2 * k + 1][...]
+            turned[:, 2 * k * local : (2 * k + 1) * local] = jnp.where(upper, came, mine).T
+            turned[:, (2 * k + 1) * local : (2 * k + 2) * local] = jnp.where(upper, mine, came).T
+
     acc[...] = jnp.zeros_like(acc)
+    d_weight[...] = jnp.zeros_like(d_weight) if first else before[...]
+    bias_ref[...] = jnp.zeros_like(bias_ref) if first else bias_before[...]
     for block, g_ref in enumerate((g_own, g_oth)):
         stats = unpacked_rows(g_ref[PAIR:, :], 4)
         for h, (query, grad) in enumerate(
@@ -638,48 +578,101 @@
         def _():
             pl.loop(0, 4)(lambda at: one(at, valid))
 
-        dkv[rows_at, :] = summed[...].astype(BF)
+        @pl.when(valid > 0)
+        def _():
+            low = summed[...].astype(BF)
+            part[rows_at, :] += dot(low, w_kv[...], NT)
+            d_weight[...] += dot(turned[:, rows_at], low, NN)
+            bias_ref[...] += jnp.sum(low.astype(F32), axis=0, keepdims=True)
 
     scale = 1.0 / math.sqrt(HD)
     for h in range(2):
         at = slice(h * HD, h * HD + HD)
         dq_own[at, :] = acc[h, at, :] * scale
         dq_oth[at, :] = (acc[2 + h, at, :] * scale).astype(BF)
-
-
-def attend_back(counts, slots, both, g_own, g_oth, kv):
+    half = d_weight.shape[0] // 2
+    if split:
+        lower_line = counts[slots + 2] == 0
+        low_half, high_half = d_weight[:half, :], d_weight[half:, :]
+        weight_refs[0][...] = jnp.where(lower_line, low_half, high_half)
+        weight_refs[1][...] = jnp.where(lower_line, high_half, low_half).astype(BF)
+    else:
+        weight_refs[0][...] = d_weight[...]
+
+    @pl.when(step == steps - 1)
+    def _():
+        for k in range(slots):
+            low = part[2 * k * local : (2 * k + 1) * local, :]
+            high = part[(2 * k + 1) * local : (2 * k + 2) * local, :]
+            to = slice(k * local, k * local + local)
+            mine_ref[to, :] = jnp.where(upper, high, low)
+            other_ref[to, :] = jnp.where(upper, low, high).astype(BF)
+
+
+def attend_back(counts, both, g_own, g_oth, kv, w_kv, pieces, before, last):
     rows, width = both.shape[0] // 2, both.shape[1]
     pairs = width // PAIR
-    keys = kv.shape[0] // slots
-    q_spec = pl.BlockSpec((2 * rows, PAIR), lambda p, c: (0, p))
+    slots = len(pieces)
+    local, model = pieces[0][0].shape
+    keys = 2 * local
+    split = last and lax.axis_size("dp") == 2
+    across = lambda p, c: (0, p)
+    whole = lambda p, c: (0, 0)
+    once = pl.Buffered(1)
     t_spec = pl.BlockSpec((PAIR, rows), lambda p, c: (p, 0))
     g_spec = pl.BlockSpec((PAIR + 16, rows), lambda p, c: (p, 0))
-    kv_spec = pl.BlockSpec((kv.shape[0], 2 * PAIR), lambda p, c: (0, p))
+    flat = [p for pair in pieces for p in pair]
+    extra = () if before is None else before
+    if split:
+        weight_outs = [((model // 2, 2 * width), F32), ((model // 2, 2 * width), BF)]
+    else:
+        weight_outs = [((model, 2 * width), F32)]
     total = width * 2 * rows * kv.shape[0]
     return pl.pallas_call(
-        functools.partial(attend_back_kernel, slots),
+        functools.partial(attend_back_kernel, slots, pairs, split, before is None),
         grid_spec=pltpu.PrefetchScalarGridSpec(
             num_scalar_prefetch=1,
             grid=(pairs,),
-            in_specs=[q_spec, g_spec, g_spec, kv_spec],
-            out_specs=[t_spec, t_spec, kv_spec],
+            in_specs=[
+                pl.BlockSpec((2 * rows, PAIR), across),
+                g_spec,
+                g_spec,
+                pl.BlockSpec((kv.shape[0], 2 * PAIR), across),
+                pl.BlockSpec((model, 2 * PAIR), across),
+            ]
+            + [pl.BlockSpec((local, model), whole, pipeline_mode=once) for _ in flat]
+            + [pl.BlockSpec((a.shape[0], 2 * PAIR), across) for a in extra],
+            out_specs=[
+                t_spec,
+                t_spec,
+                pl.BlockSpec((slots * local, model), whole, pipeline_mode=once),
+                pl.BlockSpec((slots * local, model), whole, pipeline_mode=once),
+                pl.BlockSpec((1, 2 * PAIR), across),
+            ]
+            + [pl.BlockSpec((shape[0], 2 * PAIR), across) for shape, _ in weight_outs],
             scratch_shapes=[
                 pltpu.VMEM((4, PAIR, rows), F32),
                 pltpu.VMEM((4, rows, PAIR), BF),
                 pltpu.VMEM((4, PAIR, rows), BF),
                 pltpu.VMEM((keys, 2 * PAIR), F32),
                 pltpu.VMEM((4, 2, rows), F32),
+                pltpu.VMEM((model, slots * keys), BF),
+                pltpu.VMEM((slots * keys, model), F32),
+                pltpu.VMEM((model, 2 * PAIR), F32),
             ],
         ),
         out_shape=[
             jax.ShapeDtypeStruct((width, rows), F32),
             jax.ShapeDtypeStruct((width, rows), BF),
-            jax.ShapeDtypeStruct(kv.shape, BF),
-        ],
+            jax.ShapeDtypeStruct((slots * local, model), F32),
+            jax.ShapeDtypeStruct((slots * local, model), BF),
+            jax.ShapeDtypeStruct((1, 2 * width), F32),
+        ]
+        + [jax.ShapeDtypeStruct(shape, kind) for shape, kind in weight_outs],
         compiler_params=params(),
-        cost_estimate=cost(40 * total, 8 * both.size + 4 * kv.size, total // HD),
+        cost_estimate=cost(40 * total, 8 * both.size + 4 * kv.size + 8 * len(flat) * local * model, total // HD),
         name="attend_back",
-    )(counts, both, g_own, g_oth, kv)
+    )(counts, both, g_own, g_oth, kv, w_kv, *flat, *extra)
 
 
 def merge_kernel(pairs, seqs, where, o_own, lse_own, *refs):
@@ -1117,7 +1110,8 @@
 
     starts = jnp.stack([(spot ^ k) * span + side * chip for k in range(spots)])
     key_counts = jnp.clip(lengths[:, None] - starts[None, :], 0, chip)
-    counts = jnp.concatenate([key_counts, jnp.full((seqs, 1), spot, jnp.int32)], axis=1).astype(jnp.int32)
+    facts = jnp.stack([spot, core, lax.axis_index("dp")]).astype(jnp.int32)
+    counts = jnp.concatenate([key_counts.astype(jnp.int32), jnp.broadcast_to(facts, (seqs, 3))], axis=1)
     row_counts = jnp.clip(lengths - (spot * span + part * local), 0, local).astype(jnp.int32)
     where = jnp.stack([core, lax.axis_index("dp")]).astype(jnp.int32)
 
@@ -1129,13 +1123,10 @@
 
     lines = lax.axis_size("dp")
     own_width = 2 * heads_width
-    attention_shard = pack([query_weight, key_weight, value_weight], [False] * 3)
-    feed_shard = pack([output_weight, inner_weight, outer_weight], [True, False, True])
+    attention_shard = pack([[(query_weight, False), (key_weight, False), (value_weight, False)]])
+    feed_shard = pack([[(output_weight, True), (inner_weight, False)], [(outer_weight, True)]])
     biases = jnp.concatenate([query_bias, value_bias, inner_bias])[None, :]
     x_rows = [block_input[s] for s in range(seqs)]
-
-    came, biases_came, *near = together(other_core(block_input), other_side(biases), *over_spots(attention_shard))
-    attention_near = stack([attention_shard] + near)
 
     def send_near(own):
         return [swap(own, "ctx", 2), swap(own, "ctx", 1)] if spots == 4 else over_spots(own)
@@ -1152,19 +1143,20 @@
         in_middle = jnp.logical_or(spot == 1, spot == 2)
         return [nears[1], nears[0], jnp.where(in_middle, lasts[0], lasts[1])]
 
-    begin = together(attention_near, *x_rows)
-    attention_near, first_rows_out = begin[0], begin[1]
-    attention_other, attention_line, across_0, *nears = together(
-        other_side(attention_near),
-        swap(attention_near, "dp", 1),
-        other_side(first_rows_out),
-        *send_near(first_rows_out),
+    came, across, *near = together(other_core(block_input), other_side(block_input), *over_spots(attention_shard))
+    first_out = after(x_rows[0], *near)
+    (attention_near,) = stack([attention_shard, *near])
+    diagonal = [(d * 4 + t, (1 - d) * 4 + (t ^ 2)) for d in range(2) for t in range(4)]
+    over_both = [lax.ppermute(attention_near, ("dp", "tp"), diagonal)] if lines == 2 else []
+    attention_other, attention_line, *nears = together(
+        other_side(attention_near), swap(attention_near, "dp", 1), *over_both, *send_near(first_out)
     )
-    other_line = swap(attention_other, "dp", 1)
-    across = [across_0, other_side(after(x_rows[1], attention_other))]
+    if lines == 2:
+        other_line, *nears = nears
     cores = [other_core(n) for n in nears]
     lasts = send_last(after(x_rows[0], *nears), nears[0]) if spots == 4 else []
-    other_line, across[1], *rest = together(other_line, across[1], *lasts, *cores)
+    biases_came = other_side(after(biases, *nears))
+    biases_came, *rest = together(biases_came, *lasts, *cores)
     lasts, cores = rest[: len(lasts)], rest[len(lasts) :]
     arrived = [finish(nears, lasts)]
     if spots == 4:
@@ -1187,36 +1179,42 @@
     feed_shard = after(feed_shard, arrived[0][-1])
     feed_near = over_spots(feed_shard)
     second_nears = send_near(after(x_rows[1], arrived[0][-1]))
-    q, made = project(where, pieces[0] + [(across[0], across_core)], query_full, kv_full, query_b, kv_bias)
+    weights = (query_full, kv_full, query_b, kv_bias)
+    q, made, own, packed, lse = attend(counts[0], seqs, 0, pieces[0] + [(across[0], across_core)], weights, ())
     queries, kv = [q], [made]
-    own, packed, lse = attend(counts[0], spots, seqs, 0, q, made, ())
     packs = [packed]
 
     own, *rest = together(own, *feed_near, *second_nears)
     feed_near, nears = rest[: len(feed_near)], rest[len(feed_near) :]
     across_core = other_core(across[1])
-    feed_near = stack([feed_shard] + feed_near)
-    second = after(x_rows[1], own)
     cores = [other_core(n) for n in nears]
-    lasts = send_last(after(second, *nears), nears[0]) if spots == 4 else []
-    feed_other, near_line, *rest = together(other_side(feed_near), swap(feed_near, "dp", 1), *lasts, *cores)
+    lasts = send_last(after(x_rows[1], own), nears[0]) if spots == 4 else []
+    near_a, near_b = stack([after(feed_shard, *cores)] + feed_near, feed_shard.shape[1] - unit_width - -unit_width % 128)
+    other_a, line_b, *rest = together(other_side(near_a), swap(near_b, "dp", 1), *lasts, *cores)
+    packs[0] = other_side(after(packs[0], other_a))
     lasts, cores = rest[: len(lasts)], rest[len(lasts) :]
     arrived.append(finish(nears, lasts))
     if spots == 4:
         cores = [cores[1], cores[0], other_core(arrived[1][2])]
     pieces.append([(x_rows[1], came[1])] + list(zip(arrived[1], cores)))
-    packs[0] = other_side(after(packs[0], feed_other))
-    q, made = project(where, pieces[1] + [(across[1], across_core)], query_full, kv_full, query_b, kv_bias)
+    if lines == 2:
+        last_b = [near_b, line_b]
+        sent_a = [swap(after(a, line_b), "dp", 1) for a in (near_a, other_a)]
+        sent_b = [other_side(after(b, other_a)) for b in last_b]
+    q, made, own, packed, lse = attend(counts[1], seqs, 1, pieces[1] + [(across[1], across_core)], weights, (own, lse))
     queries.append(q)
     kv.append(made)
-    own, packed, lse = attend(counts[1], spots, seqs, 1, q, made, (own, lse))
+    buffers = (own, lse)
     packs.append(other_side(packed))
-    buffers = (own, lse)
     if lines == 2:
-        feed_all = [[feed_near, feed_other], [near_line, swap(feed_other, "dp", 1, (), (own,))]]
+        sent = together(*sent_a, *sent_b, own)
+        sent_a, sent_b = list(sent[:2]), list(sent[2:4])
+        all_a = [[near_a, other_a], sent_a]
+        all_b = [[near_b, sent_b[0]], [line_b, sent_b[1]]]
     else:
-        feed_all = over_dp([feed_near, feed_other])
-    output_full, inner_full, outer_full = place(feed_all, [heads_width, unit_width, unit_width], [(0,), (1,), (2,)])
+        all_a, all_b = over_dp([near_a, other_a]), over_dp([near_b, other_side(near_b)])
+    output_full, inner_full = place(all_a, [heads_width, unit_width], [(0,), (1,)])
+    (outer_full,) = place(all_b, [unit_width], [(0,)])
 
     vectors = jnp.stack([output_bias, first_gain, first_shift, closing_offset_vector, second_gain, second_shift])
     vectors = jnp.concatenate([vectors, jnp.zeros((2, width), F32)])
@@ -1284,16 +1282,25 @@
     def sides_of(pair, width_of_side):
         return [(pair, 0, width_of_side)], [(pair, width_of_side, width_of_side)]
 
-    def kv_step(s, dkv, before):
-        mine, other, bias, *grads = kv_back(where, pieces[s], dkv, kv_full, before, s == seqs - 1)
-        total = (mine + other_core(other).astype(F32)).reshape(spots, local, width)
-        return total[0], [total[k].astype(BF) for k in range(1, spots)], bias, grads
-
-    own, oth, dkv = attend_back(counts[0], spots, queries[0], g_own[0], g_oth[0], kv[0])
-    dq_own, dq_came = [own], [other_side(oth)]
-    feed_pairs = [over_lines(d_feed, (dkv,))]
-    output_pair = over_lines(d_output, (dkv,))
-    kept_0, sent_0, kv_bias_sum, kv_grads = kv_step(0, dkv, None)
+    def back(s, g_in, before):
+        return attend_back(
+            counts[s], queries[s], g_own[s], g_in, kv[s], kv_full, pieces[s], before, s == seqs - 1
+        )
+
+    def by_spot(mine, came):
+        total = (mine + came.astype(F32)).reshape(spots, local, width)
+        return total[0], [total[k].astype(BF) for k in range(1, spots)]
+
+    shared = jnp.concatenate([second_sums[:3], first_sums[:3]])
+    shared_came = other_core(shared)
+    output_mine, output_came = over_lines(d_output)
+    g_in, output_came, shared_came = together(g_oth[0], output_came, shared_came)
+    output_pair, shared = (output_mine, output_came), shared + shared_came
+    own, oth, mine, other, kv_bias_sum, *kv_grads = back(0, g_in, None)
+    dq_own = [own]
+    dq_came_0 = other_side(oth)
+    kept_0, sent_0 = by_spot(mine, other_core(other))
+    feed_pairs = [over_lines(d_feed, (kv_bias_sum,))]
     feed_kept, feed_sent = fold_sides(
         feed_pairs,
         [
@@ -1303,34 +1310,33 @@
     )
     feed_term = other_side(feed_sent)
     came_0 = [swap(t, "ctx", k + 1) for k, t in enumerate(sent_0)]
-    g_in = after(g_oth[1], feed_sent, *sent_0)
-    own, oth, dkv = attend_back(counts[1], spots, queries[1], g_own[1], g_in, kv[1])
+    g_in, dq_came_0, *_ = together(g_oth[1], dq_came_0, feed_sent, *sent_0)
+    own, oth, mine, other, kv_bias_sum, *kv_grads = back(1, g_in, (kv_grads[0], kv_bias_sum))
     dq_own.append(own)
-    dq_came.append(other_side(oth))
-
-    dkv, feed_term, *came_0 = together(dkv, feed_term, *came_0)
-    feed_rows = fold_spots(feed_kept, feed_term)
-    feed_terms = [swap(t, "ctx", k + 1) for k, t in enumerate(feed_rows[1:])]
-    dkv = after(dkv, *feed_rows)
-    kept_1, sent_1, kv_bias_sum, kv_grads = kv_step(1, dkv, (kv_grads[0], kv_bias_sum))
+
+    oth, other, feed_term, *rest = together(oth, other, feed_term, *came_0, *kv_grads)
+    came_0, kv_grads = rest[: spots - 1], rest[spots - 1 :]
+    dq_came_1 = other_side(oth)
+    kept_1, sent_1 = by_spot(mine, other_core(other))
+    feed_all_rows = add_low(feed_kept, feed_term)
+    feed_spread = lax.all_to_all(feed_all_rows, "ctx", split_axis=0, concat_axis=0, tiled=True)
+    dq_came = [dq_came_0, after(dq_came_1, feed_all_rows, *sent_1)]
     kv_pair = over_lines(kv_grads)
     mine, other, query_bias_sum, *query_grads = query_back(
-        where, dq_own, [dq_came[0], after(dq_came[1], *kv_grads)], x_rows, [came[s] for s in range(seqs)], query_full
+        where, dq_own, dq_came, x_rows, [came[s] for s in range(seqs)], query_full
     )
     query_term = (mine + other_core(other).astype(F32)).reshape(seqs, local, width)
     query_pair = over_lines(query_grads)
     value_bias_sum = apart(kv_bias_sum)[1]
-    shared = jnp.concatenate([second_sums[:3], first_sums[:3]])
-    shared = shared + other_core(shared)
     vector = jnp.concatenate(
         [shared.reshape(1, -1), d_inner_bias, query_bias_sum.reshape(1, -1), value_bias_sum], axis=1
     )
     for bit in bits_of("dp"):
         vector = vector + swap(vector, "dp", bit)
     if lines == 2:
-        query_last, kv_last, vector, *feed_terms = together(query_pair[1], kv_pair[1], vector, *feed_terms)
+        query_last, kv_last, vector = together(query_pair[1], kv_pair[1], vector)
         query_pair, kv_pair = (query_pair[0], query_last), (kv_pair[0], kv_last)
-    came_1 = [swap(after(t, vector), "ctx", k + 1) for k, t in enumerate(sent_1)]
+    came_1 = [swap(t, "ctx", k + 1) for k, t in enumerate(sent_1)]
 
     def side_cuts(pair, offset):
         cuts = []
@@ -1347,12 +1353,13 @@
         [query_pair, kv_pair, output_pair],
         [sides_of(0, heads_width), side_cuts(1, 0), side_cuts(1, PAIR), sides_of(2, heads_width)],
     )
-    term, *came_1 = together(other_side(sent), *came_1)
+    term, feed_spread, *came_1 = together(other_side(sent), feed_spread, *came_1)
     rows = fold_spots(kept, term)
-    vector = vector + sum(swap(vector, "ctx", k) for k in range(1, spots))
+    for bit in bits_of("ctx"):
+        vector = vector + swap(vector, "ctx", bit)
     terms = [swap(t, "ctx", k + 1) for k, t in enumerate(rows[1:])]
     vector = (vector + other_side(vector))[0]
-    feed_owned = feed_rows[0] + sum(t.astype(F32) for t in feed_terms)
+    feed_owned = jnp.sum(feed_spread.reshape(spots, -1, feed_spread.shape[1]).astype(F32), axis=0)
     owned = rows[0] + sum(t.astype(F32) for t in terms)
     first_grad = first_grad.reshape(seqs, local, width)
     input_grad = jnp.stack(

time: 524 us -> 493 us (0.941)
  starting transfers between devices: 96.9 us -> 75.4 us
  waiting for transfers between devices: 170 us -> 154 us
  Pallas kernels: 207 us -> 218 us
    ppermute x67 -> x64, starting transfers between devices: 92.5 us -> 64.9 us  [swap(): lax.ppermute(after(value, *start), axis, [(i, i ^ bit) for i in range(cou...]
    ppermute x67 -> x64, waiting for transfers between devices: 152 us -> 139 us  [swap(): lax.ppermute(after(value, *start), axis, [(i, i ^ bit) for i in range(cou...]
    pallas_call x8 -> x5, Pallas kernels: 104 us -> 117 us  [the longest x2 70.8 us: attend_back(): pl.pallas_call(functools.partial(attend_back_kernel, slots, pairs, split,...]
    unnamed x144 -> x164, local copies, waits for them, and re-layouts: 16.9 us -> 13.9 us
  transfers between devices with their start and end apart: 71 -> 70, of which waited for: 32 -> 33; matrix products, arithmetic and copies ran while one was open for 5% -> 5% of each run, Pallas kernels for 27% -> 31%
where the time goes in v1:
time: 493 us; the launch traced here: 485 us
  Pallas kernels  218 us (44%)
  waiting for transfers between devices  154 us (31%)
  starting transfers between devices  75.4 us (15%)
  local copies, waits for them, and re-layouts  20.3 us (4%)
  other arithmetic  15.8 us (3%)
    ppermute x64, waiting for transfers between devices, swap(): lax.ppermute(after(value, *start), axis, [(i, i ^ bit) for i in range(cou...  139 us
    pallas_call x2, Pallas kernels, attend_back(): pl.pallas_call(functools.partial(attend_back_kernel, slots, pairs, split,...  70.8 us
    ppermute x64, starting transfers between devices, swap(): lax.ppermute(after(value, *start), axis, [(i, i ^ bit) for i in range(cou...  64.9 us
    pallas_call x2, Pallas kernels, attend(): pl.pallas_call(functools.partial(attend_kernel, slots, min(128, keys), le...  42.7 us
    pallas_call x9, Pallas kernels, call(): pl.pallas_call(kernel, grid_spec=pltpu.PrefetchScalarGridSpec(num_scalar_...  29.5 us
    pallas_call x1, Pallas kernels, feed_back(): pl.pallas_call(functools.partial(feed_back_kernel, half, lines), grid_spe...  19.8 us
    pallas_call x3, Pallas kernels, row_call(): pl.pallas_call(kernel, grid_spec=pltpu.PrefetchScalarGridSpec(num_scalar_...  15.6 us
    ppermute x2, waiting for transfers between devices, send_last(): lax.ppermute(far, 'ctx', [(2, 3), (1, 0)])  15.5 us
  transfers between devices with their start and end apart: 70, of which 33 were waited for; matrix products, arithmetic and copies ran while one was open for 5% of the time, Pallas kernels for 31%

profile of v1, /device:TPU:0, one launch (start us, length us, event | category | flops | bytes accessed | tf_op | source)
XLA Modules:
  0.0 485.4 jit_solution(9337407047607912548)
XLA Ops:
  1.2 2.6 collective-permute-start.1
  5.5 3.6 collective-permute-start.4
  13.8 6.2 %collective-permute-done.3.refs_2_ = bf16[96,640]{1,0:T(8,128)(2,1)S(1)} collective-permute-done((bf16[96,640]{1,0:T(8,128)(2,1)}, bf16[96,640]{1,0:T(8,128)(2,1)S(1)}, u32[]{:S(2)}, u32[]{:S(2)}) %collective-permute-start.3) | collective-permute-done | bytes 122912 | tf_op jit(solution)/shard_map/ppermute | solution.py:46
  20.1 2.1 collective-permute-done.1
  22.2 1.9 stack.98.refs_0_
  24.1 2.7 collective-permute-start.7
  27.7 1.9 copy.39.refs_2_
  29.6 2.1 pack.3.refs_0_
  33.5 2.6 collective-permute-start.8
  36.6 13.4 %collective-permute-done.9.refs_2_ = bf16[256,768]{1,0:T(8,128)(2,1)S(1)} collective-permute-done((bf16[256,768]{1,0:T(8,128)(2,1)S(1)}, bf16[256,768]{1,0:T(8,128)(2,1)S(1)}, u32[]{:S(2)}, u32[]{:S(2)}) %collective-permute-start.9) | collective-permute-done | bytes 393248 | tf_op jit(solution)/shard_map/ppermute | solution.py:46
  50.0 2.4 collective-permute-done.8.refs_4_
  57.6 3.9 place.3
  61.6 4.4 collective-permute-done.12
  66.1 2.5 collective-permute-start.19
  68.6 2.7 collective-permute-start.18
  72.4 2.0 collective-permute-start.21
  76.2 18.3 %attend.2 = (bf16[1024,384]{1,0:T(8,128)(2,1)}, bf16[2048,768]{1,0:T(8,128)(2,1)}, f32[2,384,512]{2,1,0:T(8,128)}, bf16[432,512]{1,0:T(8,128)(2,1)}, f32[2,3,2,512]{3,2,1,0:T(2,128)}) custom-call(s32[7]{0:T(128)} %get-tuple-element.362.counts, bf16[256,768]{1,0:T(8,128)(2,1)} %copy-done.2, bf16[256,768]{1,0:T(8,128)(2,1)} %get-tuple-element.344.refs_1_.refs_6_, ...), custom_call_target="tpu_custom_call" | custom-call | flops 12884901888 | bytes 10223616 | tf_op jit(solution)/shard_map/attend/pallas_call | solution.py:475
  94.5 5.7 %collective-permute-done.18.refs_2_ = bf16[96,1792]{1,0:T(8,128)(2,1)S(1)} collective-permute-done((bf16[96,1792]{1,0:T(8,128)(2,1)S(1)}, bf16[96,1792]{1,0:T(8,128)(2,1)S(1)}, u32[]{:S(2)}, u32[]{:S(2)}) %collective-permute-start.18) | collective-permute-done | bytes 344096 | tf_op jit(solution)/shard_map/ppermute | solution.py:46
  100.9 15.3 %collective-permute-done.20.refs_4_ = bf16[256,768]{1,0:T(8,128)(2,1)S(1)} collective-permute-done((bf16[256,768]{1,0:T(8,128)(2,1)S(1)}, bf16[256,768]{1,0:T(8,128)(2,1)S(1)}, u32[]{:S(2)}, u32[]{:S(2)}) %collective-permute-start.20) | collective-permute-done | bytes 393248 | tf_op jit(solution)/shard_map/ppermute | solution.py:46
  118.5 2.6 stack.99
  126.2 11.1 %collective-permute-done.27 = bf16[256,768]{1,0:T(8,128)(2,1)S(1)} collective-permute-done((bf16[256,768]{1,0:T(8,128)(2,1)S(1)}, bf16[256,768]{1,0:T(8,128)(2,1)S(1)}, u32[]{:S(2)}, u32[]{:S(2)}) %collective-permute-start.27) | collective-permute-done | bytes 393248 | tf_op jit(solution)/shard_map/ppermute | solution.py:1137
  137.9 3.0 collective-permute-done.24.refs_1_
  146.9 24.4 %attend.3 = (bf16[1024,384]{1,0:T(8,128)(2,1)}, bf16[2048,768]{1,0:T(8,128)(2,1)}, f32[2,384,512]{2,1,0:T(8,128)}, bf16[432,512]{1,0:T(8,128)(2,1)}, f32[2,3,2,512]{3,2,1,0:T(2,128)}) custom-call(s32[7]{0:T(128)} %get-tuple-element.363.counts, bf16[256,768]{1,0:T(8,128)(2,1)} %copy-done.3, ...), custom_call_target="tpu_custom_call", output_to_operand_aliasing={{2}: (15, {}), {4}: (16, {})} | custom-call | flops 12884901888 | bytes 10223616 | tf_op jit(solution)/shard_map/attend/pallas_call | solution.py:475
  172.0 7.3 %collective-permute-done.35.refs_3_ = bf16[384,768]{1,0:T(8,128)(2,1)S(1)} collective-permute-done((bf16[384,768]{1,0:T(8,128)(2,1)S(1)}, bf16[384,768]{1,0:T(8,128)(2,1)S(1)}, u32[]{:S(2)}, u32[]{:S(2)}) %collective-permute-start.35) | collective-permute-done | bytes 589856 | tf_op jit(solution)/shard_map/ppermute | solution.py:46
  181.7 4.9 place.4
  189.1 5.1 %merge.1 = (f32[2,384,512]{2,1,0:T(8,128)}, bf16[2,384,512]{2,1,0:T(8,128)(2,1)}, f32[2,256,768]{2,1,0:T(8,128)}, bf16[2,256,768]{2,1,0:T(8,128)(2,1)}, f32[2,3,2,512]{3,2,1,0:T(2,128)}) custom-call(s32[2]{0:T(128)} %pad_add_fusion.1.where, f32[2,384,512]{2,1,0:T(8,128)} %get-tuple-element.191.o_own, f32[2,3,2,512]{3,2,1,0:T(2,128)} %get-tuple-element.192.lse_own, ...), custom_call_target="tpu_custom_call" | custom-call | flops 603979776 | bytes 7864320 | tf_op jit(solution)/shard_map/merge/pallas_call | solution.py:717
  197.6 4.5 first_norm.1
  202.9 3.8 place.5.w_out
  207.6 14.8 %feed.1 = (bf16[1024,1536]{1,0:T(8,128)(2,1)}, bf16[1024,1536]{1,0:T(8,128)(2,1)}, f32[512,768]{1,0:T(8,128)}, bf16[512,768]{1,0:T(8,128)(2,1)}) custom-call(bf16[512,768]{1,0:T(8,128)(2,1)} %get-tuple-element.208.own_ref, bf16[512,768]{1,0:T(8,128)(2,1)} %copy-done.57, bf16[768,1536]{1,0:T(8,128)(2,1)} %get-tuple-element.209.w_in, ...), custom_call_target="tpu_custom_call" | custom-call | flops 4831838208 | bytes 15728640 | tf_op jit(solution)/shard_map/feed/pallas_call | solution.py:867
  225.7 6.0 %second_norm.1 = (f32[512,768]{1,0:T(8,128)}, f32[512,768]{1,0:T(8,128)}, bf16[512,768]{1,0:T(8,128)(2,1)}, f32[8,768]{1,0:T(8,128)}) custom-call(s32[2]{0:T(128)} %subtract_clamp_fusion.1.counts, f32[512,768]{1,0:T(8,128)} %get-tuple-element.207.normal_ref, f32[512,768]{1,0:T(8,128)} %get-tuple-element.212.mine_ref, bf16[512,768]{1,0:T(8,128)(2,1)} %copy-done.8, ...), custom_call_target="tpu_custom_call" | custom-call | flops 7864320 | bytes 9437184 | tf_op jit(solution)/shard_map/second_norm/pallas_call | solution.py:1042
  232.2 2.1 collective-permute-done.39.low_came
  235.2 19.8 %feed_back.1 = (f32[512,768]{1,0:T(8,128)}, bf16[512,768]{1,0:T(8,128)(2,1)}, f32[1,1536]{1,0:T(1,128)}, bf16[384,3072]{1,0:T(8,128)(2,1)}, bf16[384,3072]{1,0:T(8,128)(2,1)}) custom-call(s32[2]{0:T(128)} %pad_add_fusion.1.where, bf16[512,768]{1,0:T(8,128)(2,1)} %get-tuple-element.216.low_own, bf16[512,768]{1,0:T(8,128)(2,1)} %copy-done.58, ...), custom_call_target="tpu_custom_call" | custom-call | flops 9663676416 | bytes 22020096 | tf_op jit(solution)/shard_map/feed_back/pallas_call | solution.py:941
  255.4 2.1 collective-permute-done.40.came_ref
  258.5 5.0 %first_norm_back.1 = (f32[512,768]{1,0:T(8,128)}, bf16[512,768]{1,0:T(8,128)(2,1)}, f32[8,768]{1,0:T(8,128)}) custom-call(f32[512,768]{1,0:T(8,128)} %get-tuple-element.215.grad_ref, f32[512,768]{1,0:T(8,128)} %get-tuple-element.219.mine_ref, bf16[512,768]{1,0:T(8,128)(2,1)} %copy-done.14, f32[512,768]{1,0:T(8,128)} %get-tuple-element.207.normal_ref, ...), custom_call_target="tpu_custom_call" | custom-call | flops 7864320 | bytes 8652800 | tf_op jit(solution)/shard_map/first_norm_back/pallas_call | solution.py:1042
  263.9 2.1 collective-permute-done.41.came_ref
  266.9 6.6 %turn.1 = (bf16[432,512]{1,0:T(8,128)(2,1)}, bf16[432,512]{1,0:T(8,128)(2,1)}, f32[384,384]{1,0:T(8,128)}, bf16[384,384]{1,0:T(8,128)(2,1)}) custom-call(s32[2]{0:T(128)} %pad_add_fusion.1.where, bf16[2,256,768]{2,1,0:T(8,128)(2,1)} %bitcast.53, bf16[2,256,768]{2,1,0:T(8,128)(2,1)} %copy-done.9, bf16[768,384]{1,0:T(8,128)(2,1)} %get-tuple-element.204.refs_2_.weight, ...), custom_call_target="tpu_custom_call" | custom-call | flops 1207959552 | bytes 4718592 | tf_op jit(solution)/shard_map/turn/pallas_call | solution.py:794
  277.9 7.3 %collective-permute-done.43.refs_5_ = bf16[384,384]{1,0:T(8,128)(2,1)S(1)} collective-permute-done((bf16[384,384]{1,0:T(8,128)(2,1)}, bf16[384,384]{1,0:T(8,128)(2,1)S(1)}, u32[]{:S(2)}, u32[]{:S(2)}) %collective-permute-start.43) | collective-permute-done | bytes 294944 | tf_op jit(solution)/shard_map/ppermute | solution.py:46
  287.0 29.1 %attend_back.2 = (f32[384,512]{1,0:T(8,128)}, bf16[384,512]{1,0:T(8,128)(2,1)}, f32[1024,768]{1,0:T(8,128)}, bf16[1024,768]{1,0:T(8,128)(2,1)}, f32[1,768]{1,0:T(1,128)}, /*index=5*/f32[768,768]{1,0:T(8,128)}) custom-call(s32[7]{0:T(128)} %get-tuple-element.362.counts, bf16[1024,384]{1,0:T(8,128)(2,1)} %get-tuple-element.223.both, ...), custom_call_target="tpu_custom_call" | custom-call | flops 32212254720 | bytes 22020096 | tf_op jit(solution)/shard_map/attend_back/pallas_call | solution.py:631
  316.3 3.9 collective-permute-start.45
  320.2 14.6 %collective-permute-done.47.refs_1_ = bf16[384,3072]{1,0:T(8,128)(2,1)S(1)} collective-permute-done((bf16[384,3072]{1,0:T(8,128)(2,1)S(1)}, bf16[384,3072]{1,0:T(8,128)(2,1)S(1)}, u32[]{:S(2)}, u32[]{:S(2)}) %collective-permute-start.47) | collective-permute-done | bytes 2359328 | tf_op jit(solution)/shard_map/ppermute | solution.py:46
  336.3 5.0 %fold_sides.2 = (f32[384,1536]{1,0:T(8,128)}, bf16[384,1536]{1,0:T(8,128)(2,1)}) custom-call(s32[1]{0:T(128)} %bitcast.15.where, bf16[384,3072]{1,0:T(8,128)(2,1)} %get-tuple-element.238.refs_0_, bf16[384,3072]{1,0:T(8,128)(2,1)} %copy-done.1), custom_call_target="tpu_custom_call" | custom-call | bytes 8257536 | tf_op jit(solution)/shard_map/fold_sides/pallas_call | solution.py:208
  341.8 2.1 fusion.6
  344.0 2.5 collective-permute-start.52
  346.5 1.9 collective-permute-start.50
  348.4 41.6 %attend_back.3 = (f32[384,512]{1,0:T(8,128)}, bf16[384,512]{1,0:T(8,128)(2,1)}, f32[1024,768]{1,0:T(8,128)}, bf16[1024,768]{1,0:T(8,128)(2,1)}, f32[1,768]{1,0:T...) custom-call(s32[7]{0:T(128)} %get-tuple-element.363.counts, bf16[1024,384]{1,0:T(8,128)(2,1)} %get-tuple-element.235.both, ...), custom_call_target="tpu_custom_call" | custom-call | flops 32212254720 | bytes 22020096 | tf_op jit(solution)/shard_map/attend_back/pallas_call | solution.py:631
  391.1 3.9 add_low.1
  395.0 3.9 all-to-all-start
  399.0 4.0 fusion.5
  404.1 5.6 %collective-permute-done.53.refs_3_ = bf16[384,512]{1,0:T(8,128)(2,1)S(1)} collective-permute-done((bf16[384,512]{1,0:T(8,128)(2,1)}, bf16[384,512]{1,0:T(8,128)(2,1)S(1)}, u32[]{:S(2)}, u32[]{:S(2)}) %collective-permute-start.53) | collective-permute-done | bytes 393248 | tf_op jit(solution)/shard_map/ppermute | solution.py:46
  410.5 6.2 %query_back.1 = (f32[512,768]{1,0:T(8,128)}, bf16[512,768]{1,0:T(8,128)(2,1)}, f32[384,1]{1,0:T(8,128)}, f32[384,384]{1,0:T(8,128)}, bf16[384,384]{1,0:T(8,128)(2,1)}) custom-call(s32[2]{0:T(128)} %pad_add_fusion.1.where, f32[384,512]{1,0:T(8,128)} %get-tuple-element.234.refs_0_, f32[384,512]{1,0:T(8,128)} %get-tuple-element.248.refs_1_, ...), custom_call_target="tpu_custom_call" | custom-call | flops 1207959552 | bytes 8848896 | tf_op jit(solution)/shard_map/query_back/pallas_call | solution.py:68
  417.8 2.1 collective-permute-start.58
  419.9 5.2 %collective-permute-done.58 = f32[1,6912]{1,0:T(1,128)S(1)} collective-permute-done((f32[1,6912]{1,0:T(1,128)S(1)}, f32[1,6912]{1,0:T(1,128)S(1)}, u32[]{:S(2)}, u32[]{:S(2)}) %collective-permute-start.58) | collective-permute-done | bytes 27680 | tf_op jit(solution)/shard_map/ppermute | solution.py:46
  426.5 2.6 collective-permute-done.66
  429.2 2.5 collective-permute-start.67
  431.6 2.6 collective-permute-done.67
  434.7 3.6 collective-permute-start.62
  439.1 4.4 fold_sides.3
  446.8 2.1 collective-permute-done.62
  448.9 19.2 %collective-permute-done.61 = bf16[256,768]{1,0:T(8,128)(2,1)} collective-permute-done((bf16[256,768]{1,0:T(8,128)(2,1)}, bf16[256,768]{1,0:T(8,128)(2,1)}, u32[]{:S(2)}, u32[]{:S(2)}) %collective-permute-start.61) | collective-permute-done | bytes 393248 | tf_op jit(solution)/shard_map/ppermute | solution.py:46
  468.1 2.4 fold_spots.1
  470.6 2.5 collective-permute-start.64
  473.1 1.9 collective-permute-start.65
  476.0 2.2 fusion.3
  479.4 4.2 collective-permute-done.64
  (315 shorter events, 72.7 us)
Async XLA Ops:
  0.7 19.4 %collective-permute-start = (bf16[2,256,768]{2,1,0:T(8,128)(2,1)}, bf16[2,256,768]{2,1,0:T(8,128)(2,1)S(1)}, u32[]{:S(2)}, u32[]{:S(2)}) collective-permute-start(bf16[2,256,768]{2,1,0:T(8,128)(2,1)} %param.18), channel_id=1, source_target_pairs={{0,1},{1,0},{2,3},{3,2},{4,5},{5,4},{6,7},{7,6},{8,9},{9,8},{10,11... | collective-permute-start | bytes 2359304 | tf_op jit(solution)/shard_map/ppermute | solution.py:46
  1.2 20.9 %collective-permute-start.1 = (bf16[2,256,768]{2,1,0:T(8,128)(2,1)}, bf16[2,256,768]{2,1,0:T(8,128)(2,1)S(1)}, u32[]{:S(2)}, u32[]{:S(2)}) collective-permute-start(bf16[2,256,768]{2,1,0:T(8,128)(2,1)} %param.18), channel_id=1, source_target_pairs={{0,2},{1,3},{2,0},{3,1},{4,6},{5,7},{6,4},{7,5},{8,10},{9,11},{10,... | collective-permute-start | bytes 2359304 | tf_op jit(solution)/shard_map/ppermute | solution.py:46
  5.5 8.3 %collective-permute-start.4 = (bf16[96,640]{1,0:T(8,128)(2,1)}, bf16[96,640]{1,0:T(8,128)(2,1)S(1)}, u32[]{:S(2)}, u32[]{:S(2)}) collective-permute-start(bf16[96,640]{1,0:T(8,128)(2,1)} %pack.2.refs_0_), channel_id=1, source_target_pairs={{0,12},{4,8},{8,4},{12,0},{1,13},{5,9},{9,5},{13,1},{2,14},{6,10},... | collective-permute-start | bytes 368648 | tf_op jit(solution)/shard_map/ppermute | solution.py:46
  9.1 10.9 %collective-permute-start.3 = (bf16[96,640]{1,0:T(8,128)(2,1)}, bf16[96,640]{1,0:T(8,128)(2,1)S(1)}, u32[]{:S(2)}, u32[]{:S(2)}) collective-permute-start(bf16[96,640]{1,0:T(8,128)(2,1)} %pack.2.refs_0_), channel_id=1, source_target_pairs={{0,8},{4,12},{8,0},{12,4},{1,9},{5,13},{9,1},{13,5},{2,10},{6,14},... | collective-permute-start | bytes 368648 | tf_op jit(solution)/shard_map/ppermute | solution.py:46
  9.1 10.9 %collective-permute-start.2 = (bf16[96,640]{1,0:T(8,128)(2,1)}, bf16[96,640]{1,0:T(8,128)(2,1)S(1)}, u32[]{:S(2)}, u32[]{:S(2)}) collective-permute-start(bf16[96,640]{1,0:T(8,128)(2,1)} %pack.2.refs_0_), channel_id=1, source_target_pairs={{0,4},{4,0},{8,12},{12,8},{1,5},{5,1},{9,13},{13,9},{2,6},{6,2},{1... | collective-permute-start | bytes 368648 | tf_op jit(solution)/shard_map/ppermute | solution.py:46
  24.1 28.4 %collective-permute-start.7 = (bf16[384,640]{1,0:T(8,128)(2,1)}, bf16[384,640]{1,0:T(8,128)(2,1)S(1)}, u32[]{:S(2)}, u32[]{:S(2)}) collective-permute-start(bf16[384,640]{1,0:T(8,128)(2,1)} %stack.98.refs_0_), channel_id=1, source_target_pairs={{0,18},{1,19},{2,16},{3,17},{16,2},{17,3},{18,0},{19,1},{4,22},{5,... | collective-permute-start | bytes 1474568 | tf_op jit(solution)/shard_map/ppermute | solution.py:1150
  26.7 25.7 %collective-permute-start.6 = (bf16[384,640]{1,0:T(8,128)(2,1)}, bf16[384,640]{1,0:T(8,128)(2,1)S(1)}, u32[]{:S(2)}, u32[]{:S(2)}) collective-permute-start(bf16[384,640]{1,0:T(8,128)(2,1)} %stack.98.refs_0_), channel_id=1, source_target_pairs={{0,16},{16,0},{1,17},{17,1},{2,18},{18,2},{3,19},{19,3},{4,20},{20... | collective-permute-start | bytes 1474568 | tf_op jit(solution)/shard_map/ppermute | solution.py:46
  27.3 25.2 %collective-permute-start.5 = (bf16[384,640]{1,0:T(8,128)(2,1)}, bf16[384,640]{1,0:T(8,128)(2,1)}, u32[]{:S(2)}, u32[]{:S(2)}) collective-permute-start(bf16[384,640]{1,0:T(8,128)(2,1)} %stack.98.refs_0_), channel_id=1, source_target_pairs={{0,2},{1,3},{2,0},{3,1},{4,6},{5,7},{6,4},{7,5},{8,10},{9,11},{10,... | collective-permute-start | bytes 1474568 | tf_op jit(solution)/shard_map/ppermute | solution.py:46
  31.7 18.3 %collective-permute-start.9 = (bf16[256,768]{1,0:T(8,128)(2,1)S(1)}, bf16[256,768]{1,0:T(8,128)(2,1)S(1)}, u32[]{:S(2)}, u32[]{:S(2)}) collective-permute-start(bf16[256,768]{1,0:T(8,128)(2,1)S(1)} %get-tuple-element.161.refs_0_.refs_4_), channel_id=1, source_target_pairs={{0,4},{4,0},{8,12},{12,8},{1,5},{5,1},{9,13},{13,9},{2,6},{6,2},{1... | collective-permute-start | bytes 1179656 | tf_op jit(solution)/shard_map/ppermute | solution.py:46
  33.5 18.9 %collective-permute-start.8 = (bf16[256,768]{1,0:T(8,128)(2,1)S(1)}, bf16[256,768]{1,0:T(8,128)(2,1)S(1)}, u32[]{:S(2)}, u32[]{:S(2)}) collective-permute-start(bf16[256,768]{1,0:T(8,128)(2,1)S(1)} %get-tuple-element.161.refs_0_.refs_4_), channel_id=1, source_target_pairs={{0,8},{4,12},{8,0},{12,4},{1,9},{5,13},{9,1},{13,5},{2,10},{6,14},... | collective-permute-start | bytes 1179656 | tf_op jit(solution)/shard_map/ppermute | solution.py:46
  52.5 9.1 %collective-permute-start.14 = (bf16[256,768]{1,0:T(8,128)(2,1)S(1)}, bf16[256,768]{1,0:T(8,128)(2,1)S(1)}, u32[]{:S(2)}, u32[]{:S(2)}) collective-permute-start(bf16[256,768]{1,0:T(8,128)(2,1)S(1)} %collective-permute-done.9.refs_2_), channel_id=1, source_target_pairs={{0,1},{1,0},{2,3},{3,2},{4,5},{5,4},{6,7},{7,6},{8,9},{9,8},{10,11... | collective-permute-start | bytes 1179656 | tf_op jit(solution)/shard_map/ppermute | solution.py:46
  52.6 9.0 %collective-permute-start.13 = (bf16[256,768]{1,0:T(8,128)(2,1)S(1)}, bf16[256,768]{1,0:T(8,128)(2,1)S(1)}, u32[]{:S(2)}, u32[]{:S(2)}) collective-permute-start(bf16[256,768]{1,0:T(8,128)(2,1)S(1)} %collective-permute-done.8.refs_4_), channel_id=1, source_target_pairs={{0,1},{1,0},{2,3},{3,2},{4,5},{5,4},{6,7},{7,6},{8,9},{9,8},{10,11... | collective-permute-start | bytes 1179656 | tf_op jit(solution)/shard_map/ppermute | solution.py:46
  53.0 13.0 %collective-permute-start.12 = (bf16[256,768]{1,0:T(8,128)(2,1)S(1)}, bf16[256,768]{1,0:T(8,128)(2,1)S(1)}, u32[]{:S(2)}, u32[]{:S(2)}) collective-permute-start(bf16[256,768]{1,0:T(8,128)(2,1)S(1)} %collective-permute-done.8.refs_4_), channel_id=1, source_target_pairs={{8,12},{4,0},{9,13},{5,1},{10,14},{6,2},{11,15},{7,3},{24,28},{20,... | collective-permute-start | bytes 1179656 | tf_op jit(solution)/shard_map/ppermute | solution.py:1137
  54.3 7.2 %collective-permute-start.11 = (bf16[256,768]{1,0:T(8,128)(2,1)S(1)}, bf16[256,768]{1,0:T(8,128)(2,1)S(1)}, u32[]{:S(2)}, u32[]{:S(2)}) collective-permute-start(bf16[256,768]{1,0:T(8,128)(2,1)S(1)} %get-tuple-element.161.refs_0_.refs_4_), channel_id=1, source_target_pairs={{4,8},{8,4},{5,9},{9,5},{6,10},{10,6},{7,11},{11,7},{20,24},{24,20... | collective-permute-start | bytes 1179656 | tf_op jit(solution)/shard_map/ppermute | solution.py:1136
  56.0 5.6 %collective-permute-start.10 = (f32[1,1152]{1,0:T(1,128)S(1)}, f32[1,1152]{1,0:T(1,128)S(1)}, u32[]{:S(2)}, u32[]{:S(2)}) collective-permute-start(f32[1,1152]{1,0:T(1,128)S(1)} %broadcast_in_dim.12), channel_id=1, source_target_pairs={{0,2},{1,3},{2,0},{3,1},{4,6},{5,7},{6,4},{7,5},{8,10},{9,11},{10,... | collective-permute-start | bytes 13832 | tf_op jit(solution)/shard_map/ppermute | solution.py:46
  61.6 10.8 %collective-permute-start.16 = (bf16[256,768]{1,0:T(8,128)(2,1)S(1)}, bf16[256,768]{1,0:T(8,128)(2,1)S(1)}, u32[]{:S(2)}, u32[]{:S(2)}) collective-permute-start(bf16[256,768]{1,0:T(8,128)(2,1)S(1)} %get-tuple-element.343.refs_8_), channel_id=1, source_target_pairs={{0,1},{1,0},{2,3},{3,2},{4,5},{5,4},{6,7},{7,6},{8,9},{9,8},{10,11... | collective-permute-start | bytes 1179656 | tf_op jit(solution)/shard_map/ppermute | solution.py:46
  66.1 28.4 %collective-permute-start.19 = (bf16[96,1792]{1,0:T(8,128)(2,1)S(1)}, bf16[96,1792]{1,0:T(8,128)(2,1)S(1)}, u32[]{:S(2)}, u32[]{:S(2)}) collective-permute-start(bf16[96,1792]{1,0:T(8,128)(2,1)S(1)} %copy-done.6), channel_id=1, source_target_pairs={{0,12},{4,8},{8,4},{12,0},{1,13},{5,9},{9,5},{13,1},{2,14},{6,10},... | collective-permute-start | bytes 1032200 | tf_op jit(solution)/shard_map/ppermute | solution.py:46
  68.6 31.6 %collective-permute-start.18 = (bf16[96,1792]{1,0:T(8,128)(2,1)S(1)}, bf16[96,1792]{1,0:T(8,128)(2,1)S(1)}, u32[]{:S(2)}, u32[]{:S(2)}) collective-permute-start(bf16[96,1792]{1,0:T(8,128)(2,1)S(1)} %copy-done.6), channel_id=1, source_target_pairs={{0,8},{4,12},{8,0},{12,4},{1,9},{5,13},{9,1},{13,5},{2,10},{6,14},... | collective-permute-start | bytes 1032200 | tf_op jit(solution)/shard_map/ppermute | solution.py:46
  71.4 28.9 %collective-permute-start.17 = (bf16[96,1792]{1,0:T(8,128)(2,1)S(1)}, bf16[96,1792]{1,0:T(8,128)(2,1)S(1)}, u32[]{:S(2)}, u32[]{:S(2)}) collective-permute-start(bf16[96,1792]{1,0:T(8,128)(2,1)S(1)} %copy-done.6), channel_id=1, source_target_pairs={{0,4},{4,0},{8,12},{12,8},{1,5},{5,1},{9,13},{13,9},{2,6},{6,2},{1... | collective-permute-start | bytes 1032200 | tf_op jit(solution)/shard_map/ppermute | solution.py:46
  71.5 2.9 collective-permute-start.15
  72.4 28.5 %collective-permute-start.21 = (bf16[256,768]{1,0:T(8,128)(2,1)S(1)}, bf16[256,768]{1,0:T(8,128)(2,1)S(1)}, u32[]{:S(2)}, u32[]{:S(2)}) collective-permute-start(bf16[256,768]{1,0:T(8,128)(2,1)S(1)} %get-tuple-element.185.refs_0_.refs_5_), channel_id=1, source_target_pairs={{0,4},{4,0},{8,12},{12,8},{1,5},{5,1},{9,13},{13,9},{2,6},{6,2},{1... | collective-permute-start | bytes 1179656 | tf_op jit(solution)/shard_map/ppermute | solution.py:46
  74.4 41.8 %collective-permute-start.20 = (bf16[256,768]{1,0:T(8,128)(2,1)S(1)}, bf16[256,768]{1,0:T(8,128)(2,1)S(1)}, u32[]{:S(2)}, u32[]{:S(2)}) collective-permute-start(bf16[256,768]{1,0:T(8,128)(2,1)S(1)} %get-tuple-element.185.refs_0_.refs_5_), channel_id=1, source_target_pairs={{0,8},{4,12},{8,0},{12,4},{1,9},{5,13},{9,1},{13,5},{2,10},{6,14},... | collective-permute-start | bytes 1179656 | tf_op jit(solution)/shard_map/ppermute | solution.py:46
  121.1 19.8 %collective-permute-start.24 = (bf16[384,1024]{1,0:T(8,128)(2,1)}, bf16[384,1024]{1,0:T(8,128)(2,1)S(1)}, u32[]{:S(2)}, u32[]{:S(2)}) collective-permute-start(bf16[384,1024]{1,0:T(8,128)(2,1)} %get-tuple-element.198.refs_0_), channel_id=1, source_target_pairs={{0,2},{1,3},{2,0},{3,1},{4,6},{5,7},{6,4},{7,5},{8,10},{9,11},{10,... | collective-permute-start | bytes 2359304 | tf_op jit(solution)/shard_map/ppermute | solution.py:46
  122.6 15.3 %collective-permute-start.25 = (bf16[384,768]{1,0:T(8,128)(2,1)}, bf16[384,768]{1,0:T(8,128)(2,1)S(1)}, u32[]{:S(2)}, u32[]{:S(2)}) collective-permute-start(bf16[384,768]{1,0:T(8,128)(2,1)} %get-tuple-element.200.refs_0_), channel_id=1, source_target_pairs={{0,16},{16,0},{1,17},{17,1},{2,18},{18,2},{3,19},{19,3},{4,20},{20... | collective-permute-start | bytes 1769480 | tf_op jit(solution)/shard_map/ppermute | solution.py:46
  124.8 12.5 %collective-permute-start.27 = (bf16[256,768]{1,0:T(8,128)(2,1)S(1)}, bf16[256,768]{1,0:T(8,128)(2,1)S(1)}, u32[]{:S(2)}, u32[]{:S(2)}) collective-permute-start(bf16[256,768]{1,0:T(8,128)(2,1)S(1)} %collective-permute-done.20.refs_4_), channel_id=1, source_target_pairs={{8,12},{4,0},{9,13},{5,1},{10,14},{6,2},{11,15},{7,3},{24,28},{20,... | collective-permute-start | bytes 1179656 | tf_op jit(solution)/shard_map/ppermute | solution.py:1137
  126.1 18.6 %collective-permute-start.29 = (bf16[256,768]{1,0:T(8,128)(2,1)S(1)}, bf16[256,768]{1,0:T(8,128)(2,1)}, u32[]{:S(2)}, u32[]{:S(2)}) collective-permute-start(bf16[256,768]{1,0:T(8,128)(2,1)S(1)} %get-tuple-element.342.refs_8_), channel_id=1, source_target_pairs={{0,1},{1,0},{2,3},{3,2},{4,5},{5,4},{6,7},{7,6},{8,9},{9,8},{10,11... | collective-permute-start | bytes 1179656 | tf_op jit(solution)/shard_map/ppermute | solution.py:46
  140.9 5.2 %collective-permute-start.28 = (bf16[256,768]{1,0:T(8,128)(2,1)S(1)}, bf16[256,768]{1,0:T(8,128)(2,1)S(1)}, u32[]{:S(2)}, u32[]{:S(2)}) collective-permute-start(bf16[256,768]{1,0:T(8,128)(2,1)S(1)} %broadcast_select_fusion.refs_6_), channel_id=1, source_target_pairs={{0,1},{1,0},{2,3},{3,2},{4,5},{5,4},{6,7},{7,6},{8,9},{9,8},{10,11... | collective-permute-start | bytes 1179656 | tf_op jit(solution)/shard_map/ppermute | solution.py:46
  141.0 45.5 %collective-permute-start.30 = (bf16[432,512]{1,0:T(8,128)(2,1)S(1)}, bf16[432,512]{1,0:T(8,128)(2,1)S(1)}, u32[]{:S(2)}, u32[]{:S(2)}) collective-permute-start(bf16[432,512]{1,0:T(8,128)(2,1)S(1)} %copy-done.60), channel_id=1, source_target_pairs={{0,2},{1,3},{2,0},{3,1},{4,6},{5,7},{6,4},{7,5},{8,10},{9,11},{10,... | collective-permute-start | bytes 1327112 | tf_op jit(solution)/shard_map/ppermute | solution.py:46
  142.6 28.7 %collective-permute-start.34 = (bf16[384,768]{1,0:T(8,128)(2,1)}, bf16[384,768]{1,0:T(8,128)(2,1)S(1)}, u32[]{:S(2)}, u32[]{:S(2)}) collective-permute-start(bf16[384,768]{1,0:T(8,128)(2,1)} %get-tuple-element.200.refs_0_), channel_id=1, source_target_pairs={{0,2},{1,3},{2,0},{3,1},{4,6},{5,7},{6,4},{7,5},{8,10},{9,11},{10,... | collective-permute-start | bytes 1769480 | tf_op jit(solution)/shard_map/ppermute | solution.py:46
  143.1 36.2 %collective-permute-start.35 = (bf16[384,768]{1,0:T(8,128)(2,1)S(1)}, bf16[384,768]{1,0:T(8,128)(2,1)S(1)}, u32[]{:S(2)}, u32[]{:S(2)}) collective-permute-start(bf16[384,768]{1,0:T(8,128)(2,1)S(1)} %collective-permute-done.25.refs_2_), channel_id=1, source_target_pairs={{0,2},{1,3},{2,0},{3,1},{4,6},{5,7},{6,4},{7,5},{8,10},{9,11},{10,... | collective-permute-start | bytes 1769480 | tf_op jit(solution)/shard_map/ppermute | solution.py:46
  144.7 34.7 %collective-permute-start.32 = (bf16[384,1024]{1,0:T(8,128)(2,1)}, bf16[384,1024]{1,0:T(8,128)(2,1)S(1)}, u32[]{:S(2)}, u32[]{:S(2)}) collective-permute-start(bf16[384,1024]{1,0:T(8,128)(2,1)} %get-tuple-element.198.refs_0_), channel_id=1, source_target_pairs={{0,16},{16,0},{1,17},{17,1},{2,18},{18,2},{3,19},{19,3},{4,20},{20... | collective-permute-start | bytes 2359304 | tf_op jit(solution)/shard_map/ppermute | solution.py:46
  146.2 34.6 %collective-permute-start.33 = (bf16[384,1024]{1,0:T(8,128)(2,1)S(1)}, bf16[384,1024]{1,0:T(8,128)(2,1)S(1)}, u32[]{:S(2)}, u32[]{:S(2)}) collective-permute-start(bf16[384,1024]{1,0:T(8,128)(2,1)S(1)} %collective-permute-done.24.refs_1_), channel_id=1, source_target_pairs={{0,16},{16,0},{1,17},{17,1},{2,18},{18,2},{3,19},{19,3},{4,20},{20... | collective-permute-start | bytes 2359304 | tf_op jit(solution)/shard_map/ppermute | solution.py:46
  171.3 17.0 %collective-permute-start.31 = (bf16[432,512]{1,0:T(8,128)(2,1)}, bf16[432,512]{1,0:T(8,128)(2,1)S(1)}, u32[]{:S(2)}, u32[]{:S(2)}) collective-permute-start(bf16[432,512]{1,0:T(8,128)(2,1)} %get-tuple-element.196), channel_id=1, source_target_pairs={{0,2},{1,3},{2,0},{3,1},{4,6},{5,7},{6,4},{7,5},{8,10},{9,11},{10,... | collective-permute-start | bytes 1327112 | tf_op jit(solution)/shard_map/ppermute | solution.py:46
  202.1 4.7 collective-permute-start.37
  231.8 2.6 collective-permute-start.39
  255.0 2.6 collective-permute-start.40
  263.5 2.6 collective-permute-start.41
  273.6 12.7 %collective-permute-start.42 = (bf16[432,512]{1,0:T(8,128)(2,1)}, bf16[432,512]{1,0:T(8,128)(2,1)S(1)}, u32[]{:S(2)}, u32[]{:S(2)}) collective-permute-start(bf16[432,512]{1,0:T(8,128)(2,1)} %get-tuple-element.228.g_own), channel_id=1, source_target_pairs={{0,2},{1,3},{2,0},{3,1},{4,6},{5,7},{6,4},{7,5},{8,10},{9,11},{10,... | collective-permute-start | bytes 1327112 | tf_op jit(solution)/shard_map/ppermute | solution.py:46
  275.1 10.1 %collective-permute-start.43 = (bf16[384,384]{1,0:T(8,128)(2,1)}, bf16[384,384]{1,0:T(8,128)(2,1)S(1)}, u32[]{:S(2)}, u32[]{:S(2)}) collective-permute-start(bf16[384,384]{1,0:T(8,128)(2,1)} %get-tuple-element.229), channel_id=1, source_target_pairs={{0,16},{16,0},{1,17},{17,1},{2,18},{18,2},{3,19},{19,3},{4,20},{20... | collective-permute-start | bytes 884744 | tf_op jit(solution)/shard_map/ppermute | solution.py:46
  276.8 58.1 %collective-permute-start.47 = (bf16[384,3072]{1,0:T(8,128)(2,1)S(1)}, bf16[384,3072]{1,0:T(8,128)(2,1)S(1)}, u32[]{:S(2)}, u32[]{:S(2)}) collective-permute-start(bf16[384,3072]{1,0:T(8,128)(2,1)S(1)} %copy-done.56), channel_id=1, source_target_pairs={{0,16},{16,0},{1,17},{17,1},{2,18},{18,2},{3,19},{19,3},{4,20},{20... | collective-permute-start | bytes 7077896 | tf_op jit(solution)/shard_map/ppermute | solution.py:46
  316.2 25.6 %collective-permute-start.48 = (bf16[1024,768]{1,0:T(8,128)(2,1)}, bf16[1024,768]{1,0:T(8,128)(2,1)S(1)}, u32[]{:S(2)}, u32[]{:S(2)}) collective-permute-start(bf16[1024,768]{1,0:T(8,128)(2,1)} %get-tuple-element.244), channel_id=1, source_target_pairs={{0,1},{1,0},{2,3},{3,2},{4,5},{5,4},{6,7},{7,6},{8,9},{9,8},{10,11... | collective-permute-start | bytes 4718600 | tf_op jit(solution)/shard_map/ppermute | solution.py:46
  316.3 30.2 %collective-permute-start.45 = (bf16[432,512]{1,0:T(8,128)(2,1)S(1)}, bf16[432,512]{1,0:T(8,128)(2,1)}, u32[]{:S(2)}, u32[]{:S(2)}) collective-permute-start(bf16[432,512]{1,0:T(8,128)(2,1)S(1)} %copy-done.61), channel_id=1, source_target_pairs={{0,2},{1,3},{2,0},{3,1},{4,6},{5,7},{6,4},{7,5},{8,10},{9,11},{10,... | collective-permute-start | bytes 1327112 | tf_op jit(solution)/shard_map/ppermute | solution.py:46
  320.1 28.3 %collective-permute-start.46 = (bf16[384,512]{1,0:T(8,128)(2,1)}, bf16[384,512]{1,0:T(8,128)(2,1)S(1)}, u32[]{:S(2)}, u32[]{:S(2)}) collective-permute-start(bf16[384,512]{1,0:T(8,128)(2,1)} %get-tuple-element.237), channel_id=1, source_target_pairs={{0,2},{1,3},{2,0},{3,1},{4,6},{5,7},{6,4},{7,5},{8,10},{9,11},{10,... | collective-permute-start | bytes 1179656 | tf_op jit(solution)/shard_map/ppermute | solution.py:46
  341.3 48.8 %collective-permute-start.49 = (bf16[384,1536]{1,0:T(8,128)(2,1)}, bf16[384,1536]{1,0:T(8,128)(2,1)S(1)}, u32[]{:S(2)}, u32[]{:S(2)}) collective-permute-start(bf16[384,1536]{1,0:T(8,128)(2,1)} %get-tuple-element.242), channel_id=1, source_target_pairs={{0,2},{1,3},{2,0},{3,1},{4,6},{5,7},{6,4},{7,5},{8,10},{9,11},{10,... | collective-permute-start | bytes 3538952 | tf_op jit(solution)/shard_map/ppermute | solution.py:46
  344.0 46.2 %collective-permute-start.52 = (bf16[256,768]{1,0:T(8,128)(2,1)S(1)}, bf16[256,768]{1,0:T(8,128)(2,1)S(1)}, u32[]{:S(2)}, u32[]{:S(2)}) collective-permute-start(bf16[256,768]{1,0:T(8,128)(2,1)S(1)} %get-tuple-element.339), channel_id=1, source_target_pairs={{0,12},{4,8},{8,4},{12,0},{1,13},{5,9},{9,5},{13,1},{2,14},{6,10},... | collective-permute-start | bytes 1179656 | tf_op jit(solution)/shard_map/ppermute | solution.py:46
  346.5 43.6 %collective-permute-start.51 = (bf16[256,768]{1,0:T(8,128)(2,1)S(1)}, bf16[256,768]{1,0:T(8,128)(2,1)S(1)}, u32[]{:S(2)}, u32[]{:S(2)}) collective-permute-start(bf16[256,768]{1,0:T(8,128)(2,1)S(1)} %get-tuple-element.340), channel_id=1, source_target_pairs={{0,8},{4,12},{8,0},{12,4},{1,9},{5,13},{9,1},{13,5},{2,10},{6,14},... | collective-permute-start | bytes 1179656 | tf_op jit(solution)/shard_map/ppermute | solution.py:46
  346.5 43.6 %collective-permute-start.50 = (bf16[256,768]{1,0:T(8,128)(2,1)S(1)}, bf16[256,768]{1,0:T(8,128)(2,1)S(1)}, u32[]{:S(2)}, u32[]{:S(2)}) collective-permute-start(bf16[256,768]{1,0:T(8,128)(2,1)S(1)} %get-tuple-element.341), channel_id=1, source_target_pairs={{0,4},{4,0},{8,12},{12,8},{1,5},{5,1},{9,13},{13,9},{2,6},{6,2},{1... | collective-permute-start | bytes 1179656 | tf_op jit(solution)/shard_map/ppermute | solution.py:46
  390.2 8.9 %collective-permute-start.54 = (bf16[1024,768]{1,0:T(8,128)(2,1)}, bf16[1024,768]{1,0:T(8,128)(2,1)S(1)}, u32[]{:S(2)}, u32[]{:S(2)}) collective-permute-start(bf16[1024,768]{1,0:T(8,128)(2,1)} %get-tuple-element.258), channel_id=1, source_target_pairs={{0,1},{1,0},{2,3},{3,2},{4,5},{5,4},{6,7},{7,6},{8,9},{9,8},{10,11... | collective-permute-start | bytes 4718600 | tf_op jit(solution)/shard_map/ppermute | solution.py:46
  395.0 51.7 %all-to-all-start = ((bf16[4,96,1536]{2,1,0:T(8,128)(2,1)}), bf16[4,96,1536]{2,1,0:T(8,128)(2,1)S(1)}, u32[]{:S(2)}, u32[]{:S(2)}) async-start(bf16[4,96,1536]{2,1,0:T(8,128)(2,1)} %bitcast.48), calls=%async_computation | async-start | bytes 2359296 | tf_op jit(solution)/shard_map/all_to_all | solution.py:1322
  398.9 10.8 %collective-permute-start.53 = (bf16[384,512]{1,0:T(8,128)(2,1)}, bf16[384,512]{1,0:T(8,128)(2,1)S(1)}, u32[]{:S(2)}, u32[]{:S(2)}) collective-permute-start(bf16[384,512]{1,0:T(8,128)(2,1)} %get-tuple-element.254), channel_id=1, source_target_pairs={{0,2},{1,3},{2,0},{3,1},{4,6},{5,7},{6,4},{7,5},{8,10},{9,11},{10,... | collective-permute-start | bytes 1179656 | tf_op jit(solution)/shard_map/ppermute | solution.py:46
  398.9 26.2 %collective-permute-start.57 = (bf16[384,768]{1,0:T(8,128)(2,1)S(1)}, bf16[384,768]{1,0:T(8,128)(2,1)}, u32[]{:S(2)}, u32[]{:S(2)}) collective-permute-start(bf16[384,768]{1,0:T(8,128)(2,1)S(1)} %copy-done.59), channel_id=1, source_target_pairs={{0,16},{16,0},{1,17},{17,1},{2,18},{18,2},{3,19},{19,3},{4,20},{20... | collective-permute-start | bytes 1769480 | tf_op jit(solution)/shard_map/ppermute | solution.py:46
  416.7 8.5 %collective-permute-start.56 = (bf16[384,384]{1,0:T(8,128)(2,1)}, bf16[384,384]{1,0:T(8,128)(2,1)S(1)}, u32[]{:S(2)}, u32[]{:S(2)}) collective-permute-start(bf16[384,384]{1,0:T(8,128)(2,1)} %get-tuple-element.266), channel_id=1, source_target_pairs={{0,16},{16,0},{1,17},{17,1},{2,18},{18,2},{3,19},{19,3},{4,20},{20... | collective-permute-start | bytes 884744 | tf_op jit(solution)/shard_map/ppermute | solution.py:46
  416.7 29.9 %collective-permute-start.55 = (bf16[512,768]{1,0:T(8,128)(2,1)}, bf16[512,768]{1,0:T(8,128)(2,1)S(1)}, u32[]{:S(2)}, u32[]{:S(2)}) collective-permute-start(bf16[512,768]{1,0:T(8,128)(2,1)} %get-tuple-element.261), channel_id=1, source_target_pairs={{0,1},{1,0},{2,3},{3,2},{4,5},{5,4},{6,7},{7,6},{8,9},{9,8},{10,11... | collective-permute-start | bytes 2359304 | tf_op jit(solution)/shard_map/ppermute | solution.py:46
  417.8 7.3 %collective-permute-start.58 = (f32[1,6912]{1,0:T(1,128)S(1)}, f32[1,6912]{1,0:T(1,128)S(1)}, u32[]{:S(2)}, u32[]{:S(2)}) collective-permute-start(f32[1,6912]{1,0:T(1,128)S(1)} %constant_dynamic-update-slice_fusion.6), channel_id=1, source_target_pairs={{0,16},{16,0},{1,17},{17,1},{2,18},{18,2},{3,19},{19,3},{4,20},{20... | collective-permute-start | bytes 82952 | tf_op jit(solution)/shard_map/ppermute | solution.py:46
  425.2 3.9 collective-permute-start.66
  429.2 5.1 %collective-permute-start.67 = (f32[1,6912]{1,0:T(1,128)S(1)}, f32[1,6912]{1,0:T(1,128)S(1)}, u32[]{:S(2)}, u32[]{:S(2)}) collective-permute-start(f32[1,6912]{1,0:T(1,128)S(1)} %add.107), channel_id=1, source_target_pairs={{0,8},{4,12},{8,0},{12,4},{1,9},{5,13},{9,1},{13,5},{2,10},{6,14},... | collective-permute-start | bytes 82952 | tf_op jit(solution)/shard_map/ppermute | solution.py:46
  434.3 9.2 %collective-permute-start.68 = (f32[1,6912]{1,0:T(1,128)S(1)}, f32[1,6912]{1,0:T(1,128)S(1)}, u32[]{:S(2)}, u32[]{:S(2)}) collective-permute-start(f32[1,6912]{1,0:T(1,128)S(1)} %add.108), channel_id=1, source_target_pairs={{0,2},{1,3},{2,0},{3,1},{4,6},{5,7},{6,4},{7,5},{8,10},{9,11},{10,... | collective-permute-start | bytes 82952 | tf_op jit(solution)/shard_map/ppermute | solution.py:46
  434.7 14.2 %collective-permute-start.62 = (bf16[256,768]{1,0:T(8,128)(2,1)}, bf16[256,768]{1,0:T(8,128)(2,1)}, u32[]{:S(2)}, u32[]{:S(2)}) collective-permute-start(bf16[256,768]{1,0:T(8,128)(2,1)} %get-tuple-element.336), channel_id=1, source_target_pairs={{0,12},{4,8},{8,4},{12,0},{1,13},{5,9},{9,5},{13,1},{2,14},{6,10},... | collective-permute-start | bytes 1179656 | tf_op jit(solution)/shard_map/ppermute | solution.py:46
  438.3 29.8 %collective-permute-start.61 = (bf16[256,768]{1,0:T(8,128)(2,1)}, bf16[256,768]{1,0:T(8,128)(2,1)}, u32[]{:S(2)}, u32[]{:S(2)}) collective-permute-start(bf16[256,768]{1,0:T(8,128)(2,1)} %get-tuple-element.337), channel_id=1, source_target_pairs={{0,8},{4,12},{8,0},{12,4},{1,9},{5,13},{9,1},{13,5},{2,10},{6,14},... | collective-permute-start | bytes 1179656 | tf_op jit(solution)/shard_map/ppermute | solution.py:46
  438.3 29.8 %collective-permute-start.60 = (bf16[256,768]{1,0:T(8,128)(2,1)}, bf16[256,768]{1,0:T(8,128)(2,1)}, u32[]{:S(2)}, u32[]{:S(2)}) collective-permute-start(bf16[256,768]{1,0:T(8,128)(2,1)} %get-tuple-element.338), channel_id=1, source_target_pairs={{0,4},{4,0},{8,12},{12,8},{1,5},{5,1},{9,13},{13,9},{2,6},{6,2},{1... | collective-permute-start | bytes 1179656 | tf_op jit(solution)/shard_map/ppermute | solution.py:46
  443.5 24.6 %collective-permute-start.59 = (bf16[384,768]{1,0:T(8,128)(2,1)}, bf16[384,768]{1,0:T(8,128)(2,1)}, u32[]{:S(2)}, u32[]{:S(2)}) collective-permute-start(bf16[384,768]{1,0:T(8,128)(2,1)} %get-tuple-element.277), channel_id=1, source_target_pairs={{0,2},{1,3},{2,0},{3,1},{4,6},{5,7},{6,4},{7,5},{8,10},{9,11},{10,... | collective-permute-start | bytes 1769480 | tf_op jit(solution)/shard_map/ppermute | solution.py:46
  470.5 8.9 %collective-permute-start.63 = (bf16[96,768]{1,0:T(8,128)(2,1)}, bf16[96,768]{1,0:T(8,128)(2,1)S(1)}, u32[]{:S(2)}, u32[]{:S(2)}) collective-permute-start(bf16[96,768]{1,0:T(8,128)(2,1)} %get-tuple-element.284), channel_id=1, source_target_pairs={{0,4},{4,0},{8,12},{12,8},{1,5},{5,1},{9,13},{13,9},{2,6},{6,2},{1... | collective-permute-start | bytes 442376 | tf_op jit(solution)/shard_map/ppermute | solution.py:46
  470.6 13.1 %collective-permute-start.64 = (bf16[96,768]{1,0:T(8,128)(2,1)}, bf16[96,768]{1,0:T(8,128)(2,1)S(1)}, u32[]{:S(2)}, u32[]{:S(2)}) collective-permute-start(bf16[96,768]{1,0:T(8,128)(2,1)} %get-tuple-element.285), channel_id=1, source_target_pairs={{0,8},{4,12},{8,0},{12,4},{1,9},{5,13},{9,1},{13,5},{2,10},{6,14},... | collective-permute-start | bytes 442376 | tf_op jit(solution)/shard_map/ppermute | solution.py:46
  473.1 10.6 %collective-permute-start.65 = (bf16[96,768]{1,0:T(8,128)(2,1)}, bf16[96,768]{1,0:T(8,128)(2,1)S(1)}, u32[]{:S(2)}, u32[]{:S(2)}) collective-permute-start(bf16[96,768]{1,0:T(8,128)(2,1)} %get-tuple-element.286), channel_id=1, source_target_pairs={{0,12},{4,8},{8,4},{12,0},{1,13},{5,9},{9,5},{13,1},{2,14},{6,10},... | collective-permute-start | bytes 442376 | tf_op jit(solution)/shard_map/ppermute | solution.py:46
  (82 other events, 1084.8 us)
